TPU v7x, 32 devices: a whole 2x2x4 slice. The times are simulated.
32 devices in a mesh: grp: 2 (over y), frm: 8 (over z, x), tp: 2 (over core).
Axes of the slice: x: 2, y: 2, z: 4, core: 2. Of those that a mesh axis runs over, the one named last changes fastest.
Arguments:
- queries: bfloat16 [3072, 2560], P(('grp', 'frm'), 'tp'), parts along dimension 0, may hold values from -60 to 60, as said below
- key_rows: bfloat16 [3072, 2560], P(('grp', 'frm'), 'tp'), parts along dimension 0, may hold values from -60 to 60
- values: bfloat16 [3072, 2560], P(('grp', 'frm'), 'tp'), parts along dimension 0, may hold values from -6 to 6
- query_gain: float32 [2560], P('tp'), may hold values from 0.25 to 1.75
- key_gain: float32 [2560], P('tp'), may hold values from 0.25 to 1.75
- pattern: int32 [16, 4], P(('grp', 'frm')), parts along dimension 0, may hold values 0 or 1
- reference_keys: bfloat16 [64, 2560], P(('grp', 'frm'), 'tp'), parts along dimension 0, may hold values from -6 to 6
- reference_values: bfloat16 [64, 2560], P(('grp', 'frm'), 'tp'), parts along dimension 0, may hold values from -6 to 6
- reference_live: int32 [16], P(('grp', 'frm')), parts along dimension 0, may hold values from 1 to 4
Outputs:
- attention: bfloat16 [3072, 2560], P(('grp', 'frm'), 'tp'), parts along dimension 0
There are 2 independent parts, one for each index of `grp`. A program takes and returns all parts, laid end to end along the dimension named above; an argument that names none is the same for every part. Nothing has to cross between parts.
Inputs may be any that keep to these rules, and one draw needn't show every extreme that they name: `queries`: query entries lie within the range.
All inputs are finite; a program needn't handle non-finite values. No bound on the sum of `pattern` on one device may be relied on, other than what follows from the above.
Results may differ from a plain program's by a relative error of at most 0.012.
The roundings to bfloat16 on the way count: a program that leaves them out, or rounds other values in their place, can miss the bound.
Values may be sent and summed in bfloat16 or wider, within the bound.
No kernel may reach another device: no remote copies, remote signals or barrier semaphores. Data moves between devices by JAX's collectives and lax.ppermute only.
A program may use at most 64 MiB of HBM per device.

v0:
```python
import jax
import jax.numpy as jnp
from jax import lax
from jax.sharding import PartitionSpec as P

HEADS = 20
HEAD_DIM = 128
WINDOW = 2


EPSILON = 1e-06
NEG_FLOOR = -1e30


def passed_along(block, axis, distance):
    devices = range(lax.axis_size(axis))
    route = [((i - distance) % len(devices), i) for i in devices]
    return lax.ppermute(block, axis, route)


def normalize(matrix, scaling, square_sum, features):
    widened = matrix.astype(jnp.float32)
    return (widened * lax.rsqrt(square_sum / features + EPSILON)[:, None] * scaling).astype(
        jnp.bfloat16
    )


def absorb(state, query_part, key_part, value_part, allowed):
    running_max, running_sum, numerator = state
    scaling = query_part.shape[2] ** (-0.5)
    scores = (
        jnp.einsum("thd,nhd->htn", query_part, key_part, preferred_element_type=jnp.float32)
        * scaling
    )
    scores = jnp.where(allowed[None, None, :], scores, -jnp.inf)
    new_max = jnp.maximum(running_max, jnp.max(scores, axis=2))
    weights = jnp.exp(scores - new_max[:, :, None])
    fading = jnp.exp(running_max - new_max)
    running_sum = running_sum * fading + jnp.sum(weights, axis=2)
    numerator = numerator * jnp.transpose(fading)[:, :, None] + jnp.einsum(
        "htn,nhd->thd", weights.astype(jnp.bfloat16), value_part, preferred_element_type=jnp.float32
    )
    return (new_max, running_sum, numerator)


def attend(state, query_heads, key_heads, value_heads, allowed):
    group_width = query_heads.shape[1] // len(state)
    updated = []
    for group_id, group_state in enumerate(state):
        first_head = group_id * group_width
        last_head = first_head + group_width
        updated.append(
            absorb(
                group_state,
                query_heads[:, first_head:last_head],
                key_heads[:, first_head:last_head],
                value_heads[:, first_head:last_head],
                allowed,
            )
        )
    return tuple(updated)


def shards(
    queries,
    key_rows,
    values,
    query_gain,
    key_gain,
    pattern,
    reference_keys,
    reference_values,
    reference_live,
):
    tokens_here, features = queries.shape
    heads_here = features // HEAD_DIM
    squares = lax.psum(
        (
            jnp.sum(jnp.square(queries.astype(jnp.float32)), axis=1),
            jnp.sum(jnp.square(key_rows.astype(jnp.float32)), axis=1),
        ),
        "tp",
    )
    full_width = HEADS * HEAD_DIM
    normed_queries = normalize(queries, query_gain, squares[0], full_width)
    normed_keys = normalize(key_rows, key_gain, squares[1], full_width)
    query_heads = normed_queries.reshape(tokens_here, heads_here, HEAD_DIM)
    own_pair = jnp.stack([normed_keys, values])
    offsets = [column - WINDOW for column in range(WINDOW)] + [
        column + 1 for column in range(WINDOW)
    ]
    arrived = [passed_along(own_pair, "frm", -offset) for offset in offsets]
    groups = 2
    group_width = heads_here // groups
    start_state = tuple(
        (
            (
                jnp.full((group_width, tokens_here), NEG_FLOOR, jnp.float32),
                jnp.zeros((group_width, tokens_here), jnp.float32),
                jnp.zeros((tokens_here, group_width, HEAD_DIM), jnp.float32),
            )
            for group_id in range(groups)
        )
    )
    near_live = pattern[0] > 0

    def split_heads(matrix):
        return matrix.reshape(matrix.shape[0], heads_here, HEAD_DIM)

    every_pair = [own_pair] + arrived
    all_keys = split_heads(jnp.concatenate([key_value[0] for key_value in every_pair], axis=0))
    all_values = split_heads(jnp.concatenate([key_value[1] for key_value in every_pair], axis=0))
    flags = jnp.concatenate([jnp.ones((1,), jnp.bool_), near_live])
    allowed = jnp.repeat(flags, tokens_here)
    row_flags = (jnp.arange(reference_keys.shape[0], dtype=jnp.int32) < reference_live[0]).astype(
        jnp.bfloat16
    )
    pieces = (
        lax.all_gather(reference_keys, "frm", axis=0, tiled=True),
        lax.all_gather(reference_values, "frm", axis=0, tiled=True),
        lax.all_gather(row_flags, "frm", axis=0, tiled=True),
    )
    row_count = pieces[0].shape[0]
    final_state = attend(
        attend(start_state, query_heads, all_keys, all_values, allowed),
        query_heads,
        pieces[0].reshape(row_count, heads_here, HEAD_DIM),
        pieces[1].reshape(row_count, heads_here, HEAD_DIM),
        pieces[2] > 0.5,
    )
    outputs = [
        group_state[2] / jnp.transpose(group_state[1])[:, :, None] for group_state in final_state
    ]
    return jnp.concatenate(outputs, axis=1).reshape(tokens_here, features).astype(jnp.bfloat16)


def solution(mesh):
    in_specs = (
        P(("grp", "frm"), "tp"),
        P(("grp", "frm"), "tp"),
        P(("grp", "frm"), "tp"),
        P("tp"),
        P("tp"),
        P(("grp", "frm"), None),
        P(("grp", "frm"), "tp"),
        P(("grp", "frm"), "tp"),
        P(("grp", "frm")),
    )
    out_specs = P(("grp", "frm"), "tp")
    return jax.shard_map(shards, mesh=mesh, in_specs=in_specs, out_specs=out_specs, check_vma=False)
```

profile of v0, /device:TPU:0, one launch (start us, length us, event | category | flops | bytes accessed | tf_op | source)
XLA Modules:
  0.0 187.1 jit_solution(17618880381193820832)
XLA Ops:
  0.0 1.3 fusion.65
  1.3 1.2 fusion.62
  2.5 2.6 %all-reduce.1 = (f32[192]{0:T(256)S(1)}, f32[192]{0:T(256)S(1)}) all-reduce(f32[192]{0:T(256)S(1)} %fusion.65, f32[192]{0:T(256)S(1)} %fusion.62), channel_id=1, replica_groups=mesh['grp'=2,'frm'=8,'tp'=2] {'tp'}, use_global_device_ids=true, to_apply=%region_3.0 | all-reduce | flops 384 | bytes 3072 | tf_op jit(solution)/shard_map/psum | solution.py:77
  5.1 1.2 fusion.108
  6.3 2.1 %pad_maximum_fusion = bf16[2,192,1280]{2,1,0:T(8,128)(2,1)} fusion(bf16[1,192,1280]{2,1,0:T(8,128)(2,1)} %bitcast.111, bf16[1,192,1280]{2,1,0:T(8,128)(2,1)S(1)} %fusion.108), kind=kLoop, calls=%fused_computation.54 | loop fusion | flops 491520 | bytes 1966080 | tf_op jit(solution)/shard_map/stack | solution.py:88
  8.4 2.9 %collective-permute-start = (bf16[2,192,1280]{2,1,0:T(8,128)(2,1)}, bf16[2,192,1280]{2,1,0:T(8,128)(2,1)}, u32[]{:S(2)}, u32[]{:S(2)}) collective-permute-start(bf16[2,192,1280]{2,1,0:T(8,128)(2,1)} %pad_maximum_fusion), channel_id=1, source_target_pairs={{12,0},{14,2},{0,4},{2,6},{4,8},{6,10},{8,12},{10,14},{13,1},{15,3... | collective-permute-start | bytes 2949128 | tf_op jit(solution)/shard_map/ppermute | solution.py:18
  11.4 1.5 collective-permute-start.1
  12.8 3.2 %collective-permute-start.2 = (bf16[2,192,1280]{2,1,0:T(8,128)(2,1)}, bf16[2,192,1280]{2,1,0:T(8,128)(2,1)S(1)}, u32[]{:S(2)}, u32[]{:S(2)}) collective-permute-start(bf16[2,192,1280]{2,1,0:T(8,128)(2,1)} %pad_maximum_fusion), channel_id=1, source_target_pairs={{2,0},{4,2},{6,4},{8,6},{10,8},{12,10},{14,12},{0,14},{3,1},{5,3},... | collective-permute-start | bytes 2949128 | tf_op jit(solution)/shard_map/ppermute | solution.py:18
  16.1 0.3 collective-permute-start.3
  16.4 0.2 copy.51
  16.6 0.2 fusion.67
  16.8 0.3 copy.56
  17.1 0.9 constant_dynamic-update-slice_fusion.9
  18.1 0.1 pad_add_fusion
  18.1 0.1 broadcast_in_dim.53
  18.2 0.1 broadcast_in_dim.54
  18.3 0.2 fusion.64
  18.5 0.2 copy.39
  18.8 0.2 copy.41
  19.0 0.3 copy.46
  19.3 0.9 constant_dynamic-update-slice_fusion.4
  20.2 82.3 %all-gather = bf16[8,4,1280]{2,1,0:T(4,128)(2,1)S(1)} all-gather(bf16[1,4,1280]{2,1,0:T(4,128)(2,1)S(1)} %bitcast.112), channel_id=1, replica_groups=mesh['grp'=2,'frm'=8,'tp'=2] {'frm'}, dimensions={0}, use_global_device_ids=true | all-gather | bytes 92160 | tf_op jit(solution)/shard_map/all_gather | solution.py:119
  103.1 0.6 dynamic-slice
  104.4 0.2 dynamic-update-slice
  104.7 18.7 %all-reduce = bf16[32]{0:T(256)(128)(2,1)S(1)} all-reduce(bf16[32]{0:T(256)(128)(2,1)S(1)} %dynamic-update-slice), channel_id=1, replica_groups=mesh['grp'=2,'frm'=8,'tp'=2] {'frm'}, use_global_device_ids=true, to_apply=%add | all-reduce | flops 32 | bytes 128
  123.4 30.7 %all-gather.1 = bf16[8,4,1280]{2,1,0:T(4,128)(2,1)S(1)} all-gather(bf16[1,4,1280]{2,1,0:T(4,128)(2,1)S(1)} %bitcast.113), channel_id=1, replica_groups=mesh['grp'=2,'frm'=8,'tp'=2] {'frm'}, dimensions={0}, use_global_device_ids=true | all-gather | bytes 92160 | tf_op jit(solution)/shard_map/all_gather | solution.py:120
  154.2 0.2 fusion.103
  154.4 0.6 fusion.100
  155.1 0.8 fusion.102
  155.9 2.0 %fusion.99 = (bf16[1,192,1280]{2,1,0:T(8,128)(2,1)}, bf16[1,192,1280]{2,1,0:T(8,128)(2,1)S(1)}) fusion(bf16[2,192,1280]{2,1,0:T(8,128)(2,1)} %collective-permute-done), kind=kLoop, calls=%fused_computation.111 | loop fusion | bytes 1966080 | tf_op jit(solution)/shard_map/slice | solution.py:111
  158.0 0.2 copy.52
  158.2 0.3 copy.57
  158.5 2.0 %fusion.98 = (bf16[1,192,1280]{2,1,0:T(8,128)(2,1)}, bf16[1,192,1280]{2,1,0:T(8,128)(2,1)S(1)}) fusion(bf16[2,192,1280]{2,1,0:T(8,128)(2,1)} %collective-permute-done.1), kind=kLoop, calls=%fused_computation.110 | loop fusion | bytes 1966080 | tf_op jit(solution)/shard_map/slice | solution.py:111
  160.6 0.2 copy.53
  160.8 0.3 copy.58
  161.1 0.9 fusion.97
  162.0 0.2 copy.54
  162.2 0.3 copy.59
  162.5 2.0 %fusion.96 = (bf16[1,192,1280]{2,1,0:T(8,128)(2,1)}, bf16[1,192,1280]{2,1,0:T(8,128)(2,1)S(1)}) fusion(bf16[2,192,1280]{2,1,0:T(8,128)(2,1)} %collective-permute-done.3), kind=kLoop, calls=%fused_computation.108 | loop fusion | bytes 1966080 | tf_op jit(solution)/shard_map/slice | solution.py:111
  164.5 0.2 copy.55
  164.8 0.3 copy.60
  165.1 1.3 copy.42
  166.4 1.0 copy.47
  167.4 1.3 copy.43
  168.7 1.0 copy.48
  169.7 1.3 copy.44
  170.9 1.1 copy.49
  172.0 1.3 copy.45
  173.3 1.0 copy.50
  174.3 0.9 constant_dynamic-update-slice_fusion.8
  175.2 0.9 constant_dynamic-update-slice_fusion.7
  176.1 0.9 constant_dynamic-update-slice_fusion.6
  177.0 0.9 constant_dynamic-update-slice_fusion.5
  178.1 0.1 constant_dynamic-update-slice_fusion.1
  178.2 1.1 fusion
  179.3 1.9 %fusion.2 = (f32[5,192]{1,0:T(8,128)S(1)}, f32[5,192]{1,0:T(8,128)S(1)}, f32[5,192,960]{2,1,0:T(8,128)S(1)}) fusion(f32[5,192,960]{2,1,0:T(8,128)S(1)} %get-tuple-element.36, f32[5,192]{1,0:T(8,128)S(1)} %get-tuple-element.27, pred[960]{0:T(1024)(128)(4,1)S(1)} %broadcast_in_dim.54, bf16[192,10,128]{0,2,1:T(8,128)(2,1)S(1)} %bitcast.99, ...), kind=kOutput, calls=%fused_computation.6 | convolution fusion | flops 242378880 | bytes 9519616 | tf_op jit(solution)/shard_map/thd,nhd->htn/dot_general | solution.py:32
  181.3 1.0 fusion.4
  182.4 0.5 copy-done.8
  182.9 1.1 fusion.53
  184.0 1.1 fusion.48
  185.1 0.3 fusion.59
  185.5 0.3 fusion.58
  185.9 0.2 copy.66
  186.1 1.0 copy.67
  (55 shorter events, 0.6 us)
Async XLA Ops:
  0.0 16.6 %copy-start = (bf16[192,1280]{1,0:T(8,128)(2,1)S(1)}, bf16[192,1280]{1,0:T(8,128)(2,1)}, u32[]{:S(2)}) copy-start(bf16[192,1280]{1,0:T(8,128)(2,1)} %param.10) | copy-start | bytes 1474564
  0.0 16.6 %copy-start.11 = (f32[1280]{0:T(1024)S(1)}, f32[1280]{0:T(1024)}, u32[]{:S(2)}) copy-start(f32[1280]{0:T(1024)} %param.13) | copy-start | bytes 15364
  0.0 16.4 %copy-start.6 = (bf16[192,1280]{1,0:T(8,128)(2,1)S(1)}, bf16[192,1280]{1,0:T(8,128)(2,1)}, u32[]{:S(2)}) copy-start(bf16[192,1280]{1,0:T(8,128)(2,1)} %param.11) | copy-start | bytes 1474564
  8.4 9.6 %copy-start.15 = (s32[1,4]{1,0:T(1,128)S(1)}, s32[1,4]{1,0:T(1,128)}, u32[]{:S(2)}) copy-start(s32[1,4]{1,0:T(1,128)} %param.14) | copy-start | bytes 52
  8.4 9.9 %copy-start.1 = (bf16[192,1280]{1,0:T(8,128)(2,1)S(1)}, bf16[192,1280]{1,0:T(8,128)(2,1)}, u32[]{:S(2)}) copy-start(bf16[192,1280]{1,0:T(8,128)(2,1)} %param.9) | copy-start | bytes 1474564
  8.4 9.9 %copy-start.14 = (f32[1280]{0:T(1024)S(1)}, f32[1280]{0:T(1024)}, u32[]{:S(2)}) copy-start(f32[1280]{0:T(1024)} %param.12) | copy-start | bytes 15364
  8.4 147.5 %collective-permute-start = (bf16[2,192,1280]{2,1,0:T(8,128)(2,1)}, bf16[2,192,1280]{2,1,0:T(8,128)(2,1)}, u32[]{:S(2)}, u32[]{:S(2)}) collective-permute-start(bf16[2,192,1280]{2,1,0:T(8,128)(2,1)} %pad_maximum_fusion), channel_id=1, source_target_pairs={{12,0},{14,2},{0,4},{2,6},{4,8},{6,10},{8,12},{10,14},{13,1},{15,3... | collective-permute-start | bytes 2949128 | tf_op jit(solution)/shard_map/ppermute | solution.py:18
  11.4 147.2 %collective-permute-start.1 = (bf16[2,192,1280]{2,1,0:T(8,128)(2,1)}, bf16[2,192,1280]{2,1,0:T(8,128)(2,1)}, u32[]{:S(2)}, u32[]{:S(2)}) collective-permute-start(bf16[2,192,1280]{2,1,0:T(8,128)(2,1)} %pad_maximum_fusion), channel_id=1, source_target_pairs={{14,0},{0,2},{2,4},{4,6},{6,8},{8,10},{10,12},{12,14},{15,1},{1,3}... | collective-permute-start | bytes 2949128 | tf_op jit(solution)/shard_map/ppermute | solution.py:18
  12.8 148.3 %collective-permute-start.2 = (bf16[2,192,1280]{2,1,0:T(8,128)(2,1)}, bf16[2,192,1280]{2,1,0:T(8,128)(2,1)S(1)}, u32[]{:S(2)}, u32[]{:S(2)}) collective-permute-start(bf16[2,192,1280]{2,1,0:T(8,128)(2,1)} %pad_maximum_fusion), channel_id=1, source_target_pairs={{2,0},{4,2},{6,4},{8,6},{10,8},{12,10},{14,12},{0,14},{3,1},{5,3},... | collective-permute-start | bytes 2949128 | tf_op jit(solution)/shard_map/ppermute | solution.py:18
  16.1 146.5 %collective-permute-start.3 = (bf16[2,192,1280]{2,1,0:T(8,128)(2,1)}, bf16[2,192,1280]{2,1,0:T(8,128)(2,1)}, u32[]{:S(2)}, u32[]{:S(2)}) collective-permute-start(bf16[2,192,1280]{2,1,0:T(8,128)(2,1)} %pad_maximum_fusion), channel_id=1, source_target_pairs={{4,0},{6,2},{8,4},{10,6},{12,8},{14,10},{0,12},{2,14},{5,1},{7,3},... | collective-permute-start | bytes 2949128 | tf_op jit(solution)/shard_map/ppermute | solution.py:18
  18.5 1.7 copy-start.12
  18.5 84.6 %copy-start.16 = (u32[32]{0:T(128)S(1)}, u32[32]{0:T(128)}, u32[]{:S(2)}) copy-start(u32[32]{0:T(128)} %constant.29) | copy-start | bytes 388
  18.5 104.9 %copy-start.13 = (bf16[4,1280]{1,0:T(4,128)(2,1)S(1)}, bf16[4,1280]{1,0:T(4,128)(2,1)}, u32[]{:S(2)}) copy-start(bf16[4,1280]{1,0:T(4,128)(2,1)} %param.16) | copy-start | bytes 30724
  174.3 3.6 %copy-start.2 = (bf16[192,10,128]{2,0,1:T(8,128)(2,1)S(1)}, bf16[192,10,128]{2,0,1:T(8,128)(2,1)}, u32[]{:S(2)}) copy-start(bf16[192,10,128]{2,0,1:T(8,128)(2,1)} %copy.47) | copy-start | bytes 1474564
  174.3 3.6 %copy-start.9 = (bf16[960,10,128]{2,0,1:T(8,128)(2,1)S(1)}, bf16[960,10,128]{2,0,1:T(8,128)(2,1)}, u32[]{:S(2)}) copy-start(bf16[960,10,128]{2,0,1:T(8,128)(2,1)} %constant_dynamic-update-slice_fusion.4) | copy-start | bytes 7372804
  174.3 3.7 %copy-start.3 = (bf16[192,10,128]{2,0,1:T(8,128)(2,1)S(1)}, bf16[192,10,128]{2,0,1:T(8,128)(2,1)}, u32[]{:S(2)}) copy-start(bf16[192,10,128]{2,0,1:T(8,128)(2,1)} %copy.48) | copy-start | bytes 1474564
  175.2 2.9 %copy-start.4 = (bf16[192,10,128]{2,0,1:T(8,128)(2,1)S(1)}, bf16[192,10,128]{2,0,1:T(8,128)(2,1)}, u32[]{:S(2)}) copy-start(bf16[192,10,128]{2,0,1:T(8,128)(2,1)} %copy.49) | copy-start | bytes 1474564
  176.1 2.0 %copy-start.5 = (bf16[192,10,128]{2,0,1:T(8,128)(2,1)S(1)}, bf16[192,10,128]{2,0,1:T(8,128)(2,1)}, u32[]{:S(2)}) copy-start(bf16[192,10,128]{2,0,1:T(8,128)(2,1)} %copy.50) | copy-start | bytes 1474564
  179.3 1.9 %copy-start.7 = (f32[5,192,32]{1,2,0:T(8,128)S(1)}, f32[5,192,32]{1,2,0:T(8,128)}, u32[]{:S(2)}) copy-start(f32[5,192,32]{1,2,0:T(8,128)} %get-tuple-element.32) | copy-start | bytes 368644
  181.2 1.7 copy-start.8
  184.0 1.1 copy-start.10
where the time goes:
time: 188 us; the launch traced here: 187 us
  blocking collectives  134 us (71%)
  local copies, waits for them, and re-layouts  28.9 us (15%)
  starting transfers between devices  7.92 us (4%)
  other arithmetic  7.48 us (4%)
  matrix products  6.85 us (4%)
    all_gather x1, blocking collectives, shards(): lax.all_gather(reference_keys, 'frm', axis=0, tiled=True)  82.3 us
    all_gather x1, blocking collectives, shards(): lax.all_gather(reference_values, 'frm', axis=0, tiled=True)  30.7 us
    unnamed x1, blocking collectives  18.7 us
    slice x8, local copies, waits for them, and re-layouts, shards(): key_value[0]  12 us
    ppermute x4, starting transfers between devices, passed_along(): return lax.ppermute(block, axis, route)  7.92 us
    unnamed x46, local copies, waits for them, and re-layouts  6.38 us
    concatenate x6, local copies, waits for them, and re-layouts, shards(): jnp.concatenate([key_value[0] for key_value in every_pair], axis=0)  4.48 us
    dot_general x4, matrix products, absorb(): jnp.einsum('thd,nhd->htn', query_part, key_part, preferred_element_type=j...  4 us
  transfers between devices with their start and end apart: 4, of which 0 were waited for; matrix products, arithmetic and copies ran while one was open for 7% of the time, Pallas kernels for 0%

commit v1 on v0

v1 whole, which is shorter than its diff:
```python
import functools
import math

import jax
import jax.numpy as jnp
from jax import lax
from jax.experimental import pallas as pl
from jax.experimental.pallas import tpu as pltpu
from jax.sharding import PartitionSpec as P

HEADS = 20
HEAD_DIM = 128
WINDOW = 2
EPSILON = 1e-06
LANES = 128
TO_LOG2 = HEAD_DIM ** (-0.5) * math.log2(math.e)


def fetch(block, source_of):
    n = lax.axis_size("frm")
    return lax.ppermute(block, "frm", [(source_of(i) % n, i) for i in range(n)])


def after(value, *earlier):
    return lax.optimization_barrier((value,) + earlier)[0]


def far_first(i):
    return i + WINDOW if i % 2 == 0 else i - WINDOW


def far_second(i):
    return i - WINDOW if i % 2 == 0 else i + WINDOW


def beside(i):
    return i + 1 if i % 2 == 0 else i - 1


def gather_rows(rows):
    n = lax.axis_size("frm")
    if n & (n - 1):
        return lax.all_gather(rows, "frm", axis=0, tiled=True)
    distance = 1
    while distance < n:
        rows = jnp.concatenate([rows, fetch(rows, lambda i: i ^ distance)], axis=0)
        distance *= 2
    return rows


def attend_kernel(blocks, has_state, last, *refs):
    refs = list(refs)
    query_ref, bias_ref = refs[:2]
    key_refs = refs[2 : 2 + blocks]
    value_refs = refs[2 + blocks : 2 + 2 * blocks]
    rest = refs[2 + 2 * blocks :]
    if has_state:
        old_stats_ref, old_total_ref = rest[:2]
        rest = rest[2:]
    tokens, features = query_ref.shape
    heads = features // HEAD_DIM
    bias = bias_ref[...]
    lane = lax.broadcasted_iota(jnp.int32, (tokens, LANES), 1)
    stats = jnp.zeros((tokens, LANES), jnp.float32)
    for head in range(heads):
        columns = pl.ds(head * HEAD_DIM, HEAD_DIM)
        keys = jnp.concatenate([ref[:, columns] for ref in key_refs], axis=0)
        values = jnp.concatenate([ref[:, columns] for ref in value_refs], axis=0)
        scores = lax.dot_general(
            query_ref[:, columns],
            keys,
            (((1,), (1,)), ((), ())),
            preferred_element_type=jnp.float32,
        )
        scores = scores * TO_LOG2 + bias
        peak = jnp.max(scores, axis=1, keepdims=True)
        if has_state:
            old_peak = old_stats_ref[:, head : head + 1]
            peak = jnp.maximum(peak, old_peak)
        weights = jnp.exp2(scores - peak)
        total = jnp.sum(weights, axis=1, keepdims=True)
        numerator = jnp.dot(
            weights.astype(jnp.bfloat16), values, preferred_element_type=jnp.float32
        )
        if has_state:
            fading = jnp.exp2(old_peak - peak)
            total = total + old_stats_ref[:, heads + head : heads + head + 1] * fading
            numerator = numerator + old_total_ref[:, columns] * fading
        if last:
            rest[0][:, columns] = (numerator / total).astype(jnp.bfloat16)
        else:
            rest[1][:, columns] = numerator
            stats = jnp.where(lane == head, peak, stats)
            stats = jnp.where(lane == heads + head, total, stats)
    if not last:
        rest[0][...] = stats


def attend(queries, bias, keys, values, state=(), last=False):
    tokens, features = queries.shape
    rows = bias.shape[1]
    if last:
        out_shape = jax.ShapeDtypeStruct((tokens, features), jnp.bfloat16)
    else:
        out_shape = (
            jax.ShapeDtypeStruct((tokens, LANES), jnp.float32),
            jax.ShapeDtypeStruct((tokens, features), jnp.float32),
        )
    heads = features // HEAD_DIM
    return pl.pallas_call(
        functools.partial(attend_kernel, len(keys), bool(state), last),
        out_shape=out_shape,
        cost_estimate=pl.CostEstimate(
            flops=4 * tokens * rows * features,
            transcendentals=heads * tokens * rows,
            bytes_accessed=4 * rows * features + 4 * tokens * features,
        ),
        name="attend_last" if last else "attend",
    )(queries, bias, *keys, *values, *state)


def shards(
    queries,
    key_rows,
    values,
    query_gain,
    key_gain,
    pattern,
    reference_keys,
    reference_values,
    reference_live,
):
    tokens, features = queries.shape
    heads = features // HEAD_DIM
    even = lax.axis_index("frm") % 2 == 0

    far1_values = fetch(values, far_first)
    near_values = fetch(values, beside)

    slots = reference_keys.shape[0]
    live = (jnp.arange(slots, dtype=jnp.int32) < reference_live[0]).astype(jnp.bfloat16)
    reference_rows = jnp.concatenate(
        [
            reference_keys,
            reference_values,
            jnp.broadcast_to(live[:, None], (slots, LANES)),
        ],
        axis=1,
    )
    reference_rows = gather_rows(reference_rows)

    squares = lax.psum(
        jnp.stack(
            [
                jnp.sum(jnp.square(rows.astype(jnp.float32)), axis=1)
                for rows in (queries, key_rows)
            ]
        ),
        "tp",
    )

    def normalize(rows, gain, square_sum):
        scale = lax.rsqrt(square_sum / (HEADS * HEAD_DIM) + EPSILON)
        return (rows.astype(jnp.float32) * scale[:, None] * gain).astype(jnp.bfloat16)

    normed_keys = normalize(key_rows, key_gain, squares[1])
    normed_queries = normalize(queries, query_gain, squares[0])

    far1_keys = fetch(normed_keys, far_first)
    near_keys = fetch(normed_keys, beside)
    far2_values = fetch(after(values, far1_values), far_second)
    passed_values = fetch(far1_values, beside)
    far2_keys = fetch(after(normed_keys, far1_keys), far_second)
    passed_keys = fetch(far1_keys, beside)

    flags = jnp.where(even, pattern[0, ::-1], pattern[0]) > 0
    closed = jnp.where(flags, 0.0, -jnp.inf).astype(jnp.float32)
    spread = jnp.repeat(closed, tokens)[None, :]
    far1_bias, near_bias, passed_bias, far2_bias = (
        spread[:, i * tokens : (i + 1) * tokens] for i in range(4)
    )
    own_bias = jnp.zeros((1, tokens), jnp.float32)
    reference_bias = jnp.where(
        reference_rows[:, 2 * features] > 0.5, 0.0, -jnp.inf
    ).astype(jnp.float32)[None, :]

    state = attend(
        normed_queries,
        jnp.concatenate([own_bias, near_bias], axis=1),
        [normed_keys, near_keys],
        [values, near_values],
    )
    state = attend(
        normed_queries,
        jnp.concatenate([far1_bias, reference_bias], axis=1),
        [far1_keys, reference_rows[:, :features]],
        [far1_values, reference_rows[:, features : 2 * features]],
        state,
    )
    return attend(
        normed_queries,
        jnp.concatenate([passed_bias, far2_bias], axis=1),
        [passed_keys, far2_keys],
        [passed_values, far2_values],
        state,
        last=True,
    )


def solution(mesh):
    in_specs = (
        P(("grp", "frm"), "tp"),
        P(("grp", "frm"), "tp"),
        P(("grp", "frm"), "tp"),
        P("tp"),
        P("tp"),
        P(("grp", "frm"), None),
        P(("grp", "frm"), "tp"),
        P(("grp", "frm"), "tp"),
        P(("grp", "frm")),
    )
    out_specs = P(("grp", "frm"), "tp")
    return jax.shard_map(shards, mesh=mesh, in_specs=in_specs, out_specs=out_specs, check_vma=False)
```

time: 188 us -> 92.5 us (0.49)
  blocking collectives: 134 us -> 2.47 us
  waiting for transfers between devices: 0.01 us -> 41.3 us
  local copies, waits for them, and re-layouts: 28.9 us -> 4.19 us
  Pallas kernels: 0 us -> 19.9 us
  starting transfers between devices: 7.92 us -> 16.3 us
  matrix products: 6.85 us -> 0 us
    all_gather x2 -> x0, blocking collectives: 113 us -> none  [the longest x1 82.3 us: shards(): lax.all_gather(reference_keys, 'frm', axis=0, tiled=True)]
    ppermute x4 -> x11, waiting for transfers between devices: 0.01 us -> 41.3 us  [fetch(): return lax.ppermute(block, 'frm', [(source_of(i) % n, i) for i in range(n)])]
    pallas_call x0 -> x3, Pallas kernels: none -> 19.9 us  [attend(): pl.pallas_call(functools.partial(attend_kernel, len(keys), bool(state), l...]
    unnamed x1 -> x0, blocking collectives: 18.7 us -> none
    slice x14 -> x1, local copies, waits for them, and re-layouts: 13.6 us -> 0.07 us  [shards(): spread[:, i * tokens:(i + 1) * tokens]]
    ppermute x4 -> x11, starting transfers between devices: 7.92 us -> 16.3 us  [fetch(): return lax.ppermute(block, 'frm', [(source_of(i) % n, i) for i in range(n)])]
    dot_general x8 -> x0, matrix products: 6.85 us -> none  [the longest x4 4 us: absorb(): jnp.einsum('thd,nhd->htn', query_part, key_part, preferred_element_type=j...]
    concatenate x13 -> x2, local copies, waits for them, and re-layouts: 7.12 us -> 1.23 us  [the longest x1 0.67 us: shards(): jnp.concatenate([own_bias, near_bias], axis=1)]
  transfers between devices with their start and end apart: 4 -> 11, of which waited for: 0 -> 2; matrix products, arithmetic and copies ran while one was open for 7% -> 8% of each run, Pallas kernels for 0% -> 14%
where the time goes in v1:
time: 92.5 us; the launch traced here: 92 us
  waiting for transfers between devices  41.3 us (45%)
  Pallas kernels  19.9 us (22%)
  starting transfers between devices  16.3 us (18%)
  other arithmetic  6.98 us (8%)
  local copies, waits for them, and re-layouts  4.19 us (5%)
  blocking collectives  2.47 us (3%)
    ppermute x11, waiting for transfers between devices, fetch(): return lax.ppermute(block, 'frm', [(source_of(i) % n, i) for i in range(n)])  41.3 us
    pallas_call x3, Pallas kernels, attend(): pl.pallas_call(functools.partial(attend_kernel, len(keys), bool(state), l...  19.9 us
    ppermute x11, starting transfers between devices, fetch(): return lax.ppermute(block, 'frm', [(source_of(i) % n, i) for i in range(n)])  16.3 us
    unnamed x28, local copies, waits for them, and re-layouts  2.56 us
    psum x1, blocking collectives, shards(): lax.psum(jnp.stack([jnp.sum(jnp.square(rows.astype(jnp.float32)), axis=1)...  2.47 us
    concatenate x3, other arithmetic, gather_rows(): rows = jnp.concatenate([rows, fetch(rows, lambda i: i ^ distance)], axis=0)  2.21 us
  transfers between devices with their start and end apart: 11, of which 2 were waited for; matrix products, arithmetic and copies ran while one was open for 8% of the time, Pallas kernels for 14%

profile of v1, /device:TPU:0, one launch (start us, length us, event | category | flops | bytes accessed | tf_op | source)
XLA Modules:
  0.0 92.0 jit_solution(5069840706316851830)
XLA Ops:
  0.0 0.0 copy-start.1
  0.7 0.1 broadcast_in_dim.34
  0.8 0.7 pad_maximum_fusion.8
  1.5 3.0 %collective-permute-start.6 = (bf16[4,2688]{1,0:T(4,128)(2,1)S(1)}, bf16[4,2688]{1,0:T(4,128)(2,1)S(1)}, u32[]{:S(2)}, u32[]{:S(2)}) collective-permute-start(bf16[4,2688]{1,0:T(4,128)(2,1)S(1)} %pad_maximum_fusion.8), channel_id=1, source_target_pairs={{2,0},{0,2},{6,4},{4,6},{10,8},{8,10},{14,12},{12,14},{3,1},{1,3},... | collective-permute-start | bytes 64520 | tf_op jit(solution)/shard_map/ppermute | solution.py:21
  4.5 1.2 %fusion = f32[192]{0:T(256)S(1)} fusion(bf16[192,1280]{1,0:T(8,128)(2,1)} %param.9), kind=kLoop, calls=%fused_computation.4 | loop fusion | flops 737088 | bytes 492288 | tf_op jit(solution)/shard_map/reduce_sum | solution.py:155
  5.7 0.0 copy-done.1
  5.7 0.0 copy-start.9
  5.8 0.0 copy-start.10
  5.8 0.2 fusion.3
  5.9 0.0 copy-start.11
  6.0 2.5 %psum.7 = f32[2,192]{1,0:T(2,128)S(1)} all-reduce(f32[2,192]{1,0:T(2,128)S(1)} %pad_maximum_fusion.9), channel_id=1, replica_groups=mesh['grp'=2,'frm'=8,'tp'=2] {'tp'}, use_global_device_ids=true, to_apply=%region_2.3 | all-reduce | flops 384 | bytes 3072 | tf_op jit(solution)/shard_map/psum | solution.py:152
  8.5 0.0 copy-done.11
  8.5 0.0 copy-start.3
  8.5 0.0 copy-start.2
  8.5 0.2 fusion.5.refs_2_
  8.7 0.0 copy-start
  8.7 0.1 collective-permute-start.9
  8.8 4.1 %collective-permute-start = (bf16[192,1280]{1,0:T(8,128)(2,1)S(1)}, bf16[192,1280]{1,0:T(8,128)(2,1)S(1)}, u32[]{:S(2)}, u32[]{:S(2)}) collective-permute-start(bf16[192,1280]{1,0:T(8,128)(2,1)S(1)} %fusion.5.refs_2_), channel_id=1, source_target_pairs={{4,0},{14,2},{8,4},{2,6},{12,8},{6,10},{0,12},{10,14},{5,1},{15,3}... | collective-permute-start | bytes 1474568 | tf_op jit(solution)/shard_map/ppermute | solution.py:21
  12.9 0.0 copy-done.3
  12.9 0.0 collective-permute-start.10
  12.9 1.7 %collective-permute-start.3 = (bf16[192,1280]{1,0:T(8,128)(2,1)S(1)}, bf16[192,1280]{1,0:T(8,128)(2,1)S(1)}, u32[]{:S(2)}, u32[]{:S(2)}) collective-permute-start(bf16[192,1280]{1,0:T(8,128)(2,1)S(1)} %copy-done.3), channel_id=1, source_target_pairs={{4,0},{14,2},{8,4},{2,6},{12,8},{6,10},{0,12},{10,14},{5,1},{15,3}... | collective-permute-start | bytes 1474568 | tf_op jit(solution)/shard_map/ppermute | solution.py:21
  14.6 0.0 collective-permute-done.6
  14.6 0.0 copy-done.9
  14.6 0.0 copy-done.10
  14.6 0.0 copy-start.12
  14.7 0.4 collective-permute-start.7
  15.0 0.0 copy-done.2
  15.0 0.3 copy-done.12
  15.3 1.0 %fusion.2.refs_0_ = bf16[192,1280]{1,0:T(8,128)(2,1)} fusion(bf16[192,1280]{1,0:T(8,128)(2,1)S(1)} %copy-done.2, f32[1280]{0:T(1024)S(1)} %copy-done.12, f32[192]{0:T(256)S(1)} %bitcast.9), kind=kLoop, calls=%fused_computation.6 | loop fusion | flops 983040 | bytes 988928 | tf_op jit(solution)/shard_map/convert_element_type | solution.py:164
  16.3 0.7 copy-done.13
  17.0 0.1 rev.3
  17.1 17.8 %collective-permute-done.7 = bf16[8,2688]{1,0:T(8,128)(2,1)S(1)} collective-permute-done((bf16[8,2688]{1,0:T(8,128)(2,1)S(1)}, bf16[8,2688]{1,0:T(8,128)(2,1)S(1)}, u32[]{:S(2)}, u32[]{:S(2)}) %collective-permute-start.7) | collective-permute-done | bytes 43040 | tf_op jit(solution)/shard_map/ppermute | solution.py:21
  34.9 0.7 pad_maximum_fusion
  35.5 2.4 %collective-permute-start.8 = (bf16[16,2688]{1,0:T(8,128)(2,1)}, bf16[16,2688]{1,0:T(8,128)(2,1)}, u32[]{:S(2)}, u32[]{:S(2)}) collective-permute-start(bf16[16,2688]{1,0:T(8,128)(2,1)} %pad_maximum_fusion), channel_id=1, source_target_pairs={{8,0},{10,2},{12,4},{14,6},{0,8},{2,10},{4,12},{6,14},{9,1},{11,3}... | collective-permute-start | bytes 258056 | tf_op jit(solution)/shard_map/ppermute | solution.py:21
  38.0 0.1 broadcast_in_dim.33
  38.0 0.1 broadcast_in_dim_reshape.3
  38.1 0.0 collective-permute-done.refs_2_
  38.1 0.0 copy-done
  38.1 2.5 %collective-permute-start.2 = (bf16[192,1280]{1,0:T(8,128)(2,1)S(1)}, bf16[192,1280]{1,0:T(8,128)(2,1)S(1)}, u32[]{:S(2)}, u32[]{:S(2)}) collective-permute-start(bf16[192,1280]{1,0:T(8,128)(2,1)S(1)} %fusion.5.refs_2_), channel_id=1, source_target_pairs={{12,0},{6,2},{0,4},{10,6},{4,8},{14,10},{8,12},{2,14},{13,1},{7,3}... | collective-permute-start | bytes 1474568 | tf_op jit(solution)/shard_map/ppermute | solution.py:21
  40.6 0.0 collective-permute-done.3.refs_4_
  40.6 0.1 collective-permute-start.5
  40.7 23.4 %collective-permute-done.8 = bf16[16,2688]{1,0:T(8,128)(2,1)} collective-permute-done((bf16[16,2688]{1,0:T(8,128)(2,1)}, bf16[16,2688]{1,0:T(8,128)(2,1)}, u32[]{:S(2)}, u32[]{:S(2)}) %collective-permute-start.8) | collective-permute-done | bytes 86048 | tf_op jit(solution)/shard_map/ppermute | solution.py:21
  64.2 0.0 collective-permute-start.1
  64.2 0.0 collective-permute-done.9.refs_3_
  64.2 2.0 %collective-permute-start.4 = (bf16[192,1280]{1,0:T(8,128)(2,1)S(1)}, bf16[192,1280]{1,0:T(8,128)(2,1)}, u32[]{:S(2)}, u32[]{:S(2)}) collective-permute-start(bf16[192,1280]{1,0:T(8,128)(2,1)S(1)} %collective-permute-done.3.refs_4_), channel_id=1, source_target_pairs={{2,0},{0,2},{6,4},{4,6},{10,8},{8,10},{14,12},{12,14},{3,1},{1,3},... | collective-permute-start | bytes 1474568 | tf_op jit(solution)/shard_map/ppermute | solution.py:21
  66.2 0.1 fusion.11
  66.3 0.6 concatenate.30.refs_1_
  66.8 0.7 concatenate.29.refs_1_
  67.5 0.8 select_reduce_fusion
  68.3 0.7 pad_maximum_fusion.10.refs_1_
  69.0 1.5 %pad_maximum_fusion.1 = (bf16[32,1280]{1,0:T(8,128)(2,1)}, bf16[32,1280]{1,0:T(8,128)(2,1)}) fusion(bf16[16,2688]{1,0:T(8,128)(2,1)} %collective-permute-done.8, bf16[8,2688]{1,0:T(8,128)(2,1)S(1)} %collective-permute-done.7, bf16[4,2688]{1,0:T(4,128)(2,1)S(1)} %collective-permute-done.6, bf16[4,128]{1,0:T(4,128)(2,1)S(1)} %broadcast_in_dim.34, ...), kind=kLoop, calls=%fused_computation.11 | loop fusion | flops 983040 | bytes 335872 | tf_op jit(solution)/shard_map/concatenate | solution.py:46
  70.5 0.0 collective-permute-done.10.refs_5_
  70.5 0.0 copy-done.6
  70.5 0.8 copy-done.7
  71.3 5.6 %attend.2 = (f32[192,128]{1,0:T(8,128)}, f32[192,1280]{1,0:T(8,128)}) custom-call(bf16[192,1280]{1,0:T(8,128)(2,1)} %fusion.2.refs_0_, f32[1,384]{1,0:T(1,128)} %concatenate.29.refs_1_, bf16[192,1280]{1,0:T(8,128)(2,1)} %copy-done, bf16[192,1280]{1,0:T(8,128)(2,1)} %copy-done.6, bf16[192,1280]{1,0:T(8,128)(2,1)} %refs_4_.1, bf16[192,1280]{1,0:T(8,128)(2,1)} %copy-done.7), custom_call_target="tpu_custom_call" | custom-call | flops 377487360 | bytes 2949120 | tf_op jit(solution)/shard_map/attend/pallas_call | solution.py:110
  76.8 0.0 copy-done.4
  76.8 0.0 copy-done.5
  76.8 7.3 %attend.3 = (f32[192,128]{1,0:T(8,128)}, f32[192,1280]{1,0:T(8,128)}) custom-call(bf16[192,1280]{1,0:T(8,128)(2,1)} %fusion.2.refs_0_, f32[1,224]{1,0:T(1,128)} %pad_maximum_fusion.10.refs_1_, bf16[192,1280]{1,0:T(8,128)(2,1)} %copy-done.4, bf16[32,1280]{1,0:T(8,128)(2,1)} %get-tuple-element.18.refs_3_, bf16[192,1280]{1,0:T(8,128)(2,1)} %copy-done.5, ...), custom_call_target="tpu_custom_call" | custom-call | flops 220200960 | bytes 2129920 | tf_op jit(solution)/shard_map/attend/pallas_call | solution.py:110
  84.2 0.0 collective-permute-done.2.refs_3_
  84.2 0.0 collective-permute-done.1.refs_2_
  84.2 0.0 collective-permute-done.5.refs_5_
  84.2 0.0 collective-permute-done.4.refs_4_
  84.2 0.8 copy-done.8
  85.0 7.0 %attend_last.1 = bf16[192,1280]{1,0:T(8,128)(2,1)} custom-call(bf16[192,1280]{1,0:T(8,128)(2,1)} %fusion.2.refs_0_, f32[1,384]{1,0:T(1,128)} %concatenate.30.refs_1_, bf16[192,1280]{1,0:T(8,128)(2,1)} %collective-permute-done.1.refs_2_, bf16[192,1280]{1,0:T(8,128)(2,1)} %copy-done.8, bf16[192,1280]{1,0:T(8,128)(2,1)} %collective-permute-done.4.refs_4_, ...), custom_call_target="tpu_custom_call" | custom-call | flops 377487360 | bytes 2949120 | tf_op jit(solution)/shard_map/attend_last/pallas_call | solution.py:110
  (11 shorter events, 0.1 us)
Async XLA Ops:
  0.0 5.7 %copy-start.1 = (bf16[192,1280]{1,0:T(8,128)(2,1)S(1)}, bf16[192,1280]{1,0:T(8,128)(2,1)}, u32[]{:S(2)}) copy-start(bf16[192,1280]{1,0:T(8,128)(2,1)} %param.10) | copy-start | bytes 1474564
  1.5 13.1 %collective-permute-start.6 = (bf16[4,2688]{1,0:T(4,128)(2,1)S(1)}, bf16[4,2688]{1,0:T(4,128)(2,1)S(1)}, u32[]{:S(2)}, u32[]{:S(2)}) collective-permute-start(bf16[4,2688]{1,0:T(4,128)(2,1)S(1)} %pad_maximum_fusion.8), channel_id=1, source_target_pairs={{2,0},{0,2},{6,4},{4,6},{10,8},{8,10},{14,12},{12,14},{3,1},{1,3},... | collective-permute-start | bytes 64520 | tf_op jit(solution)/shard_map/ppermute | solution.py:21
  5.7 8.9 %copy-start.9 = (bf16[4,1280]{1,0:T(4,128)(2,1)S(1)}, bf16[4,1280]{1,0:T(4,128)(2,1)}, u32[]{:S(2)}) copy-start(bf16[4,1280]{1,0:T(4,128)(2,1)} %param.16) | copy-start | bytes 30724
  5.8 8.9 %copy-start.10 = (bf16[4,1280]{1,0:T(4,128)(2,1)S(1)}, bf16[4,1280]{1,0:T(4,128)(2,1)}, u32[]{:S(2)}) copy-start(bf16[4,1280]{1,0:T(4,128)(2,1)} %param.15) | copy-start | bytes 30724
  5.9 2.5 %copy-start.11 = (f32[1280]{0:T(1024)S(1)}, f32[1280]{0:T(1024)}, u32[]{:S(2)}) copy-start(f32[1280]{0:T(1024)} %param.13) | copy-start | bytes 15364
  8.5 4.4 %copy-start.3 = (bf16[192,1280]{1,0:T(8,128)(2,1)S(1)}, bf16[192,1280]{1,0:T(8,128)(2,1)}, u32[]{:S(2)}) copy-start(bf16[192,1280]{1,0:T(8,128)(2,1)} %refs_4_.1) | copy-start | bytes 1474564
  8.5 6.6 %copy-start.2 = (bf16[192,1280]{1,0:T(8,128)(2,1)S(1)}, bf16[192,1280]{1,0:T(8,128)(2,1)}, u32[]{:S(2)}) copy-start(bf16[192,1280]{1,0:T(8,128)(2,1)} %param.9) | copy-start | bytes 1474564
  8.7 29.4 %copy-start = (bf16[192,1280]{1,0:T(8,128)(2,1)}, bf16[192,1280]{1,0:T(8,128)(2,1)S(1)}, u32[]{:S(2)}) copy-start(bf16[192,1280]{1,0:T(8,128)(2,1)S(1)} %fusion.5.refs_2_) | copy-start | bytes 1474564
  8.7 55.5 %collective-permute-start.9 = (bf16[192,1280]{1,0:T(8,128)(2,1)S(1)}, bf16[192,1280]{1,0:T(8,128)(2,1)S(1)}, u32[]{:S(2)}, u32[]{:S(2)}) collective-permute-start(bf16[192,1280]{1,0:T(8,128)(2,1)S(1)} %fusion.5.refs_2_), channel_id=1, source_target_pairs={{2,0},{0,2},{6,4},{4,6},{10,8},{8,10},{14,12},{12,14},{3,1},{1,3},... | collective-permute-start | bytes 1474568 | tf_op jit(solution)/shard_map/ppermute | solution.py:21
  8.8 29.4 %collective-permute-start = (bf16[192,1280]{1,0:T(8,128)(2,1)S(1)}, bf16[192,1280]{1,0:T(8,128)(2,1)S(1)}, u32[]{:S(2)}, u32[]{:S(2)}) collective-permute-start(bf16[192,1280]{1,0:T(8,128)(2,1)S(1)} %fusion.5.refs_2_), channel_id=1, source_target_pairs={{4,0},{14,2},{8,4},{2,6},{12,8},{6,10},{0,12},{10,14},{5,1},{15,3}... | collective-permute-start | bytes 1474568 | tf_op jit(solution)/shard_map/ppermute | solution.py:21
  12.9 57.6 %collective-permute-start.10 = (bf16[192,1280]{1,0:T(8,128)(2,1)S(1)}, bf16[192,1280]{1,0:T(8,128)(2,1)S(1)}, u32[]{:S(2)}, u32[]{:S(2)}) collective-permute-start(bf16[192,1280]{1,0:T(8,128)(2,1)S(1)} %copy-done.3), channel_id=1, source_target_pairs={{2,0},{0,2},{6,4},{4,6},{10,8},{8,10},{14,12},{12,14},{3,1},{1,3},... | collective-permute-start | bytes 1474568 | tf_op jit(solution)/shard_map/ppermute | solution.py:21
  12.9 27.7 %collective-permute-start.3 = (bf16[192,1280]{1,0:T(8,128)(2,1)S(1)}, bf16[192,1280]{1,0:T(8,128)(2,1)S(1)}, u32[]{:S(2)}, u32[]{:S(2)}) collective-permute-start(bf16[192,1280]{1,0:T(8,128)(2,1)S(1)} %copy-done.3), channel_id=1, source_target_pairs={{4,0},{14,2},{8,4},{2,6},{12,8},{6,10},{0,12},{10,14},{5,1},{15,3}... | collective-permute-start | bytes 1474568 | tf_op jit(solution)/shard_map/ppermute | solution.py:21
  14.6 0.7 copy-start.12
  14.7 20.2 %collective-permute-start.7 = (bf16[8,2688]{1,0:T(8,128)(2,1)S(1)}, bf16[8,2688]{1,0:T(8,128)(2,1)S(1)}, u32[]{:S(2)}, u32[]{:S(2)}) collective-permute-start(bf16[8,2688]{1,0:T(8,128)(2,1)S(1)} %pad_maximum_fusion.7), channel_id=1, source_target_pairs={{4,0},{6,2},{0,4},{2,6},{12,8},{14,10},{8,12},{10,14},{5,1},{7,3},... | collective-permute-start | bytes 129032 | tf_op jit(solution)/shard_map/ppermute | solution.py:21
  16.3 0.7 copy-start.13
  35.5 28.6 %collective-permute-start.8 = (bf16[16,2688]{1,0:T(8,128)(2,1)}, bf16[16,2688]{1,0:T(8,128)(2,1)}, u32[]{:S(2)}, u32[]{:S(2)}) collective-permute-start(bf16[16,2688]{1,0:T(8,128)(2,1)} %pad_maximum_fusion), channel_id=1, source_target_pairs={{8,0},{10,2},{12,4},{14,6},{0,8},{2,10},{4,12},{6,14},{9,1},{11,3}... | collective-permute-start | bytes 258056 | tf_op jit(solution)/shard_map/ppermute | solution.py:21
  38.1 38.7 %copy-start.4 = (bf16[192,1280]{1,0:T(8,128)(2,1)}, bf16[192,1280]{1,0:T(8,128)(2,1)S(1)}, u32[]{:S(2)}) copy-start(bf16[192,1280]{1,0:T(8,128)(2,1)S(1)} %collective-permute-done.refs_2_) | copy-start | bytes 1474564
  38.1 46.1 %collective-permute-start.2 = (bf16[192,1280]{1,0:T(8,128)(2,1)S(1)}, bf16[192,1280]{1,0:T(8,128)(2,1)S(1)}, u32[]{:S(2)}, u32[]{:S(2)}) collective-permute-start(bf16[192,1280]{1,0:T(8,128)(2,1)S(1)} %fusion.5.refs_2_), channel_id=1, source_target_pairs={{12,0},{6,2},{0,4},{10,6},{4,8},{14,10},{8,12},{2,14},{13,1},{7,3}... | collective-permute-start | bytes 1474568 | tf_op jit(solution)/shard_map/ppermute | solution.py:21
  40.6 36.2 %copy-start.5 = (bf16[192,1280]{1,0:T(8,128)(2,1)}, bf16[192,1280]{1,0:T(8,128)(2,1)S(1)}, u32[]{:S(2)}) copy-start(bf16[192,1280]{1,0:T(8,128)(2,1)S(1)} %collective-permute-done.3.refs_4_) | copy-start | bytes 1474564
  40.6 43.6 %collective-permute-start.5 = (bf16[192,1280]{1,0:T(8,128)(2,1)S(1)}, bf16[192,1280]{1,0:T(8,128)(2,1)}, u32[]{:S(2)}, u32[]{:S(2)}) collective-permute-start(bf16[192,1280]{1,0:T(8,128)(2,1)S(1)} %copy-done.3), channel_id=1, source_target_pairs={{12,0},{6,2},{0,4},{10,6},{4,8},{14,10},{8,12},{2,14},{13,1},{7,3}... | collective-permute-start | bytes 1474568 | tf_op jit(solution)/shard_map/ppermute | solution.py:21
  64.2 20.0 %collective-permute-start.1 = (bf16[192,1280]{1,0:T(8,128)(2,1)S(1)}, bf16[192,1280]{1,0:T(8,128)(2,1)}, u32[]{:S(2)}, u32[]{:S(2)}) collective-permute-start(bf16[192,1280]{1,0:T(8,128)(2,1)S(1)} %collective-permute-done.refs_2_), channel_id=1, source_target_pairs={{2,0},{0,2},{6,4},{4,6},{10,8},{8,10},{14,12},{12,14},{3,1},{1,3},... | collective-permute-start | bytes 1474568 | tf_op jit(solution)/shard_map/ppermute | solution.py:21
  64.2 6.3 %copy-start.6 = (bf16[192,1280]{1,0:T(8,128)(2,1)}, bf16[192,1280]{1,0:T(8,128)(2,1)S(1)}, u32[]{:S(2)}) copy-start(bf16[192,1280]{1,0:T(8,128)(2,1)S(1)} %collective-permute-done.9.refs_3_) | copy-start | bytes 1474564
  64.2 20.0 %collective-permute-start.4 = (bf16[192,1280]{1,0:T(8,128)(2,1)S(1)}, bf16[192,1280]{1,0:T(8,128)(2,1)}, u32[]{:S(2)}, u32[]{:S(2)}) collective-permute-start(bf16[192,1280]{1,0:T(8,128)(2,1)S(1)} %collective-permute-done.3.refs_4_), channel_id=1, source_target_pairs={{2,0},{0,2},{6,4},{4,6},{10,8},{8,10},{14,12},{12,14},{3,1},{1,3},... | collective-permute-start | bytes 1474568 | tf_op jit(solution)/shard_map/ppermute | solution.py:21
  70.5 0.8 copy-start.7
  84.2 0.8 copy-start.8

commit v2 on v0

v2 whole, which is shorter than its diff:
```python
import math

import jax
import jax.numpy as jnp
from jax import lax
from jax.experimental import pallas as pl
from jax.experimental.pallas import tpu as pltpu
from jax.sharding import PartitionSpec as P

HEADS = 20
HEAD_DIM = 128
WINDOW = 2
EPSILON = 1e-06
LANES = 128
SCRATCH_BYTES = 24 * 2**20
DEAD = 100.0
TO_LOG2 = HEAD_DIM ** (-0.5) * math.log2(math.e)


def fetch(block, source_of, axis="frm"):
    n = lax.axis_size(axis)
    return lax.ppermute(block, axis, [(source_of(i) % n, i) for i in range(n)])


def after(value, *earlier):
    return lax.optimization_barrier((value,) + earlier)[0]


def far_first(i):
    return i + WINDOW if i % 2 == 0 else i - WINDOW


def far_second(i):
    return i - WINDOW if i % 2 == 0 else i + WINDOW


def beside(i):
    return i + 1 if i % 2 == 0 else i - 1


def in_vmem(array):
    return pltpu.with_memory_space_constraint(array, pltpu.VMEM)


VMEM = pl.BlockSpec(memory_space=pltpu.VMEM)
SMEM = pl.BlockSpec(memory_space=pltpu.SMEM)
PARAMS = pltpu.CompilerParams(vmem_limit_bytes=SCRATCH_BYTES)


CHEAP = pl.CostEstimate(flops=1, transcendentals=0, bytes_accessed=1)


def head_columns(head):
    return slice(head * HEAD_DIM, (head + 1) * HEAD_DIM)


def score(queries, keys):
    return lax.dot_general(
        queries, keys, (((1,), (1,)), ((), ())), preferred_element_type=jnp.float32
    )


def pack_kernel(live_ref, keys_ref, values_ref, rows_ref, live_smem, sems):
    slots, features = keys_ref.shape
    copies = [
        pltpu.make_async_copy(live_ref, live_smem, sems.at[0]),
        pltpu.make_async_copy(keys_ref, rows_ref.at[:, :features], sems.at[1]),
        pltpu.make_async_copy(values_ref, rows_ref.at[:, features:], sems.at[2]),
    ]
    for copy in copies:
        copy.start()
    for copy in copies:
        copy.wait()
    slot = lax.broadcasted_iota(jnp.int32, (slots, features), 0)
    keys = rows_ref[:, :features].astype(jnp.float32)
    rows_ref[:, :features] = jnp.where(slot < live_smem[0], keys, DEAD).astype(jnp.bfloat16)


def pack_rows(live, keys, values):
    slots, features = keys.shape
    return pl.pallas_call(
        pack_kernel,
        out_shape=pltpu.VMEM((slots, 2 * features), jnp.bfloat16),
        in_specs=[pl.BlockSpec(memory_space=pl.ANY)] * 3,
        out_specs=VMEM,
        scratch_shapes=[pltpu.SMEM((1,), jnp.int32), pltpu.SemaphoreType.DMA((3,))],
        compiler_params=PARAMS,
        cost_estimate=CHEAP,
        name="pack_rows",
    )(live, keys, values)


def attach_kernel(keys_ref, *refs):
    *row_refs, packed_ref = refs
    tokens, features = keys_ref.shape
    packed_ref[:tokens] = keys_ref[...]
    count = sum(ref.shape[0] for ref in row_refs)
    first = tokens
    for ref in row_refs:
        slots = ref.shape[0]
        packed_ref[first : first + slots] = ref[:, :features]
        packed_ref[first + count : first + count + slots] = ref[:, features:]
        first += slots


def attach_rows(keys, rows):
    tokens, features = keys.shape
    count = sum(part.shape[0] for part in rows)
    return pl.pallas_call(
        attach_kernel,
        out_shape=pltpu.VMEM((tokens + 2 * count, features), jnp.bfloat16),
        in_specs=[VMEM] * (1 + len(rows)),
        out_specs=VMEM,
        compiler_params=PARAMS,
        cost_estimate=CHEAP,
        name="attach_rows",
    )(*map(in_vmem, (keys, *rows)))


def squares_kernel(first_ref, second_ref, squares_ref):
    def square_sum(ref):
        rows = ref[: squares_ref.shape[0]].astype(jnp.float32)
        return jnp.sum(rows * rows, axis=1, keepdims=True)

    lane = lax.broadcasted_iota(jnp.int32, squares_ref.shape, 1)
    squares_ref[...] = jnp.where(lane == 0, square_sum(first_ref), square_sum(second_ref))


def square_sums(first, second, name):
    squares = pl.pallas_call(
        squares_kernel,
        out_shape=pltpu.VMEM((min(first.shape[0], second.shape[0]), LANES), jnp.float32),
        in_specs=[VMEM, VMEM],
        out_specs=VMEM,
        compiler_params=PARAMS,
        cost_estimate=CHEAP,
        name=name,
    )(in_vmem(first), in_vmem(second))
    return squares, fetch(squares, lambda i: i ^ 1, "tp")


def normalized(rows_ref, gain_ref, squares_refs, column):
    square_sum = sum(ref[:, column : column + 1] for ref in squares_refs)
    scale = lax.rsqrt(square_sum / (HEADS * HEAD_DIM) + EPSILON)
    rows = rows_ref[: square_sum.shape[0]].astype(jnp.float32)
    return (rows * scale * gain_ref[...][None, :]).astype(jnp.bfloat16)


def pattern_flag(pattern_ref, column):
    even = lax.rem(lax.axis_index("frm"), 2) == 0
    return jnp.where(even, pattern_ref[0, 2 * WINDOW - 1 - column], pattern_ref[0, column]) > 0


def block_bias(flag, tokens):
    return jnp.where(flag, jnp.zeros((1, tokens), jnp.float32), -jnp.inf)


def early_kernel(
    pattern_ref,
    query_gain,
    key_gain,
    queries,
    own_keys,
    near_keys,
    far_keys,
    own_squares,
    other_own_squares,
    far_squares,
    other_far_squares,
    own_values,
    near_values,
    far_values,
    query_ref,
    peaks_ref,
    totals_ref,
    partial_ref,
    keys_ref,
    scores_ref,
    weights_ref,
):
    tokens, features = query_ref.shape
    heads = features // HEAD_DIM
    bias = jnp.concatenate(
        [
            jnp.zeros((1, tokens), jnp.float32),
            block_bias(pattern_flag(pattern_ref, 1), tokens),
            block_bias(pattern_flag(pattern_ref, 0), tokens),
        ],
        axis=1,
    )
    own, far = (own_squares, other_own_squares), (far_squares, other_far_squares)
    query_ref[...] = normalized(queries, query_gain, own, 0)
    keys_ref[:tokens] = normalized(own_keys, key_gain, own, 1)
    keys_ref[tokens : 2 * tokens] = normalized(near_keys, key_gain, far, 0)
    keys_ref[2 * tokens :] = normalized(far_keys, key_gain, far, 1)
    for head in range(heads):
        columns = head_columns(head)
        scores_ref[head] = score(query_ref[:, columns], keys_ref[:, columns])
    for head in range(heads):
        scores = scores_ref[head] * TO_LOG2 + bias
        peak = jnp.max(scores, axis=1, keepdims=True)
        weights = jnp.exp2(scores - peak)
        total = jnp.sum(weights, axis=1, keepdims=True)
        weights_ref[head] = weights.astype(jnp.bfloat16)
        peaks_ref[head] = jnp.broadcast_to(peak, (tokens, LANES))
        totals_ref[head] = jnp.broadcast_to(total, (tokens, LANES))
    for head in range(heads):
        columns = head_columns(head)
        values = [ref[:, columns] for ref in (own_values, near_values, far_values)]
        partial_ref[:, columns] = jnp.dot(
            weights_ref[head],
            jnp.concatenate(values, axis=0),
            preferred_element_type=jnp.float32,
        )


def late_keys_kernel(
    pattern_ref,
    key_gain,
    query_ref,
    passed_keys,
    far_keys,
    squares,
    other_squares,
    own_packed,
    near_packed,
    old_peaks_ref,
    old_totals_ref,
    old_partial_ref,
    inverses_ref,
    partial_ref,
    weights_ref,
    keys_ref,
    values_ref,
    scores_ref,
):
    tokens, features = query_ref.shape
    heads = features // HEAD_DIM
    blocks = 2 * tokens
    count = values_ref.shape[0] // 2
    for place, packed in enumerate((own_packed, near_packed)):
        first = place * count
        keys_ref[blocks + first : blocks + first + count] = packed[tokens : tokens + count]
        values_ref[first : first + count] = packed[tokens + count :]
    marks = score(jnp.ones((8, LANES), jnp.bfloat16), keys_ref[blocks:, :LANES])
    bias = jnp.concatenate(
        [
            block_bias(pattern_flag(pattern_ref, 2), tokens),
            block_bias(pattern_flag(pattern_ref, 3), tokens),
            jnp.where(marks[:1] < 0.5 * DEAD * LANES, 0.0, -jnp.inf),
        ],
        axis=1,
    )
    keys_ref[:tokens] = normalized(passed_keys, key_gain, (squares, other_squares), 0)
    keys_ref[tokens:blocks] = normalized(far_keys, key_gain, (squares, other_squares), 1)
    for head in range(heads):
        columns = head_columns(head)
        scores_ref[head] = score(query_ref[:, columns], keys_ref[:, columns])
    for head in range(heads):
        columns = head_columns(head)
        scores = scores_ref[head] * TO_LOG2 + bias
        old_peak = old_peaks_ref[head]
        peak = jnp.maximum(old_peak, jnp.max(scores, axis=1, keepdims=True))
        weights = jnp.exp2(scores - peak[:, :1])
        total = jnp.sum(weights, axis=1, keepdims=True)
        weights = weights.astype(jnp.bfloat16)
        fading = jnp.exp2(old_peak - peak)
        inverse = 1.0 / (old_totals_ref[head] * fading + total)
        inverses_ref[head] = inverse
        weights_ref[head] = weights[:, :blocks]
        product = jnp.dot(
            weights[:, blocks:],
            values_ref[:, columns],
            preferred_element_type=jnp.float32,
        )
        partial_ref[:, columns] = (old_partial_ref[:, columns] * fading + product) * inverse


def late_values_kernel(
    inverses_ref, partial_ref, weights_ref, passed_values, far_values, out_ref, out_vmem, sems
):
    heads = weights_ref.shape[0]
    copies = []
    for head in range(heads):
        columns = head_columns(head)
        values = jnp.concatenate([passed_values[:, columns], far_values[:, columns]], axis=0)
        product = jnp.dot(weights_ref[head], values, preferred_element_type=jnp.float32)
        out_vmem[:, columns] = (
            partial_ref[:, columns] + product * inverses_ref[head]
        ).astype(jnp.bfloat16)
        copy = pltpu.make_async_copy(
            out_vmem.at[:, columns], out_ref.at[:, columns], sems.at[head]
        )
        copy.start()
        copies.append(copy)
    for copy in copies:
        copy.wait()


def attend_early(pattern, gains, queries, keys, squares, values):
    tokens, features = queries.shape
    heads = features // HEAD_DIM
    count = 3 * tokens
    return pl.pallas_call(
        early_kernel,
        out_shape=(
            pltpu.VMEM((tokens, features), jnp.bfloat16),
            pltpu.VMEM((heads, tokens, LANES), jnp.float32),
            pltpu.VMEM((heads, tokens, LANES), jnp.float32),
            pltpu.VMEM((tokens, features), jnp.float32),
        ),
        in_specs=[SMEM] + [VMEM] * 13,
        out_specs=(VMEM,) * 4,
        scratch_shapes=[
            pltpu.VMEM((count, features), jnp.bfloat16),
            pltpu.VMEM((heads, tokens, count), jnp.float32),
            pltpu.VMEM((heads, tokens, count), jnp.bfloat16),
        ],
        compiler_params=PARAMS,
        cost_estimate=CHEAP,
        name="attend_early",
    )(pattern, *map(in_vmem, (*gains, queries, *keys, *squares, *values)))


def attend_late_keys(pattern, gain, queries, keys, squares, packed, early):
    tokens, features = queries.shape
    heads = features // HEAD_DIM
    rows = packed[0].shape[0] - tokens
    count = 2 * tokens + rows
    return pl.pallas_call(
        late_keys_kernel,
        out_shape=(
            pltpu.VMEM((heads, tokens, LANES), jnp.float32),
            pltpu.VMEM((tokens, features), jnp.float32),
            pltpu.VMEM((heads, tokens, 2 * tokens), jnp.bfloat16),
        ),
        in_specs=[SMEM] + [VMEM] * 11,
        out_specs=(VMEM,) * 3,
        scratch_shapes=[
            pltpu.VMEM((count, features), jnp.bfloat16),
            pltpu.VMEM((rows, features), jnp.bfloat16),
            pltpu.VMEM((heads, tokens, count), jnp.float32),
        ],
        compiler_params=PARAMS,
        cost_estimate=CHEAP,
        name="attend_late_keys",
    )(pattern, *map(in_vmem, (gain, queries, *keys, *squares, *packed, *early)))


def attend_late_values(inverses, partial, weights, values):
    tokens, features = partial.shape
    heads = features // HEAD_DIM
    return pl.pallas_call(
        late_values_kernel,
        out_shape=jax.ShapeDtypeStruct((tokens, features), jnp.bfloat16),
        in_specs=[VMEM] * 5,
        out_specs=pl.BlockSpec(memory_space=pl.ANY),
        scratch_shapes=[
            pltpu.VMEM((tokens, features), jnp.bfloat16),
            pltpu.SemaphoreType.DMA((heads,)),
        ],
        compiler_params=PARAMS,
        cost_estimate=CHEAP,
        name="attend_late_values",
    )(*map(in_vmem, (inverses, partial, weights, *values)))


def column_rows(rows):
    n = lax.axis_size("frm")
    if n <= 8:
        return [rows] + [fetch(rows, lambda i: i + distance) for distance in range(2, n, 2)]
    distance = n // 2
    while distance > 1:
        rows = jnp.concatenate([rows, fetch(rows, lambda i: i ^ distance)], axis=0)
        distance //= 2
    return [rows]


def shards(
    queries,
    key_rows,
    values,
    query_gain,
    key_gain,
    pattern,
    reference_keys,
    reference_values,
    reference_live,
):
    rows = column_rows(pack_rows(reference_live, reference_keys, reference_values))
    packed_keys = attach_rows(key_rows, rows)

    far1_keys = fetch(key_rows, far_first)
    near_values = fetch(values, beside)
    far1_values = fetch(values, far_first)
    near_packed = fetch(packed_keys, beside)
    far2_keys = fetch(key_rows, far_second)
    far2_values = fetch(values, far_second)
    passed_keys = fetch(far1_keys, beside)
    passed_values = fetch(far1_values, beside)

    own_squares = square_sums(queries, packed_keys, "own_squares")
    far_squares = square_sums(near_packed, far1_keys, "early_squares")
    normed_queries, *early = attend_early(
        pattern,
        (query_gain, key_gain),
        queries,
        (packed_keys, near_packed, far1_keys),
        (*own_squares, *far_squares),
        (values, near_values, far1_values),
    )
    passed_keys = after(passed_keys, early[0])
    late_squares = square_sums(passed_keys, far2_keys, "late_squares")
    inverses, partial, weights = attend_late_keys(
        pattern,
        key_gain,
        normed_queries,
        (passed_keys, far2_keys),
        late_squares,
        (packed_keys, near_packed),
        early,
    )
    return attend_late_values(inverses, partial, weights, (passed_values, far2_values))


def solution(mesh):
    in_specs = (
        P(("grp", "frm"), "tp"),
        P(("grp", "frm"), "tp"),
        P(("grp", "frm"), "tp"),
        P("tp"),
        P("tp"),
        P(("grp", "frm"), None),
        P(("grp", "frm"), "tp"),
        P(("grp", "frm"), "tp"),
        P(("grp", "frm")),
    )
    out_specs = P(("grp", "frm"), "tp")
    return jax.shard_map(shards, mesh=mesh, in_specs=in_specs, out_specs=out_specs, check_vma=False)
```

time: 188 us -> 67.8 us (0.36)
  blocking collectives: 134 us -> 0 us
  starting transfers between devices: 7.92 us -> 35.9 us
  local copies, waits for them, and re-layouts: 28.9 us -> 2.45 us
  waiting for transfers between devices: 0.01 us -> 18.1 us
  Pallas kernels: 0 us -> 10.1 us
  other arithmetic: 7.48 us -> 0 us
  matrix products: 6.85 us -> 0 us
    all_gather x2 -> x0, blocking collectives: 113 us -> none  [the longest x1 82.3 us: shards(): lax.all_gather(reference_keys, 'frm', axis=0, tiled=True)]
    ppermute x4 -> x14, starting transfers between devices: 7.92 us -> 35.9 us  [fetch(): return lax.ppermute(block, axis, [(source_of(i) % n, i) for i in range(n)])]
    unnamed x1 -> x0, blocking collectives: 18.7 us -> none
    ppermute x4 -> x14, waiting for transfers between devices: 0.01 us -> 18.1 us  [fetch(): return lax.ppermute(block, axis, [(source_of(i) % n, i) for i in range(n)])]
    slice x14 -> x0, local copies, waits for them, and re-layouts: 13.6 us -> none  [the longest x8 12 us: shards(): key_value[0]]
    pallas_call x0 -> x8, Pallas kernels: none -> 10.1 us  [the longest x1 4.07 us: attend_late_keys(): pl.pallas_call(late_keys_kernel, out_shape=(pltpu.VMEM((heads, tokens, LA...]
    concatenate x13 -> x0, local copies, waits for them, and re-layouts: 7.12 us -> none  [the longest x6 4.48 us: shards(): jnp.concatenate([key_value[0] for key_value in every_pair], axis=0)]
    dot_general x8 -> x0, matrix products: 6.85 us -> none  [the longest x4 4 us: absorb(): jnp.einsum('thd,nhd->htn', query_part, key_part, preferred_element_type=j...]
  transfers between devices with their start and end apart: 4 -> 14, of which waited for: 0 -> 6; matrix products, arithmetic and copies ran while one was open for 7% -> 0% of each run, Pallas kernels for 0% -> 12%
where the time goes in v2:
time: 67.8 us; the launch traced here: 67.5 us
  starting transfers between devices  35.9 us (53%)
  waiting for transfers between devices  18.1 us (27%)
  Pallas kernels  10.1 us (15%)
  local copies, waits for them, and re-layouts  2.45 us (4%)
  between operations  0.83 us (1%)
    ppermute x14, starting transfers between devices, fetch(): return lax.ppermute(block, axis, [(source_of(i) % n, i) for i in range(n)])  35.9 us
    ppermute x14, waiting for transfers between devices, fetch(): return lax.ppermute(block, axis, [(source_of(i) % n, i) for i in range(n)])  18.1 us
    pallas_call x1, Pallas kernels, attend_late_keys(): pl.pallas_call(late_keys_kernel, out_shape=(pltpu.VMEM((heads, tokens, LA...  4.07 us
    pallas_call x1, Pallas kernels, attend_early(): pl.pallas_call(early_kernel, out_shape=(pltpu.VMEM((tokens, features), jn...  3.38 us
    unnamed x18, local copies, waits for them, and re-layouts  2.45 us
  transfers between devices with their start and end apart: 14, of which 6 were waited for; matrix products, arithmetic and copies ran while one was open for 0% of the time, Pallas kernels for 12%

profile of v2, /device:TPU:0, one launch (start us, length us, event | category | flops | bytes accessed | tf_op | source)
XLA Modules:
  0.0 67.5 jit_solution(1949043206745458482)
XLA Ops:
  0.0 0.0 copy-start
  0.7 0.0 copy-start.5
  0.7 0.7 %copy-done.5 = bf16[4,1280]{1,0:T(4,128)(2,1)S(1)} copy-done((bf16[4,1280]{1,0:T(4,128)(2,1)S(1)}, bf16[4,1280]{1,0:T(4,128)(2,1)}, u32[]{:S(2)}) %copy-start.5) | copy-done | bytes 10264
  1.4 0.0 copy-start.6
  1.4 0.7 %copy-done.6 = bf16[4,1280]{1,0:T(4,128)(2,1)S(1)} copy-done((bf16[4,1280]{1,0:T(4,128)(2,1)S(1)}, bf16[4,1280]{1,0:T(4,128)(2,1)}, u32[]{:S(2)}) %copy-start.6) | copy-done | bytes 10264
  2.1 0.6 pack_rows.1.refs_0_
  2.7 5.1 %collective-permute-start = (bf16[4,2560]{1,0:T(4,128)(2,1)S(1)}, bf16[4,2560]{1,0:T(4,128)(2,1)S(1)}, u32[]{:S(2)}, u32[]{:S(2)}) collective-permute-start(bf16[4,2560]{1,0:T(4,128)(2,1)S(1)} %pack_rows.1.refs_0_), channel_id=1, source_target_pairs={{4,0},{6,2},{8,4},{10,6},{12,8},{14,10},{0,12},{2,14},{5,1},{7,3},... | collective-permute-start | bytes 61448 | tf_op jit(solution)/shard_map/ppermute | solution.py:22
  7.8 0.0 collective-permute-start.1
  7.8 1.0 %collective-permute-start.2 = (bf16[4,2560]{1,0:T(4,128)(2,1)S(1)}, bf16[4,2560]{1,0:T(4,128)(2,1)S(1)}, u32[]{:S(2)}, u32[]{:S(2)}) collective-permute-start(bf16[4,2560]{1,0:T(4,128)(2,1)S(1)} %pack_rows.1.refs_0_), channel_id=1, source_target_pairs={{12,0},{14,2},{0,4},{2,6},{4,8},{6,10},{8,12},{10,14},{13,1},{15,3... | collective-permute-start | bytes 61448 | tf_op jit(solution)/shard_map/ppermute | solution.py:22
  8.8 2.8 %collective-permute-start.4 = (bf16[192,1280]{1,0:T(8,128)(2,1)}, bf16[192,1280]{1,0:T(8,128)(2,1)S(1)}, u32[]{:S(2)}, u32[]{:S(2)}) collective-permute-start(bf16[192,1280]{1,0:T(8,128)(2,1)} %keys_ref.3), channel_id=1, source_target_pairs={{4,0},{14,2},{8,4},{2,6},{12,8},{6,10},{0,12},{10,14},{5,1},{15,3}... | collective-permute-start | bytes 1474568 | tf_op jit(solution)/shard_map/ppermute | solution.py:22
  11.6 0.0 collective-permute-done.refs_1_
  11.6 0.9 %collective-permute-done.1.refs_2_ = bf16[4,2560]{1,0:T(4,128)(2,1)S(1)} collective-permute-done((bf16[4,2560]{1,0:T(4,128)(2,1)S(1)}, bf16[4,2560]{1,0:T(4,128)(2,1)S(1)}, u32[]{:S(2)}, u32[]{:S(2)}) %collective-permute-start.1) | collective-permute-done | bytes 20512 | tf_op jit(solution)/shard_map/ppermute | solution.py:22
  12.5 1.1 %collective-permute-done.2.refs_3_ = bf16[4,2560]{1,0:T(4,128)(2,1)S(1)} collective-permute-done((bf16[4,2560]{1,0:T(4,128)(2,1)S(1)}, bf16[4,2560]{1,0:T(4,128)(2,1)S(1)}, u32[]{:S(2)}, u32[]{:S(2)}) %collective-permute-start.2) | collective-permute-done | bytes 20512 | tf_op jit(solution)/shard_map/ppermute | solution.py:22
  13.6 0.0 copy-start.1
  13.6 1.0 %copy-done.1 = bf16[192,1280]{1,0:T(8,128)(2,1)S(1)} copy-done((bf16[192,1280]{1,0:T(8,128)(2,1)S(1)}, bf16[192,1280]{1,0:T(8,128)(2,1)}, u32[]{:S(2)}) %copy-start.1) | copy-done | bytes 491544
  14.6 0.0 copy-start.2
  14.6 0.0 copy-start.3
  14.6 0.0 copy-start.4
  14.6 0.0 copy-start.7
  14.6 0.0 copy-start.8
  14.6 0.1 attach_rows.1.second_ref.own_keys.own_packed
  14.7 1.6 %collective-permute-start.3 = (bf16[224,1280]{1,0:T(8,128)(2,1)S(1)}, bf16[224,1280]{1,0:T(8,128)(2,1)S(1)}, u32[]{:S(2)}, u32[]{:S(2)}) collective-permute-start(bf16[224,1280]{1,0:T(8,128)(2,1)S(1)} %attach_rows.1.second_ref.own_keys.own_packed), channel_id=1, source_target_pairs={{2,0},{0,2},{6,4},{4,6},{10,8},{8,10},{14,12},{12,14},{3,1},{1,3},... | collective-permute-start | bytes 1720328 | tf_op jit(solution)/shard_map/ppermute | solution.py:22
  16.3 0.5 collective-permute-start.8
  16.8 0.0 collective-permute-start.7
  16.8 0.0 copy-done
  16.8 0.3 own_squares.1
  17.1 0.1 collective-permute-start.5
  17.2 6.7 %collective-permute-done.4.second_ref.far_keys = bf16[192,1280]{1,0:T(8,128)(2,1)S(1)} collective-permute-done((bf16[192,1280]{1,0:T(8,128)(2,1)}, bf16[192,1280]{1,0:T(8,128)(2,1)S(1)}, u32[]{:S(2)}, u32[]{:S(2)}) %collective-permute-start.4) | collective-permute-done | bytes 491552 | tf_op jit(solution)/shard_map/ppermute | solution.py:22
  23.9 2.8 %collective-permute-start.9 = (bf16[192,1280]{1,0:T(8,128)(2,1)S(1)}, bf16[192,1280]{1,0:T(8,128)(2,1)S(1)}, u32[]{:S(2)}, u32[]{:S(2)}) collective-permute-start(bf16[192,1280]{1,0:T(8,128)(2,1)S(1)} %collective-permute-done.4.second_ref.far_keys), channel_id=1, source_target_pairs={{2,0},{0,2},{6,4},{4,6},{10,8},{8,10},{14,12},{12,14},{3,1},{1,3},... | collective-permute-start | bytes 1474568 | tf_op jit(solution)/shard_map/ppermute | solution.py:22
  26.6 0.0 collective-permute-done.5.other_own_squares
  26.6 0.0 copy-done.2
  26.6 0.5 collective-permute-start.10
  27.2 7.0 %collective-permute-done.8.far_values = bf16[192,1280]{1,0:T(8,128)(2,1)S(1)} collective-permute-done((bf16[192,1280]{1,0:T(8,128)(2,1)}, bf16[192,1280]{1,0:T(8,128)(2,1)S(1)}, u32[]{:S(2)}, u32[]{:S(2)}) %collective-permute-start.8) | collective-permute-done | bytes 491552 | tf_op jit(solution)/shard_map/ppermute | solution.py:22
  34.2 0.0 copy-done.3
  34.2 21.2 %collective-permute-start.13 = (bf16[192,1280]{1,0:T(8,128)(2,1)S(1)}, bf16[192,1280]{1,0:T(8,128)(2,1)S(1)}, u32[]{:S(2)}, u32[]{:S(2)}) collective-permute-start(bf16[192,1280]{1,0:T(8,128)(2,1)S(1)} %copy-done.3), channel_id=1, source_target_pairs={{12,0},{6,2},{0,4},{10,6},{4,8},{14,10},{8,12},{2,14},{13,1},{7,3}... | collective-permute-start | bytes 1474568 | tf_op jit(solution)/shard_map/ppermute | solution.py:22
  55.5 0.0 collective-permute-done.3.first_ref.near_keys.near_packed
  55.5 0.0 collective-permute-start.12
  55.5 0.3 early_squares.1.far_squares
  55.7 0.0 collective-permute-done.7.near_values
  55.7 0.1 collective-permute-start.6
  55.8 1.3 %collective-permute-done.6.other_far_squares = f32[192,128]{1,0:T(8,128)S(1)} collective-permute-done((f32[192,128]{1,0:T(8,128)S(1)}, f32[192,128]{1,0:T(8,128)S(1)}, u32[]{:S(2)}, u32[]{:S(2)}) %collective-permute-start.6) | collective-permute-done | bytes 98336 | tf_op jit(solution)/shard_map/ppermute | solution.py:22
  57.1 0.0 copy-done.4
  57.1 0.0 copy-done.7
  57.1 0.0 copy-done.8
  57.1 3.4 %attend_early.1 = (bf16[192,1280]{1,0:T(8,128)(2,1)S(1)}, f32[10,192,128]{2,1,0:T(8,128)S(1)}, f32[10,192,128]{2,1,0:T(8,128)S(1)}, f32[192,1280]{1,0:T(8,128)S(1)}) custom-call(s32[1,4]{1,0:T(1,128)S(1)} %copy-done.8, f32[1280]{0:T(1024)S(1)} %copy-done.7, f32[1280]{0:T(1024)S(1)} %copy-done.4, bf16[192,1280]{1,0:T(8,128)(2,1)S(1)} %copy-done, ...), custom_call_target="tpu_custom_call" | custom-call | flops 1 | bytes 1 | tf_op jit(solution)/shard_map/attend_early/pallas_call | solution.py:304
  60.5 0.0 collective-permute-done.9.first_ref.passed_keys
  60.5 0.0 collective-permute-done.10.second_ref.far_keys
  60.5 0.3 late_squares.1.squares
  60.8 0.2 collective-permute-start.11
  61.0 1.2 %collective-permute-done.11.other_squares = f32[192,128]{1,0:T(8,128)S(1)} collective-permute-done((f32[192,128]{1,0:T(8,128)S(1)}, f32[192,128]{1,0:T(8,128)S(1)}, u32[]{:S(2)}, u32[]{:S(2)}) %collective-permute-start.11) | collective-permute-done | bytes 98336 | tf_op jit(solution)/shard_map/ppermute | solution.py:22
  62.1 4.1 %attend_late_keys.1 = (f32[10,192,128]{2,1,0:T(8,128)S(1)}, f32[192,1280]{1,0:T(8,128)S(1)}, bf16[10,192,384]{2,1,0:T(8,128)(2,1)S(1)}) custom-call(s32[1,4]{1,0:T(1,128)S(1)} %copy-done.8, f32[1280]{0:T(1024)S(1)} %copy-done.4, bf16[192,1280]{1,0:T(8,128)(2,1)S(1)} %get-tuple-element.13.query_ref, ...), custom_call_target="tpu_custom_call" | custom-call | flops 1 | bytes 1 | tf_op jit(solution)/shard_map/attend_late_keys/pallas_call | solution.py:330
  66.2 0.0 collective-permute-done.13.far_values
  66.2 0.0 collective-permute-done.12.passed_values
  66.2 1.3 %attend_late_values.1 = bf16[192,1280]{1,0:T(8,128)(2,1)} custom-call(f32[10,192,128]{2,1,0:T(8,128)S(1)} %get-tuple-element.18.inverses_ref, f32[192,1280]{1,0:T(8,128)S(1)} %get-tuple-element.19.partial_ref, bf16[10,192,384]{2,1,0:T(8,128)(2,1)S(1)} %get-tuple-element.20.weights_ref, bf16[192,1280]{1,0:T(8,128)(2,1)S(1)} %collective-permute-done.12.passed_values, ...), custom_call_target="tpu_custom_call" | custom-call | flops 1 | bytes 1 | tf_op jit(solution)/shard_map/attend_late_values/pallas_call | solution.py:353
Async XLA Ops:
  0.0 16.8 %copy-start = (bf16[192,1280]{1,0:T(8,128)(2,1)S(1)}, bf16[192,1280]{1,0:T(8,128)(2,1)}, u32[]{:S(2)}) copy-start(bf16[192,1280]{1,0:T(8,128)(2,1)} %queries.1) | copy-start | bytes 1474564
  0.7 0.7 %copy-start.5 = (bf16[4,1280]{1,0:T(4,128)(2,1)S(1)}, bf16[4,1280]{1,0:T(4,128)(2,1)}, u32[]{:S(2)}) copy-start(bf16[4,1280]{1,0:T(4,128)(2,1)} %keys_ref.2) | copy-start | bytes 30724
  1.4 0.7 %copy-start.6 = (bf16[4,1280]{1,0:T(4,128)(2,1)S(1)}, bf16[4,1280]{1,0:T(4,128)(2,1)}, u32[]{:S(2)}) copy-start(bf16[4,1280]{1,0:T(4,128)(2,1)} %values_ref.1) | copy-start | bytes 30724
  2.7 8.9 %collective-permute-start = (bf16[4,2560]{1,0:T(4,128)(2,1)S(1)}, bf16[4,2560]{1,0:T(4,128)(2,1)S(1)}, u32[]{:S(2)}, u32[]{:S(2)}) collective-permute-start(bf16[4,2560]{1,0:T(4,128)(2,1)S(1)} %pack_rows.1.refs_0_), channel_id=1, source_target_pairs={{4,0},{6,2},{8,4},{10,6},{12,8},{14,10},{0,12},{2,14},{5,1},{7,3},... | collective-permute-start | bytes 61448 | tf_op jit(solution)/shard_map/ppermute | solution.py:22
  7.8 4.7 %collective-permute-start.1 = (bf16[4,2560]{1,0:T(4,128)(2,1)S(1)}, bf16[4,2560]{1,0:T(4,128)(2,1)S(1)}, u32[]{:S(2)}, u32[]{:S(2)}) collective-permute-start(bf16[4,2560]{1,0:T(4,128)(2,1)S(1)} %pack_rows.1.refs_0_), channel_id=1, source_target_pairs={{8,0},{10,2},{12,4},{14,6},{0,8},{2,10},{4,12},{6,14},{9,1},{11,3}... | collective-permute-start | bytes 61448 | tf_op jit(solution)/shard_map/ppermute | solution.py:22
  7.8 5.8 %collective-permute-start.2 = (bf16[4,2560]{1,0:T(4,128)(2,1)S(1)}, bf16[4,2560]{1,0:T(4,128)(2,1)S(1)}, u32[]{:S(2)}, u32[]{:S(2)}) collective-permute-start(bf16[4,2560]{1,0:T(4,128)(2,1)S(1)} %pack_rows.1.refs_0_), channel_id=1, source_target_pairs={{12,0},{14,2},{0,4},{2,6},{4,8},{6,10},{8,12},{10,14},{13,1},{15,3... | collective-permute-start | bytes 61448 | tf_op jit(solution)/shard_map/ppermute | solution.py:22
  8.8 15.0 %collective-permute-start.4 = (bf16[192,1280]{1,0:T(8,128)(2,1)}, bf16[192,1280]{1,0:T(8,128)(2,1)S(1)}, u32[]{:S(2)}, u32[]{:S(2)}) collective-permute-start(bf16[192,1280]{1,0:T(8,128)(2,1)} %keys_ref.3), channel_id=1, source_target_pairs={{4,0},{14,2},{8,4},{2,6},{12,8},{6,10},{0,12},{10,14},{5,1},{15,3}... | collective-permute-start | bytes 1474568 | tf_op jit(solution)/shard_map/ppermute | solution.py:22
  13.6 1.0 %copy-start.1 = (bf16[192,1280]{1,0:T(8,128)(2,1)S(1)}, bf16[192,1280]{1,0:T(8,128)(2,1)}, u32[]{:S(2)}) copy-start(bf16[192,1280]{1,0:T(8,128)(2,1)} %keys_ref.3) | copy-start | bytes 1474564
  14.6 12.0 %copy-start.2 = (bf16[192,1280]{1,0:T(8,128)(2,1)S(1)}, bf16[192,1280]{1,0:T(8,128)(2,1)}, u32[]{:S(2)}) copy-start(bf16[192,1280]{1,0:T(8,128)(2,1)} %keys_ref.3) | copy-start | bytes 1474564
  14.6 19.6 %copy-start.3 = (bf16[192,1280]{1,0:T(8,128)(2,1)S(1)}, bf16[192,1280]{1,0:T(8,128)(2,1)}, u32[]{:S(2)}) copy-start(bf16[192,1280]{1,0:T(8,128)(2,1)} %own_values.1) | copy-start | bytes 1474564
  14.6 42.5 %copy-start.4 = (f32[1280]{0:T(1024)S(1)}, f32[1280]{0:T(1024)}, u32[]{:S(2)}) copy-start(f32[1280]{0:T(1024)} %key_gain.3) | copy-start | bytes 15364
  14.6 42.5 %copy-start.7 = (f32[1280]{0:T(1024)S(1)}, f32[1280]{0:T(1024)}, u32[]{:S(2)}) copy-start(f32[1280]{0:T(1024)} %query_gain.1) | copy-start | bytes 15364
  14.6 42.5 %copy-start.8 = (s32[1,4]{1,0:T(1,128)S(1)}, s32[1,4]{1,0:T(1,128)}, u32[]{:S(2)}) copy-start(s32[1,4]{1,0:T(1,128)} %pattern_ref.3) | copy-start | bytes 52
  14.7 40.7 %collective-permute-start.3 = (bf16[224,1280]{1,0:T(8,128)(2,1)S(1)}, bf16[224,1280]{1,0:T(8,128)(2,1)S(1)}, u32[]{:S(2)}, u32[]{:S(2)}) collective-permute-start(bf16[224,1280]{1,0:T(8,128)(2,1)S(1)} %attach_rows.1.second_ref.own_keys.own_packed), channel_id=1, source_target_pairs={{2,0},{0,2},{6,4},{4,6},{10,8},{8,10},{14,12},{12,14},{3,1},{1,3},... | collective-permute-start | bytes 1720328 | tf_op jit(solution)/shard_map/ppermute | solution.py:22
  16.3 17.9 %collective-permute-start.8 = (bf16[192,1280]{1,0:T(8,128)(2,1)}, bf16[192,1280]{1,0:T(8,128)(2,1)S(1)}, u32[]{:S(2)}, u32[]{:S(2)}) collective-permute-start(bf16[192,1280]{1,0:T(8,128)(2,1)} %own_values.1), channel_id=1, source_target_pairs={{4,0},{14,2},{8,4},{2,6},{12,8},{6,10},{0,12},{10,14},{5,1},{15,3}... | collective-permute-start | bytes 1474568 | tf_op jit(solution)/shard_map/ppermute | solution.py:22
  16.8 38.9 %collective-permute-start.7 = (bf16[192,1280]{1,0:T(8,128)(2,1)}, bf16[192,1280]{1,0:T(8,128)(2,1)S(1)}, u32[]{:S(2)}, u32[]{:S(2)}) collective-permute-start(bf16[192,1280]{1,0:T(8,128)(2,1)} %own_values.1), channel_id=1, source_target_pairs={{2,0},{0,2},{6,4},{4,6},{10,8},{8,10},{14,12},{12,14},{3,1},{1,3},... | collective-permute-start | bytes 1474568 | tf_op jit(solution)/shard_map/ppermute | solution.py:22
  17.1 9.5 %collective-permute-start.5 = (f32[192,128]{1,0:T(8,128)S(1)}, f32[192,128]{1,0:T(8,128)S(1)}, u32[]{:S(2)}, u32[]{:S(2)}) collective-permute-start(f32[192,128]{1,0:T(8,128)S(1)} %own_squares.1), channel_id=1, source_target_pairs={{1,0},{0,1},{3,2},{2,3},{5,4},{4,5},{7,6},{6,7},{9,8},{8,9},{11,10... | collective-permute-start | bytes 294920 | tf_op jit(solution)/shard_map/ppermute | solution.py:22
  23.9 36.6 %collective-permute-start.9 = (bf16[192,1280]{1,0:T(8,128)(2,1)S(1)}, bf16[192,1280]{1,0:T(8,128)(2,1)S(1)}, u32[]{:S(2)}, u32[]{:S(2)}) collective-permute-start(bf16[192,1280]{1,0:T(8,128)(2,1)S(1)} %collective-permute-done.4.second_ref.far_keys), channel_id=1, source_target_pairs={{2,0},{0,2},{6,4},{4,6},{10,8},{8,10},{14,12},{12,14},{3,1},{1,3},... | collective-permute-start | bytes 1474568 | tf_op jit(solution)/shard_map/ppermute | solution.py:22
  26.6 33.9 %collective-permute-start.10 = (bf16[192,1280]{1,0:T(8,128)(2,1)S(1)}, bf16[192,1280]{1,0:T(8,128)(2,1)S(1)}, u32[]{:S(2)}, u32[]{:S(2)}) collective-permute-start(bf16[192,1280]{1,0:T(8,128)(2,1)S(1)} %copy-done.2), channel_id=1, source_target_pairs={{12,0},{6,2},{0,4},{10,6},{4,8},{14,10},{8,12},{2,14},{13,1},{7,3}... | collective-permute-start | bytes 1474568 | tf_op jit(solution)/shard_map/ppermute | solution.py:22
  34.2 32.0 %collective-permute-start.13 = (bf16[192,1280]{1,0:T(8,128)(2,1)S(1)}, bf16[192,1280]{1,0:T(8,128)(2,1)S(1)}, u32[]{:S(2)}, u32[]{:S(2)}) collective-permute-start(bf16[192,1280]{1,0:T(8,128)(2,1)S(1)} %copy-done.3), channel_id=1, source_target_pairs={{12,0},{6,2},{0,4},{10,6},{4,8},{14,10},{8,12},{2,14},{13,1},{7,3}... | collective-permute-start | bytes 1474568 | tf_op jit(solution)/shard_map/ppermute | solution.py:22
  55.5 10.8 %collective-permute-start.12 = (bf16[192,1280]{1,0:T(8,128)(2,1)S(1)}, bf16[192,1280]{1,0:T(8,128)(2,1)S(1)}, u32[]{:S(2)}, u32[]{:S(2)}) collective-permute-start(bf16[192,1280]{1,0:T(8,128)(2,1)S(1)} %collective-permute-done.8.far_values), channel_id=1, source_target_pairs={{2,0},{0,2},{6,4},{4,6},{10,8},{8,10},{14,12},{12,14},{3,1},{1,3},... | collective-permute-start | bytes 1474568 | tf_op jit(solution)/shard_map/ppermute | solution.py:22
  55.7 1.4 %collective-permute-start.6 = (f32[192,128]{1,0:T(8,128)S(1)}, f32[192,128]{1,0:T(8,128)S(1)}, u32[]{:S(2)}, u32[]{:S(2)}) collective-permute-start(f32[192,128]{1,0:T(8,128)S(1)} %early_squares.1.far_squares), channel_id=1, source_target_pairs={{1,0},{0,1},{3,2},{2,3},{5,4},{4,5},{7,6},{6,7},{9,8},{8,9},{11,10... | collective-permute-start | bytes 294920 | tf_op jit(solution)/shard_map/ppermute | solution.py:22
  60.8 1.4 %collective-permute-start.11 = (f32[192,128]{1,0:T(8,128)S(1)}, f32[192,128]{1,0:T(8,128)S(1)}, u32[]{:S(2)}, u32[]{:S(2)}) collective-permute-start(f32[192,128]{1,0:T(8,128)S(1)} %late_squares.1.squares), channel_id=1, source_target_pairs={{1,0},{0,1},{3,2},{2,3},{5,4},{4,5},{7,6},{6,7},{9,8},{8,9},{11,10... | collective-permute-start | bytes 294920 | tf_op jit(solution)/shard_map/ppermute | solution.py:22

commit v3 on v2

--- a/solution.py
+++ b/solution.py
@@ -40,6 +40,10 @@
 
 def in_vmem(array):
     return pltpu.with_memory_space_constraint(array, pltpu.VMEM)
+
+
+def in_hbm(array):
+    return pltpu.with_memory_space_constraint(array, pltpu.HBM)
 
 
 VMEM = pl.BlockSpec(memory_space=pltpu.VMEM)
@@ -81,20 +85,70 @@
     return pl.pallas_call(
         pack_kernel,
         out_shape=pltpu.VMEM((slots, 2 * features), jnp.bfloat16),
-        in_specs=[pl.BlockSpec(memory_space=pl.ANY)] * 3,
+        in_specs=[pl.BlockSpec(memory_space=pltpu.HBM)] * 3,
         out_specs=VMEM,
         scratch_shapes=[pltpu.SMEM((1,), jnp.int32), pltpu.SemaphoreType.DMA((3,))],
         compiler_params=PARAMS,
         cost_estimate=CHEAP,
         name="pack_rows",
-    )(live, keys, values)
-
-
-def attach_kernel(keys_ref, *refs):
+    )(live, in_hbm(keys), in_hbm(values))
+
+
+def squares_kernel(*refs):
+    *row_refs, squares_ref = refs
+    lane = lax.broadcasted_iota(jnp.int32, squares_ref.shape, 1)
+    squares = jnp.zeros(squares_ref.shape, jnp.float32)
+    for column, ref in enumerate(row_refs):
+        rows = ref[...].astype(jnp.float32)
+        squares = jnp.where(lane == column, jnp.sum(rows * rows, axis=1, keepdims=True), squares)
+    squares_ref[...] = squares
+
+
+def square_sums(name, blocks, earlier=()):
+    squares = pl.pallas_call(
+        squares_kernel,
+        out_shape=pltpu.VMEM((blocks[0].shape[0], LANES), jnp.float32),
+        in_specs=[VMEM] * len(blocks),
+        out_specs=VMEM,
+        compiler_params=PARAMS,
+        cost_estimate=CHEAP,
+        name=name,
+    )(*map(in_vmem, blocks))
+    squares = after(squares, *earlier)
+    return squares, fetch(squares, lambda i: i ^ 1, "tp")
+
+
+def normalized(rows_ref, gain_ref, squares_refs, column):
+    square_sum = sum(ref[:, column : column + 1] for ref in squares_refs)
+    scale = lax.rsqrt(square_sum / (HEADS * HEAD_DIM) + EPSILON)
+    rows = rows_ref[...].astype(jnp.float32)
+    return (rows * scale * gain_ref[...][None, :]).astype(jnp.bfloat16)
+
+
+def prepare_kernel(
+    queries, keys, query_gain, key_gain, squares, other_squares, query_ref, key_ref
+):
+    query_ref[...] = normalized(queries, query_gain, (squares, other_squares), 0)
+    key_ref[...] = normalized(keys, key_gain, (squares, other_squares), 1)
+
+
+def prepare(queries, keys, gains, squares):
+    return pl.pallas_call(
+        prepare_kernel,
+        out_shape=(pltpu.VMEM(keys.shape, jnp.bfloat16),) * 2,
+        in_specs=[VMEM] * 6,
+        out_specs=(VMEM,) * 2,
+        compiler_params=PARAMS,
+        cost_estimate=CHEAP,
+        name="prepare",
+    )(*map(in_vmem, (queries, keys, *gains, *squares)))
+
+
+def prepare_far_kernel(keys, gain, squares, other_squares, *refs):
     *row_refs, packed_ref = refs
-    tokens, features = keys_ref.shape
-    packed_ref[:tokens] = keys_ref[...]
-    count = sum(ref.shape[0] for ref in row_refs)
+    tokens, features = keys.shape
+    count = (packed_ref.shape[0] - tokens) // 2
+    packed_ref[:tokens] = normalized(keys, gain, (squares, other_squares), 0)
     first = tokens
     for ref in row_refs:
         slots = ref.shape[0]
@@ -103,47 +157,18 @@
         first += slots
 
 
-def attach_rows(keys, rows):
+def prepare_far(keys, gain, squares, rows):
     tokens, features = keys.shape
     count = sum(part.shape[0] for part in rows)
     return pl.pallas_call(
-        attach_kernel,
+        prepare_far_kernel,
         out_shape=pltpu.VMEM((tokens + 2 * count, features), jnp.bfloat16),
-        in_specs=[VMEM] * (1 + len(rows)),
+        in_specs=[VMEM] * (4 + len(rows)),
         out_specs=VMEM,
         compiler_params=PARAMS,
         cost_estimate=CHEAP,
-        name="attach_rows",
-    )(*map(in_vmem, (keys, *rows)))
-
-
-def squares_kernel(first_ref, second_ref, squares_ref):
-    def square_sum(ref):
-        rows = ref[: squares_ref.shape[0]].astype(jnp.float32)
-        return jnp.sum(rows * rows, axis=1, keepdims=True)
-
-    lane = lax.broadcasted_iota(jnp.int32, squares_ref.shape, 1)
-    squares_ref[...] = jnp.where(lane == 0, square_sum(first_ref), square_sum(second_ref))
-
-
-def square_sums(first, second, name):
-    squares = pl.pallas_call(
-        squares_kernel,
-        out_shape=pltpu.VMEM((min(first.shape[0], second.shape[0]), LANES), jnp.float32),
-        in_specs=[VMEM, VMEM],
-        out_specs=VMEM,
-        compiler_params=PARAMS,
-        cost_estimate=CHEAP,
-        name=name,
-    )(in_vmem(first), in_vmem(second))
-    return squares, fetch(squares, lambda i: i ^ 1, "tp")
-
-
-def normalized(rows_ref, gain_ref, squares_refs, column):
-    square_sum = sum(ref[:, column : column + 1] for ref in squares_refs)
-    scale = lax.rsqrt(square_sum / (HEADS * HEAD_DIM) + EPSILON)
-    rows = rows_ref[: square_sum.shape[0]].astype(jnp.float32)
-    return (rows * scale * gain_ref[...][None, :]).astype(jnp.bfloat16)
+        name="prepare_far",
+    )(*map(in_vmem, (keys, gain, *squares, *rows)))
 
 
 def pattern_flag(pattern_ref, column):
@@ -155,26 +180,23 @@
     return jnp.where(flag, jnp.zeros((1, tokens), jnp.float32), -jnp.inf)
 
 
+def softmax_parts(scores_ref, head, bias):
+    scores = scores_ref[head] * TO_LOG2 + bias
+    return scores, jnp.max(scores, axis=1, keepdims=True)
+
+
 def early_kernel(
     pattern_ref,
-    query_gain,
-    key_gain,
-    queries,
+    query_ref,
     own_keys,
     near_keys,
-    far_keys,
-    own_squares,
-    other_own_squares,
-    far_squares,
-    other_far_squares,
+    far_packed,
     own_values,
     near_values,
     far_values,
-    query_ref,
     peaks_ref,
     totals_ref,
     partial_ref,
-    keys_ref,
     scores_ref,
     weights_ref,
 ):
@@ -188,17 +210,12 @@
         ],
         axis=1,
     )
-    own, far = (own_squares, other_own_squares), (far_squares, other_far_squares)
-    query_ref[...] = normalized(queries, query_gain, own, 0)
-    keys_ref[:tokens] = normalized(own_keys, key_gain, own, 1)
-    keys_ref[tokens : 2 * tokens] = normalized(near_keys, key_gain, far, 0)
-    keys_ref[2 * tokens :] = normalized(far_keys, key_gain, far, 1)
     for head in range(heads):
         columns = head_columns(head)
-        scores_ref[head] = score(query_ref[:, columns], keys_ref[:, columns])
-    for head in range(heads):
-        scores = scores_ref[head] * TO_LOG2 + bias
-        peak = jnp.max(scores, axis=1, keepdims=True)
+        keys = [own_keys[:, columns], near_keys[:, columns], far_packed[:tokens, columns]]
+        scores_ref[head] = score(query_ref[:, columns], jnp.concatenate(keys, axis=0))
+    for head in range(heads):
+        scores, peak = softmax_parts(scores_ref, head, bias)
         weights = jnp.exp2(scores - peak)
         total = jnp.sum(weights, axis=1, keepdims=True)
         weights_ref[head] = weights.astype(jnp.bfloat16)
@@ -216,14 +233,10 @@
 
 def late_keys_kernel(
     pattern_ref,
-    key_gain,
     query_ref,
-    passed_keys,
+    own_packed,
+    passed_packed,
     far_keys,
-    squares,
-    other_squares,
-    own_packed,
-    near_packed,
     old_peaks_ref,
     old_totals_ref,
     old_partial_ref,
@@ -238,7 +251,9 @@
     heads = features // HEAD_DIM
     blocks = 2 * tokens
     count = values_ref.shape[0] // 2
-    for place, packed in enumerate((own_packed, near_packed)):
+    keys_ref[:tokens] = passed_packed[:tokens]
+    keys_ref[tokens:blocks] = far_keys[...]
+    for place, packed in enumerate((own_packed, passed_packed)):
         first = place * count
         keys_ref[blocks + first : blocks + first + count] = packed[tokens : tokens + count]
         values_ref[first : first + count] = packed[tokens + count :]
@@ -251,27 +266,23 @@
         ],
         axis=1,
     )
-    keys_ref[:tokens] = normalized(passed_keys, key_gain, (squares, other_squares), 0)
-    keys_ref[tokens:blocks] = normalized(far_keys, key_gain, (squares, other_squares), 1)
     for head in range(heads):
         columns = head_columns(head)
         scores_ref[head] = score(query_ref[:, columns], keys_ref[:, columns])
     for head in range(heads):
         columns = head_columns(head)
-        scores = scores_ref[head] * TO_LOG2 + bias
+        scores, peak = softmax_parts(scores_ref, head, bias)
         old_peak = old_peaks_ref[head]
-        peak = jnp.maximum(old_peak, jnp.max(scores, axis=1, keepdims=True))
+        peak = jnp.maximum(old_peak, peak)
         weights = jnp.exp2(scores - peak[:, :1])
+        fading = jnp.exp2(old_peak - peak)
         total = jnp.sum(weights, axis=1, keepdims=True)
-        weights = weights.astype(jnp.bfloat16)
-        fading = jnp.exp2(old_peak - peak)
         inverse = 1.0 / (old_totals_ref[head] * fading + total)
         inverses_ref[head] = inverse
+        weights = weights.astype(jnp.bfloat16)
         weights_ref[head] = weights[:, :blocks]
         product = jnp.dot(
-            weights[:, blocks:],
-            values_ref[:, columns],
-            preferred_element_type=jnp.float32,
+            weights[:, blocks:], values_ref[:, columns], preferred_element_type=jnp.float32
         )
         partial_ref[:, columns] = (old_partial_ref[:, columns] * fading + product) * inverse
 
@@ -297,35 +308,33 @@
         copy.wait()
 
 
-def attend_early(pattern, gains, queries, keys, squares, values):
+def attend_early(pattern, queries, keys, values):
     tokens, features = queries.shape
     heads = features // HEAD_DIM
     count = 3 * tokens
     return pl.pallas_call(
         early_kernel,
         out_shape=(
-            pltpu.VMEM((tokens, features), jnp.bfloat16),
             pltpu.VMEM((heads, tokens, LANES), jnp.float32),
             pltpu.VMEM((heads, tokens, LANES), jnp.float32),
             pltpu.VMEM((tokens, features), jnp.float32),
         ),
-        in_specs=[SMEM] + [VMEM] * 13,
-        out_specs=(VMEM,) * 4,
+        in_specs=[SMEM] + [VMEM] * 7,
+        out_specs=(VMEM,) * 3,
         scratch_shapes=[
-            pltpu.VMEM((count, features), jnp.bfloat16),
             pltpu.VMEM((heads, tokens, count), jnp.float32),
             pltpu.VMEM((heads, tokens, count), jnp.bfloat16),
         ],
         compiler_params=PARAMS,
         cost_estimate=CHEAP,
         name="attend_early",
-    )(pattern, *map(in_vmem, (*gains, queries, *keys, *squares, *values)))
-
-
-def attend_late_keys(pattern, gain, queries, keys, squares, packed, early):
+    )(pattern, *map(in_vmem, (queries, *keys, *values)))
+
+
+def attend_late_keys(pattern, queries, own_packed, passed_packed, far_keys, state):
     tokens, features = queries.shape
     heads = features // HEAD_DIM
-    rows = packed[0].shape[0] - tokens
+    rows = own_packed.shape[0] - tokens
     count = 2 * tokens + rows
     return pl.pallas_call(
         late_keys_kernel,
@@ -334,7 +343,7 @@
             pltpu.VMEM((tokens, features), jnp.float32),
             pltpu.VMEM((heads, tokens, 2 * tokens), jnp.bfloat16),
         ),
-        in_specs=[SMEM] + [VMEM] * 11,
+        in_specs=[SMEM] + [VMEM] * 7,
         out_specs=(VMEM,) * 3,
         scratch_shapes=[
             pltpu.VMEM((count, features), jnp.bfloat16),
@@ -344,7 +353,7 @@
         compiler_params=PARAMS,
         cost_estimate=CHEAP,
         name="attend_late_keys",
-    )(pattern, *map(in_vmem, (gain, queries, *keys, *squares, *packed, *early)))
+    )(pattern, *map(in_vmem, (queries, own_packed, passed_packed, far_keys, *state)))
 
 
 def attend_late_values(inverses, partial, weights, values):
@@ -387,38 +396,30 @@
     reference_values,
     reference_live,
 ):
-    rows = column_rows(pack_rows(reference_live, reference_keys, reference_values))
-    packed_keys = attach_rows(key_rows, rows)
-
-    far1_keys = fetch(key_rows, far_first)
+    far1_keys = fetch(in_hbm(key_rows), far_first)
     near_values = fetch(values, beside)
+    rows = pack_rows(reference_live, reference_keys, reference_values)
     far1_values = fetch(values, far_first)
-    near_packed = fetch(packed_keys, beside)
-    far2_keys = fetch(key_rows, far_second)
-    far2_values = fetch(values, far_second)
-    passed_keys = fetch(far1_keys, beside)
+    rows = column_rows(rows)
+    own_squares = square_sums("own_squares", (queries, key_rows), rows)
+    normed_queries, normed_keys = prepare(queries, key_rows, (query_gain, key_gain), own_squares)
+    near_keys = fetch(normed_keys, beside)
+    far1_squares = square_sums("far_squares", (far1_keys,), (near_values,))
+    far1_packed = prepare_far(far1_keys, key_gain, far1_squares, rows)
+
+    passed_packed = fetch(after(far1_packed, near_values, near_keys), beside)
+    far2_keys = fetch(after(normed_keys, far1_values), far_second)
+    far2_values = fetch(after(values, far1_values), far_second)
     passed_values = fetch(far1_values, beside)
 
-    own_squares = square_sums(queries, packed_keys, "own_squares")
-    far_squares = square_sums(near_packed, far1_keys, "early_squares")
-    normed_queries, *early = attend_early(
+    state = attend_early(
         pattern,
-        (query_gain, key_gain),
-        queries,
-        (packed_keys, near_packed, far1_keys),
-        (*own_squares, *far_squares),
+        normed_queries,
+        (normed_keys, near_keys, far1_packed),
         (values, near_values, far1_values),
     )
-    passed_keys = after(passed_keys, early[0])
-    late_squares = square_sums(passed_keys, far2_keys, "late_squares")
     inverses, partial, weights = attend_late_keys(
-        pattern,
-        key_gain,
-        normed_queries,
-        (passed_keys, far2_keys),
-        late_squares,
-        (packed_keys, near_packed),
-        early,
+        pattern, normed_queries, far1_packed, passed_packed, far2_keys, state
     )
     return attend_late_values(inverses, partial, weights, (passed_values, far2_values))
 

time: 67.8 us -> 58.2 us (0.86)
  starting transfers between devices: 35.9 us -> 17 us
  waiting for transfers between devices: 18.1 us -> 26.9 us
  local copies, waits for them, and re-layouts: 2.45 us -> 3.46 us
    ppermute x14 -> x13, starting transfers between devices: 35.9 us -> 17 us  [fetch(): return lax.ppermute(block, axis, [(source_of(i) % n, i) for i in range(n)])]
    ppermute x14 -> x13, waiting for transfers between devices: 18.1 us -> 26.9 us  [fetch(): return lax.ppermute(block, axis, [(source_of(i) % n, i) for i in range(n)])]
    unnamed x18 -> x12, local copies, waits for them, and re-layouts: 2.45 us -> 3.46 us
  transfers between devices with their start and end apart: 14 -> 13, of which waited for: 6 -> 7; matrix products, arithmetic and copies ran while one was open for 0% -> 0% of each run, Pallas kernels for 12% -> 13%
where the time goes in v3:
time: 58.2 us; the launch traced here: 57.8 us
  waiting for transfers between devices  26.9 us (46%)
  starting transfers between devices  17 us (29%)
  Pallas kernels  9.73 us (17%)
  local copies, waits for them, and re-layouts  3.46 us (6%)
  between operations  0.73 us (1%)
    ppermute x13, waiting for transfers between devices, fetch(): return lax.ppermute(block, axis, [(source_of(i) % n, i) for i in range(n)])  26.9 us
    ppermute x13, starting transfers between devices, fetch(): return lax.ppermute(block, axis, [(source_of(i) % n, i) for i in range(n)])  17 us
    pallas_call x1, Pallas kernels, attend_late_keys(): pl.pallas_call(late_keys_kernel, out_shape=(pltpu.VMEM((heads, tokens, LA...  3.81 us
    unnamed x12, local copies, waits for them, and re-layouts  3.46 us
    pallas_call x1, Pallas kernels, attend_early(): pl.pallas_call(early_kernel, out_shape=(pltpu.VMEM((heads, tokens, LANES)...  2.93 us
    pallas_call x1, Pallas kernels, attend_late_values(): pl.pallas_call(late_values_kernel, out_shape=jax.ShapeDtypeStruct((tokens...  1.3 us
  transfers between devices with their start and end apart: 13, of which 7 were waited for; matrix products, arithmetic and copies ran while one was open for 0% of the time, Pallas kernels for 13%

profile of v3, /device:TPU:0, one launch (start us, length us, event | category | flops | bytes accessed | tf_op | source)
XLA Modules:
  0.0 57.8 jit_solution(2384770654916238057)
XLA Ops:
  0.7 0.8 %pack_rows.1.refs_0_ = bf16[4,2560]{1,0:T(4,128)(2,1)S(1)} custom-call(s32[1]{0:T(128)S(6)} %copy.10.live_ref, bf16[4,1280]{1,0:T(4,128)(2,1)} %keys_ref.1, bf16[4,1280]{1,0:T(4,128)(2,1)} %values_ref.1), custom_call_target="tpu_custom_call" | custom-call | flops 1 | bytes 1 | tf_op jit(solution)/shard_map/pack_rows/pallas_call | solution.py:85
  1.4 5.1 %collective-permute-start = (bf16[4,2560]{1,0:T(4,128)(2,1)S(1)}, bf16[4,2560]{1,0:T(4,128)(2,1)S(1)}, u32[]{:S(2)}, u32[]{:S(2)}) collective-permute-start(bf16[4,2560]{1,0:T(4,128)(2,1)S(1)} %pack_rows.1.refs_0_), channel_id=1, source_target_pairs={{4,0},{6,2},{8,4},{10,6},{12,8},{14,10},{0,12},{2,14},{5,1},{7,3},... | collective-permute-start | bytes 61448 | tf_op jit(solution)/shard_map/ppermute | solution.py:22
  6.5 0.0 collective-permute-start.1
  6.5 1.0 %collective-permute-start.2 = (bf16[4,2560]{1,0:T(4,128)(2,1)S(1)}, bf16[4,2560]{1,0:T(4,128)(2,1)S(1)}, u32[]{:S(2)}, u32[]{:S(2)}) collective-permute-start(bf16[4,2560]{1,0:T(4,128)(2,1)S(1)} %pack_rows.1.refs_0_), channel_id=1, source_target_pairs={{12,0},{14,2},{0,4},{2,6},{4,8},{6,10},{8,12},{10,14},{13,1},{15,3... | collective-permute-start | bytes 61448 | tf_op jit(solution)/shard_map/ppermute | solution.py:22
  7.5 1.5 %collective-permute-start.5 = (bf16[192,1280]{1,0:T(8,128)(2,1)}, bf16[192,1280]{1,0:T(8,128)(2,1)S(1)}, u32[]{:S(2)}, u32[]{:S(2)}) collective-permute-start(bf16[192,1280]{1,0:T(8,128)(2,1)} %own_values.1), channel_id=1, source_target_pairs={{2,0},{0,2},{6,4},{4,6},{10,8},{8,10},{14,12},{12,14},{3,1},{1,3},... | collective-permute-start | bytes 1474568 | tf_op jit(solution)/shard_map/ppermute | solution.py:22
  9.0 2.8 %collective-permute-start.4 = (bf16[192,1280]{1,0:T(8,128)(2,1)}, bf16[192,1280]{1,0:T(8,128)(2,1)S(1)}, u32[]{:S(2)}, u32[]{:S(2)}) collective-permute-start(bf16[192,1280]{1,0:T(8,128)(2,1)} %keys.1), channel_id=1, source_target_pairs={{4,0},{14,2},{8,4},{2,6},{12,8},{6,10},{0,12},{10,14},{5,1},{15,3}... | collective-permute-start | bytes 1474568 | tf_op jit(solution)/shard_map/ppermute | solution.py:22
  11.8 0.0 copy-start
  11.8 1.0 %copy-done = bf16[192,1280]{1,0:T(8,128)(2,1)S(1)} copy-done((bf16[192,1280]{1,0:T(8,128)(2,1)S(1)}, bf16[192,1280]{1,0:T(8,128)(2,1)}, u32[]{:S(2)}) %copy-start) | copy-done | bytes 491544
  12.9 0.0 copy-start.1
  12.9 1.0 %copy-done.1 = bf16[192,1280]{1,0:T(8,128)(2,1)S(1)} copy-done((bf16[192,1280]{1,0:T(8,128)(2,1)S(1)}, bf16[192,1280]{1,0:T(8,128)(2,1)}, u32[]{:S(2)}) %copy-start.1) | copy-done | bytes 491544
  13.9 0.0 copy-start.2
  13.9 0.0 copy-start.5
  13.9 0.3 own_squares.1.squares
  14.2 0.0 collective-permute-done.refs_1_
  14.2 0.0 collective-permute-done.1.refs_2_
  14.2 0.0 collective-permute-done.2.refs_3_
  14.2 0.1 collective-permute-start.3
  14.3 1.3 %collective-permute-done.3.other_squares = f32[192,128]{1,0:T(8,128)S(1)} collective-permute-done((f32[192,128]{1,0:T(8,128)S(1)}, f32[192,128]{1,0:T(8,128)S(1)}, u32[]{:S(2)}, u32[]{:S(2)}) %collective-permute-start.3) | collective-permute-done | bytes 98336 | tf_op jit(solution)/shard_map/ppermute | solution.py:22
  15.6 0.0 copy-start.3
  15.6 0.7 %copy-done.3 = f32[1280]{0:T(1024)S(1)} copy-done((f32[1280]{0:T(1024)S(1)}, f32[1280]{0:T(1024)}, u32[]{:S(2)}) %copy-start.3) | copy-done | bytes 5144
  16.3 0.0 copy-start.4
  16.3 0.7 %copy-done.4 = f32[1280]{0:T(1024)S(1)} copy-done((f32[1280]{0:T(1024)S(1)}, f32[1280]{0:T(1024)}, u32[]{:S(2)}) %copy-start.4) | copy-done | bytes 5144
  17.0 0.3 prepare.1
  17.3 0.3 collective-permute-start.7
  17.5 0.0 copy-done.2
  17.5 1.3 %collective-permute-start.9 = (bf16[192,1280]{1,0:T(8,128)(2,1)S(1)}, bf16[192,1280]{1,0:T(8,128)(2,1)S(1)}, u32[]{:S(2)}, u32[]{:S(2)}) collective-permute-start(bf16[192,1280]{1,0:T(8,128)(2,1)S(1)} %copy-done.2), channel_id=1, source_target_pairs={{4,0},{14,2},{8,4},{2,6},{12,8},{6,10},{0,12},{10,14},{5,1},{15,3}... | collective-permute-start | bytes 1474568 | tf_op jit(solution)/shard_map/ppermute | solution.py:22
  18.9 5.0 %collective-permute-done.4.refs_0_.keys = bf16[192,1280]{1,0:T(8,128)(2,1)S(1)} collective-permute-done((bf16[192,1280]{1,0:T(8,128)(2,1)}, bf16[192,1280]{1,0:T(8,128)(2,1)S(1)}, u32[]{:S(2)}, u32[]{:S(2)}) %collective-permute-start.4) | collective-permute-done | bytes 491552 | tf_op jit(solution)/shard_map/ppermute | solution.py:22
  23.8 0.2 far_squares.1.squares
  24.0 0.0 collective-permute-done.5.near_values
  24.0 0.1 collective-permute-start.6
  24.1 1.3 %collective-permute-done.6.other_squares = f32[192,128]{1,0:T(8,128)S(1)} collective-permute-done((f32[192,128]{1,0:T(8,128)S(1)}, f32[192,128]{1,0:T(8,128)S(1)}, u32[]{:S(2)}, u32[]{:S(2)}) %collective-permute-start.6) | collective-permute-done | bytes 98336 | tf_op jit(solution)/shard_map/ppermute | solution.py:22
  25.4 0.2 prepare_far.1.far_packed.own_packed
  25.6 5.0 %collective-permute-done.7.near_keys = bf16[192,1280]{1,0:T(8,128)(2,1)S(1)} collective-permute-done((bf16[192,1280]{1,0:T(8,128)(2,1)S(1)}, bf16[192,1280]{1,0:T(8,128)(2,1)S(1)}, u32[]{:S(2)}, u32[]{:S(2)}) %collective-permute-start.7) | collective-permute-done | bytes 491552 | tf_op jit(solution)/shard_map/ppermute | solution.py:22
  30.6 1.3 %collective-permute-start.8 = (bf16[224,1280]{1,0:T(8,128)(2,1)S(1)}, bf16[224,1280]{1,0:T(8,128)(2,1)S(1)}, u32[]{:S(2)}, u32[]{:S(2)}) collective-permute-start(bf16[224,1280]{1,0:T(8,128)(2,1)S(1)} %prepare_far.1.far_packed.own_packed), channel_id=1, source_target_pairs={{2,0},{0,2},{6,4},{4,6},{10,8},{8,10},{14,12},{12,14},{3,1},{1,3},... | collective-permute-start | bytes 1720328 | tf_op jit(solution)/shard_map/ppermute | solution.py:22
  31.9 0.7 %collective-permute-done.9.far_values = bf16[192,1280]{1,0:T(8,128)(2,1)S(1)} collective-permute-done((bf16[192,1280]{1,0:T(8,128)(2,1)S(1)}, bf16[192,1280]{1,0:T(8,128)(2,1)S(1)}, u32[]{:S(2)}, u32[]{:S(2)}) %collective-permute-start.9) | collective-permute-done | bytes 491552 | tf_op jit(solution)/shard_map/ppermute | solution.py:22
  32.6 1.8 %collective-permute-start.10 = (bf16[192,1280]{1,0:T(8,128)(2,1)S(1)}, bf16[192,1280]{1,0:T(8,128)(2,1)S(1)}, u32[]{:S(2)}, u32[]{:S(2)}) collective-permute-start(bf16[192,1280]{1,0:T(8,128)(2,1)S(1)} %get-tuple-element.23.own_keys), channel_id=1, source_target_pairs={{12,0},{6,2},{0,4},{10,6},{4,8},{14,10},{8,12},{2,14},{13,1},{7,3}... | collective-permute-start | bytes 1474568 | tf_op jit(solution)/shard_map/ppermute | solution.py:22
  34.4 0.3 collective-permute-start.12
  34.7 1.4 %collective-permute-start.11 = (bf16[192,1280]{1,0:T(8,128)(2,1)S(1)}, bf16[192,1280]{1,0:T(8,128)(2,1)S(1)}, u32[]{:S(2)}, u32[]{:S(2)}) collective-permute-start(bf16[192,1280]{1,0:T(8,128)(2,1)S(1)} %collective-permute-done.9.far_values), channel_id=1, source_target_pairs={{2,0},{0,2},{6,4},{4,6},{10,8},{8,10},{14,12},{12,14},{3,1},{1,3},... | collective-permute-start | bytes 1474568 | tf_op jit(solution)/shard_map/ppermute | solution.py:22
  36.1 0.0 copy-done.5
  36.1 2.9 %attend_early.1 = (f32[10,192,128]{2,1,0:T(8,128)S(1)}, f32[10,192,128]{2,1,0:T(8,128)S(1)}, f32[192,1280]{1,0:T(8,128)S(1)}) custom-call(s32[1,4]{1,0:T(1,128)S(1)} %copy-done.5, bf16[192,1280]{1,0:T(8,128)(2,1)S(1)} %get-tuple-element.19.query_ref, bf16[192,1280]{1,0:T(8,128)(2,1)S(1)} %get-tuple-element.23.own_keys, ...), custom_call_target="tpu_custom_call" | custom-call | flops 1 | bytes 1 | tf_op jit(solution)/shard_map/attend_early/pallas_call | solution.py:315
  39.0 9.7 %collective-permute-done.10.far_keys = bf16[192,1280]{1,0:T(8,128)(2,1)S(1)} collective-permute-done((bf16[192,1280]{1,0:T(8,128)(2,1)S(1)}, bf16[192,1280]{1,0:T(8,128)(2,1)S(1)}, u32[]{:S(2)}, u32[]{:S(2)}) %collective-permute-start.10) | collective-permute-done | bytes 491552 | tf_op jit(solution)/shard_map/ppermute | solution.py:22
  48.7 0.0 collective-permute-done.8.passed_packed
  48.7 3.8 %attend_late_keys.1 = (f32[10,192,128]{2,1,0:T(8,128)S(1)}, f32[192,1280]{1,0:T(8,128)S(1)}, bf16[10,192,384]{2,1,0:T(8,128)(2,1)S(1)}) custom-call(s32[1,4]{1,0:T(1,128)S(1)} %copy-done.5, bf16[192,1280]{1,0:T(8,128)(2,1)S(1)} %get-tuple-element.19.query_ref, bf16[224,1280]{1,0:T(8,128)(2,1)S(1)} %prepare_far.1.far_packed.own_packed, ...), custom_call_target="tpu_custom_call" | custom-call | flops 1 | bytes 1 | tf_op jit(solution)/shard_map/attend_late_keys/pallas_call | solution.py:339
  52.6 3.9 %collective-permute-done.12.far_values = bf16[192,1280]{1,0:T(8,128)(2,1)S(1)} collective-permute-done((bf16[192,1280]{1,0:T(8,128)(2,1)S(1)}, bf16[192,1280]{1,0:T(8,128)(2,1)S(1)}, u32[]{:S(2)}, u32[]{:S(2)}) %collective-permute-start.12) | collective-permute-done | bytes 491552 | tf_op jit(solution)/shard_map/ppermute | solution.py:22
  56.5 0.0 collective-permute-done.11.passed_values
  56.5 1.3 %attend_late_values.1 = bf16[192,1280]{1,0:T(8,128)(2,1)} custom-call(f32[10,192,128]{2,1,0:T(8,128)S(1)} %get-tuple-element.27.inverses_ref, f32[192,1280]{1,0:T(8,128)S(1)} %get-tuple-element.28.partial_ref, bf16[10,192,384]{2,1,0:T(8,128)(2,1)S(1)} %get-tuple-element.29.weights_ref, bf16[192,1280]{1,0:T(8,128)(2,1)S(1)} %collective-permute-done.11.passed_values, ...), custom_call_target="tpu_custom_call" | custom-call | flops 1 | bytes 1 | tf_op jit(solution)/shard_map/attend_late_values/pallas_call | solution.py:362
Async XLA Ops:
  1.4 12.8 %collective-permute-start = (bf16[4,2560]{1,0:T(4,128)(2,1)S(1)}, bf16[4,2560]{1,0:T(4,128)(2,1)S(1)}, u32[]{:S(2)}, u32[]{:S(2)}) collective-permute-start(bf16[4,2560]{1,0:T(4,128)(2,1)S(1)} %pack_rows.1.refs_0_), channel_id=1, source_target_pairs={{4,0},{6,2},{8,4},{10,6},{12,8},{14,10},{0,12},{2,14},{5,1},{7,3},... | collective-permute-start | bytes 61448 | tf_op jit(solution)/shard_map/ppermute | solution.py:22
  6.5 7.7 %collective-permute-start.1 = (bf16[4,2560]{1,0:T(4,128)(2,1)S(1)}, bf16[4,2560]{1,0:T(4,128)(2,1)S(1)}, u32[]{:S(2)}, u32[]{:S(2)}) collective-permute-start(bf16[4,2560]{1,0:T(4,128)(2,1)S(1)} %pack_rows.1.refs_0_), channel_id=1, source_target_pairs={{8,0},{10,2},{12,4},{14,6},{0,8},{2,10},{4,12},{6,14},{9,1},{11,3}... | collective-permute-start | bytes 61448 | tf_op jit(solution)/shard_map/ppermute | solution.py:22
  6.5 7.7 %collective-permute-start.2 = (bf16[4,2560]{1,0:T(4,128)(2,1)S(1)}, bf16[4,2560]{1,0:T(4,128)(2,1)S(1)}, u32[]{:S(2)}, u32[]{:S(2)}) collective-permute-start(bf16[4,2560]{1,0:T(4,128)(2,1)S(1)} %pack_rows.1.refs_0_), channel_id=1, source_target_pairs={{12,0},{14,2},{0,4},{2,6},{4,8},{6,10},{8,12},{10,14},{13,1},{15,3... | collective-permute-start | bytes 61448 | tf_op jit(solution)/shard_map/ppermute | solution.py:22
  7.5 16.5 %collective-permute-start.5 = (bf16[192,1280]{1,0:T(8,128)(2,1)}, bf16[192,1280]{1,0:T(8,128)(2,1)S(1)}, u32[]{:S(2)}, u32[]{:S(2)}) collective-permute-start(bf16[192,1280]{1,0:T(8,128)(2,1)} %own_values.1), channel_id=1, source_target_pairs={{2,0},{0,2},{6,4},{4,6},{10,8},{8,10},{14,12},{12,14},{3,1},{1,3},... | collective-permute-start | bytes 1474568 | tf_op jit(solution)/shard_map/ppermute | solution.py:22
  9.0 14.8 %collective-permute-start.4 = (bf16[192,1280]{1,0:T(8,128)(2,1)}, bf16[192,1280]{1,0:T(8,128)(2,1)S(1)}, u32[]{:S(2)}, u32[]{:S(2)}) collective-permute-start(bf16[192,1280]{1,0:T(8,128)(2,1)} %keys.1), channel_id=1, source_target_pairs={{4,0},{14,2},{8,4},{2,6},{12,8},{6,10},{0,12},{10,14},{5,1},{15,3}... | collective-permute-start | bytes 1474568 | tf_op jit(solution)/shard_map/ppermute | solution.py:22
  11.8 1.0 %copy-start = (bf16[192,1280]{1,0:T(8,128)(2,1)S(1)}, bf16[192,1280]{1,0:T(8,128)(2,1)}, u32[]{:S(2)}) copy-start(bf16[192,1280]{1,0:T(8,128)(2,1)} %queries.1) | copy-start | bytes 1474564
  12.9 1.0 %copy-start.1 = (bf16[192,1280]{1,0:T(8,128)(2,1)S(1)}, bf16[192,1280]{1,0:T(8,128)(2,1)}, u32[]{:S(2)}) copy-start(bf16[192,1280]{1,0:T(8,128)(2,1)} %keys.1) | copy-start | bytes 1474564
  13.9 3.6 %copy-start.2 = (bf16[192,1280]{1,0:T(8,128)(2,1)S(1)}, bf16[192,1280]{1,0:T(8,128)(2,1)}, u32[]{:S(2)}) copy-start(bf16[192,1280]{1,0:T(8,128)(2,1)} %own_values.1) | copy-start | bytes 1474564
  13.9 22.2 %copy-start.5 = (s32[1,4]{1,0:T(1,128)S(1)}, s32[1,4]{1,0:T(1,128)}, u32[]{:S(2)}) copy-start(s32[1,4]{1,0:T(1,128)} %pattern_ref.3) | copy-start | bytes 52
  14.2 1.4 %collective-permute-start.3 = (f32[192,128]{1,0:T(8,128)S(1)}, f32[192,128]{1,0:T(8,128)S(1)}, u32[]{:S(2)}, u32[]{:S(2)}) collective-permute-start(f32[192,128]{1,0:T(8,128)S(1)} %own_squares.1.squares), channel_id=1, source_target_pairs={{1,0},{0,1},{3,2},{2,3},{5,4},{4,5},{7,6},{6,7},{9,8},{8,9},{11,10... | collective-permute-start | bytes 294920 | tf_op jit(solution)/shard_map/ppermute | solution.py:22
  15.6 0.7 %copy-start.3 = (f32[1280]{0:T(1024)S(1)}, f32[1280]{0:T(1024)}, u32[]{:S(2)}) copy-start(f32[1280]{0:T(1024)} %gain.1) | copy-start | bytes 15364
  16.3 0.7 %copy-start.4 = (f32[1280]{0:T(1024)S(1)}, f32[1280]{0:T(1024)}, u32[]{:S(2)}) copy-start(f32[1280]{0:T(1024)} %query_gain.1) | copy-start | bytes 15364
  17.3 13.3 %collective-permute-start.7 = (bf16[192,1280]{1,0:T(8,128)(2,1)S(1)}, bf16[192,1280]{1,0:T(8,128)(2,1)S(1)}, u32[]{:S(2)}, u32[]{:S(2)}) collective-permute-start(bf16[192,1280]{1,0:T(8,128)(2,1)S(1)} %get-tuple-element.23.own_keys), channel_id=1, source_target_pairs={{2,0},{0,2},{6,4},{4,6},{10,8},{8,10},{14,12},{12,14},{3,1},{1,3},... | collective-permute-start | bytes 1474568 | tf_op jit(solution)/shard_map/ppermute | solution.py:22
  17.5 15.0 %collective-permute-start.9 = (bf16[192,1280]{1,0:T(8,128)(2,1)S(1)}, bf16[192,1280]{1,0:T(8,128)(2,1)S(1)}, u32[]{:S(2)}, u32[]{:S(2)}) collective-permute-start(bf16[192,1280]{1,0:T(8,128)(2,1)S(1)} %copy-done.2), channel_id=1, source_target_pairs={{4,0},{14,2},{8,4},{2,6},{12,8},{6,10},{0,12},{10,14},{5,1},{15,3}... | collective-permute-start | bytes 1474568 | tf_op jit(solution)/shard_map/ppermute | solution.py:22
  24.0 1.4 %collective-permute-start.6 = (f32[192,128]{1,0:T(8,128)S(1)}, f32[192,128]{1,0:T(8,128)S(1)}, u32[]{:S(2)}, u32[]{:S(2)}) collective-permute-start(f32[192,128]{1,0:T(8,128)S(1)} %far_squares.1.squares), channel_id=1, source_target_pairs={{1,0},{0,1},{3,2},{2,3},{5,4},{4,5},{7,6},{6,7},{9,8},{8,9},{11,10... | collective-permute-start | bytes 294920 | tf_op jit(solution)/shard_map/ppermute | solution.py:22
  30.6 18.1 %collective-permute-start.8 = (bf16[224,1280]{1,0:T(8,128)(2,1)S(1)}, bf16[224,1280]{1,0:T(8,128)(2,1)S(1)}, u32[]{:S(2)}, u32[]{:S(2)}) collective-permute-start(bf16[224,1280]{1,0:T(8,128)(2,1)S(1)} %prepare_far.1.far_packed.own_packed), channel_id=1, source_target_pairs={{2,0},{0,2},{6,4},{4,6},{10,8},{8,10},{14,12},{12,14},{3,1},{1,3},... | collective-permute-start | bytes 1720328 | tf_op jit(solution)/shard_map/ppermute | solution.py:22
  32.6 16.2 %collective-permute-start.10 = (bf16[192,1280]{1,0:T(8,128)(2,1)S(1)}, bf16[192,1280]{1,0:T(8,128)(2,1)S(1)}, u32[]{:S(2)}, u32[]{:S(2)}) collective-permute-start(bf16[192,1280]{1,0:T(8,128)(2,1)S(1)} %get-tuple-element.23.own_keys), channel_id=1, source_target_pairs={{12,0},{6,2},{0,4},{10,6},{4,8},{14,10},{8,12},{2,14},{13,1},{7,3}... | collective-permute-start | bytes 1474568 | tf_op jit(solution)/shard_map/ppermute | solution.py:22
  34.4 22.1 %collective-permute-start.12 = (bf16[192,1280]{1,0:T(8,128)(2,1)S(1)}, bf16[192,1280]{1,0:T(8,128)(2,1)S(1)}, u32[]{:S(2)}, u32[]{:S(2)}) collective-permute-start(bf16[192,1280]{1,0:T(8,128)(2,1)S(1)} %copy-done.2), channel_id=1, source_target_pairs={{12,0},{6,2},{0,4},{10,6},{4,8},{14,10},{8,12},{2,14},{13,1},{7,3}... | collective-permute-start | bytes 1474568 | tf_op jit(solution)/shard_map/ppermute | solution.py:22
  34.7 21.8 %collective-permute-start.11 = (bf16[192,1280]{1,0:T(8,128)(2,1)S(1)}, bf16[192,1280]{1,0:T(8,128)(2,1)S(1)}, u32[]{:S(2)}, u32[]{:S(2)}) collective-permute-start(bf16[192,1280]{1,0:T(8,128)(2,1)S(1)} %collective-permute-done.9.far_values), channel_id=1, source_target_pairs={{2,0},{0,2},{6,4},{4,6},{10,8},{8,10},{14,12},{12,14},{3,1},{1,3},... | collective-permute-start | bytes 1474568 | tf_op jit(solution)/shard_map/ppermute | solution.py:22

commit v4 on v3

--- a/solution.py
+++ b/solution.py
@@ -13,7 +13,7 @@
 EPSILON = 1e-06
 LANES = 128
 SCRATCH_BYTES = 24 * 2**20
-DEAD = 100.0
+DEAD = float("inf")
 TO_LOG2 = HEAD_DIM ** (-0.5) * math.log2(math.e)
 
 
@@ -64,12 +64,11 @@
     )
 
 
-def pack_kernel(live_ref, keys_ref, values_ref, rows_ref, live_smem, sems):
+def pack_kernel(live_ref, keys_ref, values_ref, rows_ref, sems):
     slots, features = keys_ref.shape
     copies = [
-        pltpu.make_async_copy(live_ref, live_smem, sems.at[0]),
-        pltpu.make_async_copy(keys_ref, rows_ref.at[:, :features], sems.at[1]),
-        pltpu.make_async_copy(values_ref, rows_ref.at[:, features:], sems.at[2]),
+        pltpu.make_async_copy(keys_ref, rows_ref.at[:, :features], sems.at[0]),
+        pltpu.make_async_copy(values_ref, rows_ref.at[:, features:], sems.at[1]),
     ]
     for copy in copies:
         copy.start()
@@ -77,7 +76,7 @@
         copy.wait()
     slot = lax.broadcasted_iota(jnp.int32, (slots, features), 0)
     keys = rows_ref[:, :features].astype(jnp.float32)
-    rows_ref[:, :features] = jnp.where(slot < live_smem[0], keys, DEAD).astype(jnp.bfloat16)
+    rows_ref[:, :features] = jnp.where(slot < live_ref[0], keys, DEAD).astype(jnp.bfloat16)
 
 
 def pack_rows(live, keys, values):
@@ -85,9 +84,9 @@
     return pl.pallas_call(
         pack_kernel,
         out_shape=pltpu.VMEM((slots, 2 * features), jnp.bfloat16),
-        in_specs=[pl.BlockSpec(memory_space=pltpu.HBM)] * 3,
+        in_specs=[SMEM] + [pl.BlockSpec(memory_space=pltpu.HBM)] * 2,
         out_specs=VMEM,
-        scratch_shapes=[pltpu.SMEM((1,), jnp.int32), pltpu.SemaphoreType.DMA((3,))],
+        scratch_shapes=[pltpu.SemaphoreType.DMA((2,))],
         compiler_params=PARAMS,
         cost_estimate=CHEAP,
         name="pack_rows",
@@ -181,7 +180,7 @@
 
 
 def softmax_parts(scores_ref, head, bias):
-    scores = scores_ref[head] * TO_LOG2 + bias
+    scores = jnp.where(bias < 0, bias, scores_ref[head] * TO_LOG2)
     return scores, jnp.max(scores, axis=1, keepdims=True)
 
 
@@ -262,7 +261,7 @@
         [
             block_bias(pattern_flag(pattern_ref, 2), tokens),
             block_bias(pattern_flag(pattern_ref, 3), tokens),
-            jnp.where(marks[:1] < 0.5 * DEAD * LANES, 0.0, -jnp.inf),
+            jnp.where(jnp.abs(marks[:1]) < DEAD, 0.0, -jnp.inf),
         ],
         axis=1,
     )
@@ -408,7 +407,7 @@
     far1_packed = prepare_far(far1_keys, key_gain, far1_squares, rows)
 
     passed_packed = fetch(after(far1_packed, near_values, near_keys), beside)
-    far2_keys = fetch(after(normed_keys, far1_values), far_second)
+    far2_keys = fetch(after(normed_keys, near_keys), far_second)
     far2_values = fetch(after(values, far1_values), far_second)
     passed_values = fetch(far1_values, beside)
 

time: 58.2 us -> 58 us (level)
  waiting for transfers between devices: 26.9 us -> 26 us
  starting transfers between devices: 17 us -> 17.6 us
    ppermute x13, waiting for transfers between devices: 26.9 us -> 26 us  [fetch(): return lax.ppermute(block, axis, [(source_of(i) % n, i) for i in range(n)])]
    ppermute x13, starting transfers between devices: 17 us -> 17.6 us  [fetch(): return lax.ppermute(block, axis, [(source_of(i) % n, i) for i in range(n)])]
  transfers between devices with their start and end apart: 13 -> 13, of which waited for: 7 -> 6; matrix products, arithmetic and copies ran while one was open for 0% -> 0% of each run, Pallas kernels for 13% -> 13%
where the time goes in v4:
time: 58 us; the launch traced here: 57.5 us
  waiting for transfers between devices  26 us (45%)
  starting transfers between devices  17.6 us (30%)
  Pallas kernels  9.74 us (17%)
  local copies, waits for them, and re-layouts  3.46 us (6%)
  between operations  0.73 us (1%)
    ppermute x13, waiting for transfers between devices, fetch(): return lax.ppermute(block, axis, [(source_of(i) % n, i) for i in range(n)])  26 us
    ppermute x13, starting transfers between devices, fetch(): return lax.ppermute(block, axis, [(source_of(i) % n, i) for i in range(n)])  17.6 us
    pallas_call x1, Pallas kernels, attend_late_keys(): pl.pallas_call(late_keys_kernel, out_shape=(pltpu.VMEM((heads, tokens, LA...  3.82 us
    unnamed x12, local copies, waits for them, and re-layouts  3.46 us
    pallas_call x1, Pallas kernels, attend_early(): pl.pallas_call(early_kernel, out_shape=(pltpu.VMEM((heads, tokens, LANES)...  2.94 us
    pallas_call x1, Pallas kernels, attend_late_values(): pl.pallas_call(late_values_kernel, out_shape=jax.ShapeDtypeStruct((tokens...  1.3 us
  transfers between devices with their start and end apart: 13, of which 6 were waited for; matrix products, arithmetic and copies ran while one was open for 0% of the time, Pallas kernels for 13%

profile of v4, /device:TPU:0, one launch (start us, length us, event | category | flops | bytes accessed | tf_op | source)
XLA Modules:
  0.0 57.5 jit_solution(8661515281826200277)
XLA Ops:
  0.7 0.7 %pack_rows.1.refs_0_ = bf16[4,2560]{1,0:T(4,128)(2,1)S(1)} custom-call(s32[1]{0:T(128)S(6)} %copy.10.live_ref, bf16[4,1280]{1,0:T(4,128)(2,1)} %keys_ref.1, bf16[4,1280]{1,0:T(4,128)(2,1)} %values_ref.1), custom_call_target="tpu_custom_call" | custom-call | flops 1 | bytes 1 | tf_op jit(solution)/shard_map/pack_rows/pallas_call | solution.py:84
  1.4 5.1 %collective-permute-start = (bf16[4,2560]{1,0:T(4,128)(2,1)S(1)}, bf16[4,2560]{1,0:T(4,128)(2,1)S(1)}, u32[]{:S(2)}, u32[]{:S(2)}) collective-permute-start(bf16[4,2560]{1,0:T(4,128)(2,1)S(1)} %pack_rows.1.refs_0_), channel_id=1, source_target_pairs={{4,0},{6,2},{8,4},{10,6},{12,8},{14,10},{0,12},{2,14},{5,1},{7,3},... | collective-permute-start | bytes 61448 | tf_op jit(solution)/shard_map/ppermute | solution.py:22
  6.5 0.0 collective-permute-start.1
  6.5 1.0 %collective-permute-start.2 = (bf16[4,2560]{1,0:T(4,128)(2,1)S(1)}, bf16[4,2560]{1,0:T(4,128)(2,1)S(1)}, u32[]{:S(2)}, u32[]{:S(2)}) collective-permute-start(bf16[4,2560]{1,0:T(4,128)(2,1)S(1)} %pack_rows.1.refs_0_), channel_id=1, source_target_pairs={{12,0},{14,2},{0,4},{2,6},{4,8},{6,10},{8,12},{10,14},{13,1},{15,3... | collective-permute-start | bytes 61448 | tf_op jit(solution)/shard_map/ppermute | solution.py:22
  7.5 1.5 %collective-permute-start.5 = (bf16[192,1280]{1,0:T(8,128)(2,1)}, bf16[192,1280]{1,0:T(8,128)(2,1)S(1)}, u32[]{:S(2)}, u32[]{:S(2)}) collective-permute-start(bf16[192,1280]{1,0:T(8,128)(2,1)} %own_values.1), channel_id=1, source_target_pairs={{2,0},{0,2},{6,4},{4,6},{10,8},{8,10},{14,12},{12,14},{3,1},{1,3},... | collective-permute-start | bytes 1474568 | tf_op jit(solution)/shard_map/ppermute | solution.py:22
  9.0 2.8 %collective-permute-start.4 = (bf16[192,1280]{1,0:T(8,128)(2,1)}, bf16[192,1280]{1,0:T(8,128)(2,1)S(1)}, u32[]{:S(2)}, u32[]{:S(2)}) collective-permute-start(bf16[192,1280]{1,0:T(8,128)(2,1)} %keys.1), channel_id=1, source_target_pairs={{4,0},{14,2},{8,4},{2,6},{12,8},{6,10},{0,12},{10,14},{5,1},{15,3}... | collective-permute-start | bytes 1474568 | tf_op jit(solution)/shard_map/ppermute | solution.py:22
  11.8 0.0 copy-start
  11.8 1.0 %copy-done = bf16[192,1280]{1,0:T(8,128)(2,1)S(1)} copy-done((bf16[192,1280]{1,0:T(8,128)(2,1)S(1)}, bf16[192,1280]{1,0:T(8,128)(2,1)}, u32[]{:S(2)}) %copy-start) | copy-done | bytes 491544
  12.9 0.0 copy-start.1
  12.9 1.0 %copy-done.1 = bf16[192,1280]{1,0:T(8,128)(2,1)S(1)} copy-done((bf16[192,1280]{1,0:T(8,128)(2,1)S(1)}, bf16[192,1280]{1,0:T(8,128)(2,1)}, u32[]{:S(2)}) %copy-start.1) | copy-done | bytes 491544
  13.9 0.0 copy-start.2
  13.9 0.0 copy-start.5
  13.9 0.3 own_squares.1.squares
  14.2 0.0 collective-permute-done.refs_1_
  14.2 0.0 collective-permute-done.1.refs_2_
  14.2 0.0 collective-permute-done.2.refs_3_
  14.2 0.1 collective-permute-start.3
  14.3 1.3 %collective-permute-done.3.other_squares = f32[192,128]{1,0:T(8,128)S(1)} collective-permute-done((f32[192,128]{1,0:T(8,128)S(1)}, f32[192,128]{1,0:T(8,128)S(1)}, u32[]{:S(2)}, u32[]{:S(2)}) %collective-permute-start.3) | collective-permute-done | bytes 98336 | tf_op jit(solution)/shard_map/ppermute | solution.py:22
  15.5 0.0 copy-start.3
  15.5 0.7 %copy-done.3 = f32[1280]{0:T(1024)S(1)} copy-done((f32[1280]{0:T(1024)S(1)}, f32[1280]{0:T(1024)}, u32[]{:S(2)}) %copy-start.3) | copy-done | bytes 5144
  16.2 0.0 copy-start.4
  16.2 0.7 %copy-done.4 = f32[1280]{0:T(1024)S(1)} copy-done((f32[1280]{0:T(1024)S(1)}, f32[1280]{0:T(1024)}, u32[]{:S(2)}) %copy-start.4) | copy-done | bytes 5144
  16.9 0.3 prepare.1
  17.2 0.3 collective-permute-start.7
  17.5 0.0 copy-done.2
  17.5 1.3 %collective-permute-start.10 = (bf16[192,1280]{1,0:T(8,128)(2,1)S(1)}, bf16[192,1280]{1,0:T(8,128)(2,1)S(1)}, u32[]{:S(2)}, u32[]{:S(2)}) collective-permute-start(bf16[192,1280]{1,0:T(8,128)(2,1)S(1)} %copy-done.2), channel_id=1, source_target_pairs={{4,0},{14,2},{8,4},{2,6},{12,8},{6,10},{0,12},{10,14},{5,1},{15,3}... | collective-permute-start | bytes 1474568 | tf_op jit(solution)/shard_map/ppermute | solution.py:22
  18.9 5.0 %collective-permute-done.4.refs_0_.keys = bf16[192,1280]{1,0:T(8,128)(2,1)S(1)} collective-permute-done((bf16[192,1280]{1,0:T(8,128)(2,1)}, bf16[192,1280]{1,0:T(8,128)(2,1)S(1)}, u32[]{:S(2)}, u32[]{:S(2)}) %collective-permute-start.4) | collective-permute-done | bytes 491552 | tf_op jit(solution)/shard_map/ppermute | solution.py:22
  23.8 0.2 far_squares.1.squares
  24.0 0.0 collective-permute-done.5.near_values
  24.0 0.1 collective-permute-start.6
  24.1 1.3 %collective-permute-done.6.other_squares = f32[192,128]{1,0:T(8,128)S(1)} collective-permute-done((f32[192,128]{1,0:T(8,128)S(1)}, f32[192,128]{1,0:T(8,128)S(1)}, u32[]{:S(2)}, u32[]{:S(2)}) %collective-permute-start.6) | collective-permute-done | bytes 98336 | tf_op jit(solution)/shard_map/ppermute | solution.py:22
  25.4 0.2 prepare_far.1.far_packed.own_packed
  25.6 5.0 %collective-permute-done.7.near_keys = bf16[192,1280]{1,0:T(8,128)(2,1)S(1)} collective-permute-done((bf16[192,1280]{1,0:T(8,128)(2,1)S(1)}, bf16[192,1280]{1,0:T(8,128)(2,1)S(1)}, u32[]{:S(2)}, u32[]{:S(2)}) %collective-permute-start.7) | collective-permute-done | bytes 491552 | tf_op jit(solution)/shard_map/ppermute | solution.py:22
  30.6 1.3 %collective-permute-start.8 = (bf16[224,1280]{1,0:T(8,128)(2,1)S(1)}, bf16[224,1280]{1,0:T(8,128)(2,1)S(1)}, u32[]{:S(2)}, u32[]{:S(2)}) collective-permute-start(bf16[224,1280]{1,0:T(8,128)(2,1)S(1)} %prepare_far.1.far_packed.own_packed), channel_id=1, source_target_pairs={{2,0},{0,2},{6,4},{4,6},{10,8},{8,10},{14,12},{12,14},{3,1},{1,3},... | collective-permute-start | bytes 1720328 | tf_op jit(solution)/shard_map/ppermute | solution.py:22
  31.9 2.5 %collective-permute-start.9 = (bf16[192,1280]{1,0:T(8,128)(2,1)S(1)}, bf16[192,1280]{1,0:T(8,128)(2,1)S(1)}, u32[]{:S(2)}, u32[]{:S(2)}) collective-permute-start(bf16[192,1280]{1,0:T(8,128)(2,1)S(1)} %get-tuple-element.23.own_keys), channel_id=1, source_target_pairs={{12,0},{6,2},{0,4},{10,6},{4,8},{14,10},{8,12},{2,14},{13,1},{7,3}... | collective-permute-start | bytes 1474568 | tf_op jit(solution)/shard_map/ppermute | solution.py:22
  34.4 0.0 collective-permute-done.10.far_values
  34.4 0.3 collective-permute-start.12
  34.6 1.4 %collective-permute-start.11 = (bf16[192,1280]{1,0:T(8,128)(2,1)S(1)}, bf16[192,1280]{1,0:T(8,128)(2,1)S(1)}, u32[]{:S(2)}, u32[]{:S(2)}) collective-permute-start(bf16[192,1280]{1,0:T(8,128)(2,1)S(1)} %collective-permute-done.10.far_values), channel_id=1, source_target_pairs={{2,0},{0,2},{6,4},{4,6},{10,8},{8,10},{14,12},{12,14},{3,1},{1,3},... | collective-permute-start | bytes 1474568 | tf_op jit(solution)/shard_map/ppermute | solution.py:22
  36.1 0.0 copy-done.5
  36.1 2.9 %attend_early.1 = (f32[10,192,128]{2,1,0:T(8,128)S(1)}, f32[10,192,128]{2,1,0:T(8,128)S(1)}, f32[192,1280]{1,0:T(8,128)S(1)}) custom-call(s32[1,4]{1,0:T(1,128)S(1)} %copy-done.5, bf16[192,1280]{1,0:T(8,128)(2,1)S(1)} %get-tuple-element.19.query_ref, bf16[192,1280]{1,0:T(8,128)(2,1)S(1)} %get-tuple-element.23.own_keys, ...), custom_call_target="tpu_custom_call" | custom-call | flops 1 | bytes 1 | tf_op jit(solution)/shard_map/attend_early/pallas_call | solution.py:314
  39.0 8.8 %collective-permute-done.9.far_keys = bf16[192,1280]{1,0:T(8,128)(2,1)S(1)} collective-permute-done((bf16[192,1280]{1,0:T(8,128)(2,1)S(1)}, bf16[192,1280]{1,0:T(8,128)(2,1)S(1)}, u32[]{:S(2)}, u32[]{:S(2)}) %collective-permute-start.9) | collective-permute-done | bytes 491552 | tf_op jit(solution)/shard_map/ppermute | solution.py:22
  47.8 0.0 collective-permute-done.8.passed_packed
  47.8 3.8 %attend_late_keys.1 = (f32[10,192,128]{2,1,0:T(8,128)S(1)}, f32[192,1280]{1,0:T(8,128)S(1)}, bf16[10,192,384]{2,1,0:T(8,128)(2,1)S(1)}) custom-call(s32[1,4]{1,0:T(1,128)S(1)} %copy-done.5, bf16[192,1280]{1,0:T(8,128)(2,1)S(1)} %get-tuple-element.19.query_ref, bf16[224,1280]{1,0:T(8,128)(2,1)S(1)} %prepare_far.1.far_packed.own_packed, ...), custom_call_target="tpu_custom_call" | custom-call | flops 1 | bytes 1 | tf_op jit(solution)/shard_map/attend_late_keys/pallas_call | solution.py:338
  51.7 4.6 %collective-permute-done.12.far_values = bf16[192,1280]{1,0:T(8,128)(2,1)S(1)} collective-permute-done((bf16[192,1280]{1,0:T(8,128)(2,1)S(1)}, bf16[192,1280]{1,0:T(8,128)(2,1)S(1)}, u32[]{:S(2)}, u32[]{:S(2)}) %collective-permute-start.12) | collective-permute-done | bytes 491552 | tf_op jit(solution)/shard_map/ppermute | solution.py:22
  56.2 0.0 collective-permute-done.11.passed_values
  56.2 1.3 %attend_late_values.1 = bf16[192,1280]{1,0:T(8,128)(2,1)} custom-call(f32[10,192,128]{2,1,0:T(8,128)S(1)} %get-tuple-element.27.inverses_ref, f32[192,1280]{1,0:T(8,128)S(1)} %get-tuple-element.28.partial_ref, bf16[10,192,384]{2,1,0:T(8,128)(2,1)S(1)} %get-tuple-element.29.weights_ref, bf16[192,1280]{1,0:T(8,128)(2,1)S(1)} %collective-permute-done.11.passed_values, ...), custom_call_target="tpu_custom_call" | custom-call | flops 1 | bytes 1 | tf_op jit(solution)/shard_map/attend_late_values/pallas_call | solution.py:361
Async XLA Ops:
  1.4 12.8 %collective-permute-start = (bf16[4,2560]{1,0:T(4,128)(2,1)S(1)}, bf16[4,2560]{1,0:T(4,128)(2,1)S(1)}, u32[]{:S(2)}, u32[]{:S(2)}) collective-permute-start(bf16[4,2560]{1,0:T(4,128)(2,1)S(1)} %pack_rows.1.refs_0_), channel_id=1, source_target_pairs={{4,0},{6,2},{8,4},{10,6},{12,8},{14,10},{0,12},{2,14},{5,1},{7,3},... | collective-permute-start | bytes 61448 | tf_op jit(solution)/shard_map/ppermute | solution.py:22
  6.5 7.7 %collective-permute-start.1 = (bf16[4,2560]{1,0:T(4,128)(2,1)S(1)}, bf16[4,2560]{1,0:T(4,128)(2,1)S(1)}, u32[]{:S(2)}, u32[]{:S(2)}) collective-permute-start(bf16[4,2560]{1,0:T(4,128)(2,1)S(1)} %pack_rows.1.refs_0_), channel_id=1, source_target_pairs={{8,0},{10,2},{12,4},{14,6},{0,8},{2,10},{4,12},{6,14},{9,1},{11,3}... | collective-permute-start | bytes 61448 | tf_op jit(solution)/shard_map/ppermute | solution.py:22
  6.5 7.7 %collective-permute-start.2 = (bf16[4,2560]{1,0:T(4,128)(2,1)S(1)}, bf16[4,2560]{1,0:T(4,128)(2,1)S(1)}, u32[]{:S(2)}, u32[]{:S(2)}) collective-permute-start(bf16[4,2560]{1,0:T(4,128)(2,1)S(1)} %pack_rows.1.refs_0_), channel_id=1, source_target_pairs={{12,0},{14,2},{0,4},{2,6},{4,8},{6,10},{8,12},{10,14},{13,1},{15,3... | collective-permute-start | bytes 61448 | tf_op jit(solution)/shard_map/ppermute | solution.py:22
  7.5 16.5 %collective-permute-start.5 = (bf16[192,1280]{1,0:T(8,128)(2,1)}, bf16[192,1280]{1,0:T(8,128)(2,1)S(1)}, u32[]{:S(2)}, u32[]{:S(2)}) collective-permute-start(bf16[192,1280]{1,0:T(8,128)(2,1)} %own_values.1), channel_id=1, source_target_pairs={{2,0},{0,2},{6,4},{4,6},{10,8},{8,10},{14,12},{12,14},{3,1},{1,3},... | collective-permute-start | bytes 1474568 | tf_op jit(solution)/shard_map/ppermute | solution.py:22
  9.0 14.8 %collective-permute-start.4 = (bf16[192,1280]{1,0:T(8,128)(2,1)}, bf16[192,1280]{1,0:T(8,128)(2,1)S(1)}, u32[]{:S(2)}, u32[]{:S(2)}) collective-permute-start(bf16[192,1280]{1,0:T(8,128)(2,1)} %keys.1), channel_id=1, source_target_pairs={{4,0},{14,2},{8,4},{2,6},{12,8},{6,10},{0,12},{10,14},{5,1},{15,3}... | collective-permute-start | bytes 1474568 | tf_op jit(solution)/shard_map/ppermute | solution.py:22
  11.8 1.0 %copy-start = (bf16[192,1280]{1,0:T(8,128)(2,1)S(1)}, bf16[192,1280]{1,0:T(8,128)(2,1)}, u32[]{:S(2)}) copy-start(bf16[192,1280]{1,0:T(8,128)(2,1)} %queries.1) | copy-start | bytes 1474564
  12.9 1.0 %copy-start.1 = (bf16[192,1280]{1,0:T(8,128)(2,1)S(1)}, bf16[192,1280]{1,0:T(8,128)(2,1)}, u32[]{:S(2)}) copy-start(bf16[192,1280]{1,0:T(8,128)(2,1)} %keys.1) | copy-start | bytes 1474564
  13.9 3.6 %copy-start.2 = (bf16[192,1280]{1,0:T(8,128)(2,1)S(1)}, bf16[192,1280]{1,0:T(8,128)(2,1)}, u32[]{:S(2)}) copy-start(bf16[192,1280]{1,0:T(8,128)(2,1)} %own_values.1) | copy-start | bytes 1474564
  13.9 22.2 %copy-start.5 = (s32[1,4]{1,0:T(1,128)S(1)}, s32[1,4]{1,0:T(1,128)}, u32[]{:S(2)}) copy-start(s32[1,4]{1,0:T(1,128)} %pattern_ref.3) | copy-start | bytes 52
  14.2 1.4 %collective-permute-start.3 = (f32[192,128]{1,0:T(8,128)S(1)}, f32[192,128]{1,0:T(8,128)S(1)}, u32[]{:S(2)}, u32[]{:S(2)}) collective-permute-start(f32[192,128]{1,0:T(8,128)S(1)} %own_squares.1.squares), channel_id=1, source_target_pairs={{1,0},{0,1},{3,2},{2,3},{5,4},{4,5},{7,6},{6,7},{9,8},{8,9},{11,10... | collective-permute-start | bytes 294920 | tf_op jit(solution)/shard_map/ppermute | solution.py:22
  15.5 0.7 %copy-start.3 = (f32[1280]{0:T(1024)S(1)}, f32[1280]{0:T(1024)}, u32[]{:S(2)}) copy-start(f32[1280]{0:T(1024)} %gain.1) | copy-start | bytes 15364
  16.2 0.7 %copy-start.4 = (f32[1280]{0:T(1024)S(1)}, f32[1280]{0:T(1024)}, u32[]{:S(2)}) copy-start(f32[1280]{0:T(1024)} %query_gain.1) | copy-start | bytes 15364
  17.2 13.3 %collective-permute-start.7 = (bf16[192,1280]{1,0:T(8,128)(2,1)S(1)}, bf16[192,1280]{1,0:T(8,128)(2,1)S(1)}, u32[]{:S(2)}, u32[]{:S(2)}) collective-permute-start(bf16[192,1280]{1,0:T(8,128)(2,1)S(1)} %get-tuple-element.23.own_keys), channel_id=1, source_target_pairs={{2,0},{0,2},{6,4},{4,6},{10,8},{8,10},{14,12},{12,14},{3,1},{1,3},... | collective-permute-start | bytes 1474568 | tf_op jit(solution)/shard_map/ppermute | solution.py:22
  17.5 16.8 %collective-permute-start.10 = (bf16[192,1280]{1,0:T(8,128)(2,1)S(1)}, bf16[192,1280]{1,0:T(8,128)(2,1)S(1)}, u32[]{:S(2)}, u32[]{:S(2)}) collective-permute-start(bf16[192,1280]{1,0:T(8,128)(2,1)S(1)} %copy-done.2), channel_id=1, source_target_pairs={{4,0},{14,2},{8,4},{2,6},{12,8},{6,10},{0,12},{10,14},{5,1},{15,3}... | collective-permute-start | bytes 1474568 | tf_op jit(solution)/shard_map/ppermute | solution.py:22
  24.0 1.4 %collective-permute-start.6 = (f32[192,128]{1,0:T(8,128)S(1)}, f32[192,128]{1,0:T(8,128)S(1)}, u32[]{:S(2)}, u32[]{:S(2)}) collective-permute-start(f32[192,128]{1,0:T(8,128)S(1)} %far_squares.1.squares), channel_id=1, source_target_pairs={{1,0},{0,1},{3,2},{2,3},{5,4},{4,5},{7,6},{6,7},{9,8},{8,9},{11,10... | collective-permute-start | bytes 294920 | tf_op jit(solution)/shard_map/ppermute | solution.py:22
  30.6 17.2 %collective-permute-start.8 = (bf16[224,1280]{1,0:T(8,128)(2,1)S(1)}, bf16[224,1280]{1,0:T(8,128)(2,1)S(1)}, u32[]{:S(2)}, u32[]{:S(2)}) collective-permute-start(bf16[224,1280]{1,0:T(8,128)(2,1)S(1)} %prepare_far.1.far_packed.own_packed), channel_id=1, source_target_pairs={{2,0},{0,2},{6,4},{4,6},{10,8},{8,10},{14,12},{12,14},{3,1},{1,3},... | collective-permute-start | bytes 1720328 | tf_op jit(solution)/shard_map/ppermute | solution.py:22
  31.9 16.0 %collective-permute-start.9 = (bf16[192,1280]{1,0:T(8,128)(2,1)S(1)}, bf16[192,1280]{1,0:T(8,128)(2,1)S(1)}, u32[]{:S(2)}, u32[]{:S(2)}) collective-permute-start(bf16[192,1280]{1,0:T(8,128)(2,1)S(1)} %get-tuple-element.23.own_keys), channel_id=1, source_target_pairs={{12,0},{6,2},{0,4},{10,6},{4,8},{14,10},{8,12},{2,14},{13,1},{7,3}... | collective-permute-start | bytes 1474568 | tf_op jit(solution)/shard_map/ppermute | solution.py:22
  34.4 21.9 %collective-permute-start.12 = (bf16[192,1280]{1,0:T(8,128)(2,1)S(1)}, bf16[192,1280]{1,0:T(8,128)(2,1)S(1)}, u32[]{:S(2)}, u32[]{:S(2)}) collective-permute-start(bf16[192,1280]{1,0:T(8,128)(2,1)S(1)} %copy-done.2), channel_id=1, source_target_pairs={{12,0},{6,2},{0,4},{10,6},{4,8},{14,10},{8,12},{2,14},{13,1},{7,3}... | collective-permute-start | bytes 1474568 | tf_op jit(solution)/shard_map/ppermute | solution.py:22
  34.6 21.6 %collective-permute-start.11 = (bf16[192,1280]{1,0:T(8,128)(2,1)S(1)}, bf16[192,1280]{1,0:T(8,128)(2,1)S(1)}, u32[]{:S(2)}, u32[]{:S(2)}) collective-permute-start(bf16[192,1280]{1,0:T(8,128)(2,1)S(1)} %collective-permute-done.10.far_values), channel_id=1, source_target_pairs={{2,0},{0,2},{6,4},{4,6},{10,8},{8,10},{14,12},{12,14},{3,1},{1,3},... | collective-permute-start | bytes 1474568 | tf_op jit(solution)/shard_map/ppermute | solution.py:22

commit v5 on v4

--- a/solution.py
+++ b/solution.py
@@ -52,6 +52,10 @@
 
 
 CHEAP = pl.CostEstimate(flops=1, transcendentals=0, bytes_accessed=1)
+
+EARLY = pl.CostEstimate(flops=5*10**9, transcendentals=0, bytes_accessed=1)
+SMALL_HOLD = pl.CostEstimate(flops=2*10**9, transcendentals=0, bytes_accessed=1)
+HOLD = pl.CostEstimate(flops=3 * 10**10, transcendentals=0, bytes_accessed=1)
 
 
 def head_columns(head):
@@ -93,81 +97,118 @@
     )(live, in_hbm(keys), in_hbm(values))
 
 
-def squares_kernel(*refs):
-    *row_refs, squares_ref = refs
+def load_kernel(*refs):
+    sources, loaded = refs[:4], refs[4:8]
+    squares_ref, sems = refs[8:]
+    copies = [
+        pltpu.make_async_copy(source, target, sems.at[i])
+        for i, (source, target) in enumerate(zip(sources, loaded))
+    ]
+    for copy in copies:
+        copy.start()
     lane = lax.broadcasted_iota(jnp.int32, squares_ref.shape, 1)
     squares = jnp.zeros(squares_ref.shape, jnp.float32)
-    for column, ref in enumerate(row_refs):
-        rows = ref[...].astype(jnp.float32)
-        squares = jnp.where(lane == column, jnp.sum(rows * rows, axis=1, keepdims=True), squares)
+    for column, copy in enumerate(copies):
+        copy.wait()
+        if column < 2:
+            rows = loaded[column][...].astype(jnp.float32)
+            sums = jnp.sum(rows * rows, axis=1, keepdims=True)
+            squares = jnp.where(lane == column, sums, squares)
     squares_ref[...] = squares
 
 
-def square_sums(name, blocks, earlier=()):
-    squares = pl.pallas_call(
-        squares_kernel,
-        out_shape=pltpu.VMEM((blocks[0].shape[0], LANES), jnp.float32),
-        in_specs=[VMEM] * len(blocks),
-        out_specs=VMEM,
-        compiler_params=PARAMS,
-        cost_estimate=CHEAP,
-        name=name,
-    )(*map(in_vmem, blocks))
-    squares = after(squares, *earlier)
-    return squares, fetch(squares, lambda i: i ^ 1, "tp")
+def load(queries, keys, gains):
+    operands = (queries, keys, *gains)
+    return pl.pallas_call(
+        load_kernel,
+        out_shape=(
+            *(pltpu.VMEM(operand.shape, operand.dtype) for operand in operands),
+            pltpu.VMEM((queries.shape[0], LANES), jnp.float32),
+        ),
+        in_specs=[pl.BlockSpec(memory_space=pltpu.HBM)] * 4,
+        out_specs=(VMEM,) * 5,
+        scratch_shapes=[pltpu.SemaphoreType.DMA((4,))],
+        compiler_params=PARAMS,
+        cost_estimate=CHEAP,
+        name="load",
+    )(*map(in_hbm, operands))
 
 
 def normalized(rows_ref, gain_ref, squares_refs, column):
     square_sum = sum(ref[:, column : column + 1] for ref in squares_refs)
     scale = lax.rsqrt(square_sum / (HEADS * HEAD_DIM) + EPSILON)
-    rows = rows_ref[...].astype(jnp.float32)
+    rows = rows_ref[: scale.shape[0]].astype(jnp.float32)
     return (rows * scale * gain_ref[...][None, :]).astype(jnp.bfloat16)
 
 
-def prepare_kernel(
-    queries, keys, query_gain, key_gain, squares, other_squares, query_ref, key_ref
-):
+def prepare_kernel(queries, keys, query_gain, key_gain, squares, other_squares, *refs):
+    *row_refs, query_ref, key_ref, packed_ref, pair_ref = refs
+    tokens, features = keys.shape
     query_ref[...] = normalized(queries, query_gain, (squares, other_squares), 0)
-    key_ref[...] = normalized(keys, key_gain, (squares, other_squares), 1)
-
-
-def prepare(queries, keys, gains, squares):
-    return pl.pallas_call(
-        prepare_kernel,
-        out_shape=(pltpu.VMEM(keys.shape, jnp.bfloat16),) * 2,
-        in_specs=[VMEM] * 6,
-        out_specs=(VMEM,) * 2,
-        compiler_params=PARAMS,
-        cost_estimate=CHEAP,
-        name="prepare",
-    )(*map(in_vmem, (queries, keys, *gains, *squares)))
-
-
-def prepare_far_kernel(keys, gain, squares, other_squares, *refs):
-    *row_refs, packed_ref = refs
-    tokens, features = keys.shape
-    count = (packed_ref.shape[0] - tokens) // 2
-    packed_ref[:tokens] = normalized(keys, gain, (squares, other_squares), 0)
-    first = tokens
+    normed_keys = normalized(keys, key_gain, (squares, other_squares), 1)
+    key_ref[...] = normed_keys
+    packed_ref[:tokens] = normed_keys
+    count = pair_ref.shape[0]
+    first = 0
     for ref in row_refs:
-        slots = ref.shape[0]
-        packed_ref[first : first + slots] = ref[:, :features]
-        packed_ref[first + count : first + count + slots] = ref[:, features:]
-        first += slots
-
-
-def prepare_far(keys, gain, squares, rows):
+        pair_ref[first : first + ref.shape[0]] = ref[...]
+        first += ref.shape[0]
+    packed_ref[tokens : tokens + count] = pair_ref[:, :features]
+    packed_ref[tokens + count :] = pair_ref[:, features:]
+
+
+def prepare(queries, keys, gains, squares, rows):
     tokens, features = keys.shape
     count = sum(part.shape[0] for part in rows)
     return pl.pallas_call(
-        prepare_far_kernel,
-        out_shape=pltpu.VMEM((tokens + 2 * count, features), jnp.bfloat16),
-        in_specs=[VMEM] * (4 + len(rows)),
+        prepare_kernel,
+        out_shape=(
+            pltpu.VMEM((tokens, features), jnp.bfloat16),
+            pltpu.VMEM((tokens, features), jnp.bfloat16),
+            pltpu.VMEM((tokens + 2 * count, features), jnp.bfloat16),
+            pltpu.VMEM((count, 2 * features), jnp.bfloat16),
+        ),
+        in_specs=[VMEM] * (6 + len(rows)),
+        out_specs=(VMEM,) * 4,
+        compiler_params=PARAMS,
+        cost_estimate=CHEAP,
+        name="prepare",
+    )(*map(in_vmem, (queries, keys, *gains, *squares, *rows)))
+
+
+def halve_kernel(rows, first_ref, second_ref):
+    half = first_ref.shape[0]
+    first_ref[...] = rows[:half]
+    second_ref[...] = rows[half:]
+
+
+def halve(rows):
+    half = pltpu.VMEM((rows.shape[0] // 2, rows.shape[1]), rows.dtype)
+    return pl.pallas_call(
+        halve_kernel,
+        out_shape=(half, half),
+        in_specs=[VMEM],
+        out_specs=(VMEM,) * 2,
+        compiler_params=PARAMS,
+        cost_estimate=CHEAP,
+        name="halve",
+    )(in_vmem(rows))
+
+
+def strip_kernel(packed, key_ref):
+    key_ref[...] = packed[: key_ref.shape[0]]
+
+
+def strip(packed, tokens, cost=None):
+    return pl.pallas_call(
+        strip_kernel,
+        out_shape=pltpu.VMEM((tokens, packed.shape[1]), jnp.bfloat16),
+        in_specs=[VMEM],
         out_specs=VMEM,
         compiler_params=PARAMS,
-        cost_estimate=CHEAP,
-        name="prepare_far",
-    )(*map(in_vmem, (keys, gain, *squares, *rows)))
+        cost_estimate=cost or CHEAP,
+        name="strip",
+    )(in_vmem(packed))
 
 
 def pattern_flag(pattern_ref, column):
@@ -189,7 +230,7 @@
     query_ref,
     own_keys,
     near_keys,
-    far_packed,
+    far_keys,
     own_values,
     near_values,
     far_values,
@@ -211,7 +252,7 @@
     )
     for head in range(heads):
         columns = head_columns(head)
-        keys = [own_keys[:, columns], near_keys[:, columns], far_packed[:tokens, columns]]
+        keys = [ref[:, columns] for ref in (own_keys, near_keys, far_keys)]
         scores_ref[head] = score(query_ref[:, columns], jnp.concatenate(keys, axis=0))
     for head in range(heads):
         scores, peak = softmax_parts(scores_ref, head, bias)
@@ -233,29 +274,32 @@
 def late_keys_kernel(
     pattern_ref,
     query_ref,
-    own_packed,
-    passed_packed,
-    far_keys,
+    passed_keys,
+    far_packed,
+    far1_packed,
     old_peaks_ref,
     old_totals_ref,
     old_partial_ref,
-    inverses_ref,
-    partial_ref,
-    weights_ref,
-    keys_ref,
-    values_ref,
-    scores_ref,
+    *refs,
 ):
+    *row_refs, inverses_ref, partial_ref, weights_ref, keys_ref, values_ref, scores_ref = refs
     tokens, features = query_ref.shape
     heads = features // HEAD_DIM
     blocks = 2 * tokens
-    count = values_ref.shape[0] // 2
-    keys_ref[:tokens] = passed_packed[:tokens]
-    keys_ref[tokens:blocks] = far_keys[...]
-    for place, packed in enumerate((own_packed, passed_packed)):
-        first = place * count
-        keys_ref[blocks + first : blocks + first + count] = packed[tokens : tokens + count]
-        values_ref[first : first + count] = packed[tokens + count :]
+    keys_ref[:tokens] = passed_keys[...]
+    keys_ref[tokens:blocks] = far_packed[:tokens]
+    first = 0
+    for ref in row_refs:
+        count = ref.shape[0]
+        keys_ref[blocks + first : blocks + first + count] = ref[:, :features]
+        values_ref[first : first + count] = ref[:, features:]
+        first += count
+    for packed in (far_packed, far1_packed):
+        count = (packed.shape[0] - tokens) // 2
+        if count:
+            keys_ref[blocks + first : blocks + first + count] = packed[tokens : tokens + count]
+            values_ref[first : first + count] = packed[tokens + count :]
+            first += count
     marks = score(jnp.ones((8, LANES), jnp.bfloat16), keys_ref[blocks:, :LANES])
     bias = jnp.concatenate(
         [
@@ -287,13 +331,15 @@
 
 
 def late_values_kernel(
-    inverses_ref, partial_ref, weights_ref, passed_values, far_values, out_ref, out_vmem, sems
+    inverses_ref, partial_ref, weights_ref, first_half, second_half, far_values, out_ref, out_vmem, sems
 ):
     heads = weights_ref.shape[0]
     copies = []
     for head in range(heads):
         columns = head_columns(head)
-        values = jnp.concatenate([passed_values[:, columns], far_values[:, columns]], axis=0)
+        values = jnp.concatenate(
+            [ref[:, columns] for ref in (first_half, second_half, far_values)], axis=0
+        )
         product = jnp.dot(weights_ref[head], values, preferred_element_type=jnp.float32)
         out_vmem[:, columns] = (
             partial_ref[:, columns] + product * inverses_ref[head]
@@ -325,16 +371,18 @@
             pltpu.VMEM((heads, tokens, count), jnp.bfloat16),
         ],
         compiler_params=PARAMS,
-        cost_estimate=CHEAP,
+        cost_estimate=EARLY,
         name="attend_early",
     )(pattern, *map(in_vmem, (queries, *keys, *values)))
 
 
-def attend_late_keys(pattern, queries, own_packed, passed_packed, far_keys, state):
+def attend_late_keys(pattern, queries, passed_keys, far_packed, far1_packed, rows, state):
     tokens, features = queries.shape
     heads = features // HEAD_DIM
-    rows = own_packed.shape[0] - tokens
-    count = 2 * tokens + rows
+    attached = (far_packed.shape[0] + far1_packed.shape[0]) // 2 - tokens
+    slots = attached + sum(part.shape[0] for part in rows)
+    count = 2 * tokens + slots
+    operands = (queries, passed_keys, far_packed, far1_packed, *state, *rows)
     return pl.pallas_call(
         late_keys_kernel,
         out_shape=(
@@ -342,17 +390,17 @@
             pltpu.VMEM((tokens, features), jnp.float32),
             pltpu.VMEM((heads, tokens, 2 * tokens), jnp.bfloat16),
         ),
-        in_specs=[SMEM] + [VMEM] * 7,
+        in_specs=[SMEM] + [VMEM] * len(operands),
         out_specs=(VMEM,) * 3,
         scratch_shapes=[
             pltpu.VMEM((count, features), jnp.bfloat16),
-            pltpu.VMEM((rows, features), jnp.bfloat16),
+            pltpu.VMEM((slots, features), jnp.bfloat16),
             pltpu.VMEM((heads, tokens, count), jnp.float32),
         ],
         compiler_params=PARAMS,
         cost_estimate=CHEAP,
         name="attend_late_keys",
-    )(pattern, *map(in_vmem, (queries, own_packed, passed_packed, far_keys, *state)))
+    )(pattern, *map(in_vmem, operands))
 
 
 def attend_late_values(inverses, partial, weights, values):
@@ -361,7 +409,7 @@
     return pl.pallas_call(
         late_values_kernel,
         out_shape=jax.ShapeDtypeStruct((tokens, features), jnp.bfloat16),
-        in_specs=[VMEM] * 5,
+        in_specs=[VMEM] * 6,
         out_specs=pl.BlockSpec(memory_space=pl.ANY),
         scratch_shapes=[
             pltpu.VMEM((tokens, features), jnp.bfloat16),
@@ -373,15 +421,9 @@
     )(*map(in_vmem, (inverses, partial, weights, *values)))
 
 
-def column_rows(rows):
+def other_rows(pair):
     n = lax.axis_size("frm")
-    if n <= 8:
-        return [rows] + [fetch(rows, lambda i: i + distance) for distance in range(2, n, 2)]
-    distance = n // 2
-    while distance > 1:
-        rows = jnp.concatenate([rows, fetch(rows, lambda i: i ^ distance)], axis=0)
-        distance //= 2
-    return [rows]
+    return [fetch(pair, lambda i: i + distance) for distance in range(4, n - 2, 2)]
 
 
 def shards(
@@ -395,32 +437,40 @@
     reference_values,
     reference_live,
 ):
-    far1_keys = fetch(in_hbm(key_rows), far_first)
-    near_values = fetch(values, beside)
+    tokens = queries.shape[0]
+    far1_values = fetch(values, far_first)
     rows = pack_rows(reference_live, reference_keys, reference_values)
-    far1_values = fetch(values, far_first)
-    rows = column_rows(rows)
-    own_squares = square_sums("own_squares", (queries, key_rows), rows)
-    normed_queries, normed_keys = prepare(queries, key_rows, (query_gain, key_gain), own_squares)
+    rows = [rows, fetch(rows, beside)]
+    near_values = fetch(after(values, *rows), beside)
+    *loaded, squares = load(queries, key_rows, (query_gain, key_gain))
+    own_squares = (squares, fetch(squares, lambda i: i ^ 1, "tp"))
+    normed_queries, normed_keys, packed_keys, pair = prepare(
+        *loaded[:2], loaded[2:], own_squares, rows
+    )
     near_keys = fetch(normed_keys, beside)
-    far1_squares = square_sums("far_squares", (far1_keys,), (near_values,))
-    far1_packed = prepare_far(far1_keys, key_gain, far1_squares, rows)
-
-    passed_packed = fetch(after(far1_packed, near_values, near_keys), beside)
-    far2_keys = fetch(after(normed_keys, near_keys), far_second)
-    far2_values = fetch(after(values, far1_values), far_second)
-    passed_values = fetch(far1_values, beside)
+    far1_packed = fetch(packed_keys, far_first)
+    held = strip(after(pair, far1_values), pair.shape[0], SMALL_HOLD)
+    held = strip(after(held, near_values), pair.shape[0], HOLD)
+    rows = [pair] + other_rows(held)
+
+    far1_keys = strip(far1_packed, tokens)
+    passed_keys = fetch(after(far1_keys, near_keys, *rows), beside)
+    far2_packed = fetch(after(packed_keys, far1_packed), far_second)
+    far2_values = fetch(after(values, far1_keys), far_second)
+    first_half, second_half = halve(far1_values)
+    passed_first = fetch(first_half, beside)
+    passed_second = fetch(after(second_half, far1_keys), beside)
 
     state = attend_early(
         pattern,
-        normed_queries,
-        (normed_keys, near_keys, far1_packed),
+        after(normed_queries, passed_first),
+        (normed_keys, near_keys, far1_keys),
         (values, near_values, far1_values),
     )
     inverses, partial, weights = attend_late_keys(
-        pattern, normed_queries, far1_packed, passed_packed, far2_keys, state
-    )
-    return attend_late_values(inverses, partial, weights, (passed_values, far2_values))
+        pattern, normed_queries, passed_keys, far2_packed, far1_packed, rows, state
+    )
+    return attend_late_values(inverses, partial, weights, (passed_first, passed_second, far2_values))
 
 
 def solution(mesh):

time: 58 us -> 56.7 us (0.978)
  waiting for transfers between devices: 26 us -> 32.8 us
  starting transfers between devices: 17.6 us -> 12.3 us
  local copies, waits for them, and re-layouts: 3.46 us -> 0.01 us
  Pallas kernels: 9.74 us -> 10.6 us
    ppermute x13 -> x12, waiting for transfers between devices: 26 us -> 32.8 us  [fetch(): return lax.ppermute(block, axis, [(source_of(i) % n, i) for i in range(n)])]
    ppermute x13 -> x12, starting transfers between devices: 17.6 us -> 12.3 us  [fetch(): return lax.ppermute(block, axis, [(source_of(i) % n, i) for i in range(n)])]
    unnamed x12 -> x4, local copies, waits for them, and re-layouts: 3.46 us -> 0.01 us
    pallas_call x4 -> x6, Pallas kernels: 0.94 us -> 1.81 us  [the longest x1 1.42 us: load(): pl.pallas_call(load_kernel, out_shape=(*(pltpu.VMEM(operand.shape, operan...]
  transfers between devices with their start and end apart: 13 -> 12, of which waited for: 6 -> 8; matrix products, arithmetic and copies ran while one was open for 0% -> 0% of each run, Pallas kernels for 13% -> 17%
where the time goes in v5:
time: 56.7 us; the launch traced here: 56.4 us
  waiting for transfers between devices  32.8 us (58%)
  starting transfers between devices  12.3 us (22%)
  Pallas kernels  10.6 us (19%)
  between operations  0.74 us (1%)
    ppermute x12, waiting for transfers between devices, fetch(): return lax.ppermute(block, axis, [(source_of(i) % n, i) for i in range(n)])  32.8 us
    ppermute x12, starting transfers between devices, fetch(): return lax.ppermute(block, axis, [(source_of(i) % n, i) for i in range(n)])  12.3 us
    pallas_call x1, Pallas kernels, attend_late_keys(): pl.pallas_call(late_keys_kernel, out_shape=(pltpu.VMEM((heads, tokens, LA...  3.82 us
    pallas_call x1, Pallas kernels, attend_early(): pl.pallas_call(early_kernel, out_shape=(pltpu.VMEM((heads, tokens, LANES)...  2.96 us
    pallas_call x1, Pallas kernels, load(): pl.pallas_call(load_kernel, out_shape=(*(pltpu.VMEM(operand.shape, operan...  1.42 us
    pallas_call x1, Pallas kernels, attend_late_values(): pl.pallas_call(late_values_kernel, out_shape=jax.ShapeDtypeStruct((tokens...  1.27 us
  transfers between devices with their start and end apart: 12, of which 8 were waited for; matrix products, arithmetic and copies ran while one was open for 0% of the time, Pallas kernels for 17%

profile of v5, /device:TPU:0, one launch (start us, length us, event | category | flops | bytes accessed | tf_op | source)
XLA Modules:
  0.0 56.4 jit_solution(5157418038666591386)
XLA Ops:
  0.0 5.0 %collective-permute-start.4 = (bf16[192,1280]{1,0:T(8,128)(2,1)}, bf16[192,1280]{1,0:T(8,128)(2,1)S(1)}, u32[]{:S(2)}, u32[]{:S(2)}) collective-permute-start(bf16[192,1280]{1,0:T(8,128)(2,1)} %own_values.1), channel_id=1, source_target_pairs={{4,0},{14,2},{8,4},{2,6},{12,8},{6,10},{0,12},{10,14},{5,1},{15,3}... | collective-permute-start | bytes 1474568 | tf_op jit(solution)/shard_map/ppermute | solution.py:22
  5.7 0.7 %pack_rows.1.refs_0_ = bf16[4,2560]{1,0:T(4,128)(2,1)S(1)} custom-call(s32[1]{0:T(128)S(6)} %copy.10.live_ref, bf16[4,1280]{1,0:T(4,128)(2,1)} %keys_ref.1, bf16[4,1280]{1,0:T(4,128)(2,1)} %values_ref.1), custom_call_target="tpu_custom_call" | custom-call | flops 1 | bytes 1 | tf_op jit(solution)/shard_map/pack_rows/pallas_call | solution.py:88
  6.5 0.1 collective-permute-start.1
  6.5 3.8 %collective-permute-done.1.refs_1_ = bf16[4,2560]{1,0:T(4,128)(2,1)S(1)} collective-permute-done((bf16[4,2560]{1,0:T(4,128)(2,1)S(1)}, bf16[4,2560]{1,0:T(4,128)(2,1)S(1)}, u32[]{:S(2)}, u32[]{:S(2)}) %collective-permute-start.1) | collective-permute-done | bytes 20512 | tf_op jit(solution)/shard_map/ppermute | solution.py:22
  10.3 0.0 collective-permute-start.5
  10.3 1.4 %load.1 = (bf16[192,1280]{1,0:T(8,128)(2,1)S(1)}, bf16[192,1280]{1,0:T(8,128)(2,1)S(1)}, f32[1280]{0:T(1024)S(1)}, f32[1280]{0:T(1024)S(1)}, f32[192,128]{1,0:T(8,128)S(1)}) custom-call(bf16[192,1280]{1,0:T(8,128)(2,1)} %refs_0_.1, bf16[192,1280]{1,0:T(8,128)(2,1)} %refs_1_.1, f32[1280]{0:T(1024)} %refs_2_.1, f32[1280]{0:T(1024)} %refs_3_.1), custom_call_target="tpu_custom_call" | custom-call | flops 1 | bytes 1 | tf_op jit(solution)/shard_map/load/pallas_call | solution.py:122
  11.7 0.1 collective-permute-start
  11.8 1.3 %collective-permute-done.other_squares = f32[192,128]{1,0:T(8,128)S(1)} collective-permute-done((f32[192,128]{1,0:T(8,128)S(1)}, f32[192,128]{1,0:T(8,128)S(1)}, u32[]{:S(2)}, u32[]{:S(2)}) %collective-permute-start) | collective-permute-done | bytes 98336 | tf_op jit(solution)/shard_map/ppermute | solution.py:22
  13.1 0.3 prepare.1
  13.4 2.1 %collective-permute-start.3 = (bf16[192,1280]{1,0:T(8,128)(2,1)S(1)}, bf16[192,1280]{1,0:T(8,128)(2,1)S(1)}, u32[]{:S(2)}, u32[]{:S(2)}) collective-permute-start(bf16[192,1280]{1,0:T(8,128)(2,1)S(1)} %get-tuple-element.37.own_keys), channel_id=1, source_target_pairs={{2,0},{0,2},{6,4},{4,6},{10,8},{8,10},{14,12},{12,14},{3,1},{1,3},... | collective-permute-start | bytes 1474568 | tf_op jit(solution)/shard_map/ppermute | solution.py:22
  15.5 0.4 collective-permute-start.2
  16.0 0.0 collective-permute-done.4.rows.far_values
  16.0 2.1 %collective-permute-start.9 = (bf16[96,1280]{1,0:T(8,128)(2,1)S(1)}, bf16[96,1280]{1,0:T(8,128)(2,1)S(1)}, u32[]{:S(2)}, u32[]{:S(2)}) collective-permute-start(bf16[96,1280]{1,0:T(8,128)(2,1)S(1)} %get-tuple-element.44), channel_id=1, source_target_pairs={{2,0},{0,2},{6,4},{4,6},{10,8},{8,10},{14,12},{12,14},{3,1},{1,3},... | collective-permute-start | bytes 737288 | tf_op jit(solution)/shard_map/ppermute | solution.py:22
  18.1 0.0 copy-start.1
  18.1 0.0 copy-start
  18.1 6.6 %collective-permute-done.5.near_values = bf16[192,1280]{1,0:T(8,128)(2,1)S(1)} collective-permute-done((bf16[192,1280]{1,0:T(8,128)(2,1)}, bf16[192,1280]{1,0:T(8,128)(2,1)S(1)}, u32[]{:S(2)}, u32[]{:S(2)}) %collective-permute-start.5) | collective-permute-done | bytes 491552 | tf_op jit(solution)/shard_map/ppermute | solution.py:22
  24.7 0.0 collective-permute-start.6
  24.7 5.6 %collective-permute-done.2.packed.far1_packed = bf16[208,1280]{1,0:T(8,128)(2,1)S(1)} collective-permute-done((bf16[208,1280]{1,0:T(8,128)(2,1)S(1)}, bf16[208,1280]{1,0:T(8,128)(2,1)S(1)}, u32[]{:S(2)}, u32[]{:S(2)}) %collective-permute-start.2) | collective-permute-done | bytes 532512 | tf_op jit(solution)/shard_map/ppermute | solution.py:22
  30.3 0.0 collective-permute-start.8
  30.3 0.0 collective-permute-done.6.refs_1_
  30.3 4.9 %collective-permute-done.3.near_keys = bf16[192,1280]{1,0:T(8,128)(2,1)S(1)} collective-permute-done((bf16[192,1280]{1,0:T(8,128)(2,1)S(1)}, bf16[192,1280]{1,0:T(8,128)(2,1)S(1)}, u32[]{:S(2)}, u32[]{:S(2)}) %collective-permute-start.3) | collective-permute-done | bytes 491552 | tf_op jit(solution)/shard_map/ppermute | solution.py:22
  35.2 0.0 collective-permute-start.7
  35.2 0.0 copy-done.1
  35.2 1.0 %collective-permute-start.11 = (bf16[192,1280]{1,0:T(8,128)(2,1)S(1)}, bf16[192,1280]{1,0:T(8,128)(2,1)S(1)}, u32[]{:S(2)}, u32[]{:S(2)}) collective-permute-start(bf16[192,1280]{1,0:T(8,128)(2,1)S(1)} %copy-done.1), channel_id=1, source_target_pairs={{12,0},{6,2},{0,4},{10,6},{4,8},{14,10},{8,12},{2,14},{13,1},{7,3}... | collective-permute-start | bytes 1474568 | tf_op jit(solution)/shard_map/ppermute | solution.py:22
  36.3 1.4 %collective-permute-start.10 = (bf16[96,1280]{1,0:T(8,128)(2,1)S(1)}, bf16[96,1280]{1,0:T(8,128)(2,1)S(1)}, u32[]{:S(2)}, u32[]{:S(2)}) collective-permute-start(bf16[96,1280]{1,0:T(8,128)(2,1)S(1)} %get-tuple-element.53), channel_id=1, source_target_pairs={{2,0},{0,2},{6,4},{4,6},{10,8},{8,10},{14,12},{12,14},{3,1},{1,3},... | collective-permute-start | bytes 737288 | tf_op jit(solution)/shard_map/ppermute | solution.py:22
  37.7 2.8 %collective-permute-done.9.first_half = bf16[96,1280]{1,0:T(8,128)(2,1)S(1)} collective-permute-done((bf16[96,1280]{1,0:T(8,128)(2,1)S(1)}, bf16[96,1280]{1,0:T(8,128)(2,1)S(1)}, u32[]{:S(2)}, u32[]{:S(2)}) %collective-permute-start.9) | collective-permute-done | bytes 245792 | tf_op jit(solution)/shard_map/ppermute | solution.py:22
  40.5 0.0 copy-done
  40.5 3.0 %attend_early.1 = (f32[10,192,128]{2,1,0:T(8,128)S(1)}, f32[10,192,128]{2,1,0:T(8,128)S(1)}, f32[192,1280]{1,0:T(8,128)S(1)}) custom-call(s32[1,4]{1,0:T(1,128)S(1)} %copy-done, bf16[192,1280]{1,0:T(8,128)(2,1)S(1)} %get-tuple-element.45.query_ref, bf16[192,1280]{1,0:T(8,128)(2,1)S(1)} %get-tuple-element.37.own_keys, ...), custom_call_target="tpu_custom_call" | custom-call | flops 5000000000 | bytes 1 | tf_op jit(solution)/shard_map/attend_early/pallas_call | solution.py:360
  43.4 7.6 %collective-permute-done.7.passed_keys = bf16[192,1280]{1,0:T(8,128)(2,1)S(1)} collective-permute-done((bf16[192,1280]{1,0:T(8,128)(2,1)S(1)}, bf16[192,1280]{1,0:T(8,128)(2,1)S(1)}, u32[]{:S(2)}, u32[]{:S(2)}) %collective-permute-start.7) | collective-permute-done | bytes 491552 | tf_op jit(solution)/shard_map/ppermute | solution.py:22
  51.0 0.0 collective-permute-done.8.far_packed
  51.0 3.8 %attend_late_keys.1 = (f32[10,192,128]{2,1,0:T(8,128)S(1)}, f32[192,1280]{1,0:T(8,128)S(1)}, bf16[10,192,384]{2,1,0:T(8,128)(2,1)S(1)}) custom-call(s32[1,4]{1,0:T(1,128)S(1)} %copy-done, bf16[192,1280]{1,0:T(8,128)(2,1)S(1)} %get-tuple-element.45.query_ref, bf16[192,1280]{1,0:T(8,128)(2,1)S(1)} %collective-permute-done.7.passed_keys, ...), custom_call_target="tpu_custom_call" | custom-call | flops 1 | bytes 1 | tf_op jit(solution)/shard_map/attend_late_keys/pallas_call | solution.py:386
  54.8 0.0 collective-permute-done.10.second_half
  54.8 0.3 collective-permute-done.11.far_values
  55.2 1.3 %attend_late_values.1 = bf16[192,1280]{1,0:T(8,128)(2,1)} custom-call(f32[10,192,128]{2,1,0:T(8,128)S(1)} %get-tuple-element.49.inverses_ref, f32[192,1280]{1,0:T(8,128)S(1)} %get-tuple-element.50.partial_ref, bf16[10,192,384]{2,1,0:T(8,128)(2,1)S(1)} %get-tuple-element.51.weights_ref, bf16[96,1280]{1,0:T(8,128)(2,1)S(1)} %collective-permute-done.9.first_half, ...), custom_call_target="tpu_custom_call" | custom-call | flops 1 | bytes 1 | tf_op jit(solution)/shard_map/attend_late_values/pallas_call | solution.py:409
  (4 shorter events, 0.1 us)
Async XLA Ops:
  0.0 16.0 %collective-permute-start.4 = (bf16[192,1280]{1,0:T(8,128)(2,1)}, bf16[192,1280]{1,0:T(8,128)(2,1)S(1)}, u32[]{:S(2)}, u32[]{:S(2)}) collective-permute-start(bf16[192,1280]{1,0:T(8,128)(2,1)} %own_values.1), channel_id=1, source_target_pairs={{4,0},{14,2},{8,4},{2,6},{12,8},{6,10},{0,12},{10,14},{5,1},{15,3}... | collective-permute-start | bytes 1474568 | tf_op jit(solution)/shard_map/ppermute | solution.py:22
  6.5 3.8 %collective-permute-start.1 = (bf16[4,2560]{1,0:T(4,128)(2,1)S(1)}, bf16[4,2560]{1,0:T(4,128)(2,1)S(1)}, u32[]{:S(2)}, u32[]{:S(2)}) collective-permute-start(bf16[4,2560]{1,0:T(4,128)(2,1)S(1)} %pack_rows.1.refs_0_), channel_id=1, source_target_pairs={{2,0},{0,2},{6,4},{4,6},{10,8},{8,10},{14,12},{12,14},{3,1},{1,3},... | collective-permute-start | bytes 61448 | tf_op jit(solution)/shard_map/ppermute | solution.py:22
  10.3 14.4 %collective-permute-start.5 = (bf16[192,1280]{1,0:T(8,128)(2,1)}, bf16[192,1280]{1,0:T(8,128)(2,1)S(1)}, u32[]{:S(2)}, u32[]{:S(2)}) collective-permute-start(bf16[192,1280]{1,0:T(8,128)(2,1)} %own_values.1), channel_id=1, source_target_pairs={{2,0},{0,2},{6,4},{4,6},{10,8},{8,10},{14,12},{12,14},{3,1},{1,3},... | collective-permute-start | bytes 1474568 | tf_op jit(solution)/shard_map/ppermute | solution.py:22
  11.7 1.4 %collective-permute-start = (f32[192,128]{1,0:T(8,128)S(1)}, f32[192,128]{1,0:T(8,128)S(1)}, u32[]{:S(2)}, u32[]{:S(2)}) collective-permute-start(f32[192,128]{1,0:T(8,128)S(1)} %get-tuple-element.34.squares), channel_id=1, source_target_pairs={{1,0},{0,1},{3,2},{2,3},{5,4},{4,5},{7,6},{6,7},{9,8},{8,9},{11,10... | collective-permute-start | bytes 294920 | tf_op jit(solution)/shard_map/ppermute | solution.py:22
  13.4 21.8 %collective-permute-start.3 = (bf16[192,1280]{1,0:T(8,128)(2,1)S(1)}, bf16[192,1280]{1,0:T(8,128)(2,1)S(1)}, u32[]{:S(2)}, u32[]{:S(2)}) collective-permute-start(bf16[192,1280]{1,0:T(8,128)(2,1)S(1)} %get-tuple-element.37.own_keys), channel_id=1, source_target_pairs={{2,0},{0,2},{6,4},{4,6},{10,8},{8,10},{14,12},{12,14},{3,1},{1,3},... | collective-permute-start | bytes 1474568 | tf_op jit(solution)/shard_map/ppermute | solution.py:22
  15.5 14.8 %collective-permute-start.2 = (bf16[208,1280]{1,0:T(8,128)(2,1)S(1)}, bf16[208,1280]{1,0:T(8,128)(2,1)S(1)}, u32[]{:S(2)}, u32[]{:S(2)}) collective-permute-start(bf16[208,1280]{1,0:T(8,128)(2,1)S(1)} %get-tuple-element.43), channel_id=1, source_target_pairs={{4,0},{14,2},{8,4},{2,6},{12,8},{6,10},{0,12},{10,14},{5,1},{15,3}... | collective-permute-start | bytes 1597448 | tf_op jit(solution)/shard_map/ppermute | solution.py:22
  16.0 24.5 %collective-permute-start.9 = (bf16[96,1280]{1,0:T(8,128)(2,1)S(1)}, bf16[96,1280]{1,0:T(8,128)(2,1)S(1)}, u32[]{:S(2)}, u32[]{:S(2)}) collective-permute-start(bf16[96,1280]{1,0:T(8,128)(2,1)S(1)} %get-tuple-element.44), channel_id=1, source_target_pairs={{2,0},{0,2},{6,4},{4,6},{10,8},{8,10},{14,12},{12,14},{3,1},{1,3},... | collective-permute-start | bytes 737288 | tf_op jit(solution)/shard_map/ppermute | solution.py:22
  18.1 17.1 %copy-start.1 = (bf16[192,1280]{1,0:T(8,128)(2,1)S(1)}, bf16[192,1280]{1,0:T(8,128)(2,1)}, u32[]{:S(2)}) copy-start(bf16[192,1280]{1,0:T(8,128)(2,1)} %own_values.1) | copy-start | bytes 1474564
  18.1 22.4 %copy-start = (s32[1,4]{1,0:T(1,128)S(1)}, s32[1,4]{1,0:T(1,128)}, u32[]{:S(2)}) copy-start(s32[1,4]{1,0:T(1,128)} %pattern_ref.3) | copy-start | bytes 52
  24.7 5.6 %collective-permute-start.6 = (bf16[8,2560]{1,0:T(8,128)(2,1)S(1)}, bf16[8,2560]{1,0:T(8,128)(2,1)S(1)}, u32[]{:S(2)}, u32[]{:S(2)}) collective-permute-start(bf16[8,2560]{1,0:T(8,128)(2,1)S(1)} %strip.5), channel_id=1, source_target_pairs={{8,0},{10,2},{12,4},{14,6},{0,8},{2,10},{4,12},{6,14},{9,1},{11,3}... | collective-permute-start | bytes 122888 | tf_op jit(solution)/shard_map/ppermute | solution.py:22
  30.3 20.7 %collective-permute-start.8 = (bf16[208,1280]{1,0:T(8,128)(2,1)S(1)}, bf16[208,1280]{1,0:T(8,128)(2,1)S(1)}, u32[]{:S(2)}, u32[]{:S(2)}) collective-permute-start(bf16[208,1280]{1,0:T(8,128)(2,1)S(1)} %get-tuple-element.43), channel_id=1, source_target_pairs={{12,0},{6,2},{0,4},{10,6},{4,8},{14,10},{8,12},{2,14},{13,1},{7,3}... | collective-permute-start | bytes 1597448 | tf_op jit(solution)/shard_map/ppermute | solution.py:22
  35.2 15.8 %collective-permute-start.7 = (bf16[192,1280]{1,0:T(8,128)(2,1)S(1)}, bf16[192,1280]{1,0:T(8,128)(2,1)S(1)}, u32[]{:S(2)}, u32[]{:S(2)}) collective-permute-start(bf16[192,1280]{1,0:T(8,128)(2,1)S(1)} %strip.3.far_keys), channel_id=1, source_target_pairs={{2,0},{0,2},{6,4},{4,6},{10,8},{8,10},{14,12},{12,14},{3,1},{1,3},... | collective-permute-start | bytes 1474568 | tf_op jit(solution)/shard_map/ppermute | solution.py:22
  35.2 19.9 %collective-permute-start.11 = (bf16[192,1280]{1,0:T(8,128)(2,1)S(1)}, bf16[192,1280]{1,0:T(8,128)(2,1)S(1)}, u32[]{:S(2)}, u32[]{:S(2)}) collective-permute-start(bf16[192,1280]{1,0:T(8,128)(2,1)S(1)} %copy-done.1), channel_id=1, source_target_pairs={{12,0},{6,2},{0,4},{10,6},{4,8},{14,10},{8,12},{2,14},{13,1},{7,3}... | collective-permute-start | bytes 1474568 | tf_op jit(solution)/shard_map/ppermute | solution.py:22
  36.3 18.6 %collective-permute-start.10 = (bf16[96,1280]{1,0:T(8,128)(2,1)S(1)}, bf16[96,1280]{1,0:T(8,128)(2,1)S(1)}, u32[]{:S(2)}, u32[]{:S(2)}) collective-permute-start(bf16[96,1280]{1,0:T(8,128)(2,1)S(1)} %get-tuple-element.53), channel_id=1, source_target_pairs={{2,0},{0,2},{6,4},{4,6},{10,8},{8,10},{14,12},{12,14},{3,1},{1,3},... | collective-permute-start | bytes 737288 | tf_op jit(solution)/shard_map/ppermute | solution.py:22

commit v6 on v5

--- a/solution.py
+++ b/solution.py
@@ -54,8 +54,7 @@
 CHEAP = pl.CostEstimate(flops=1, transcendentals=0, bytes_accessed=1)
 
 EARLY = pl.CostEstimate(flops=5*10**9, transcendentals=0, bytes_accessed=1)
-SMALL_HOLD = pl.CostEstimate(flops=2*10**9, transcendentals=0, bytes_accessed=1)
-HOLD = pl.CostEstimate(flops=3 * 10**10, transcendentals=0, bytes_accessed=1)
+HOLD = pl.CostEstimate(flops=8 * 10**9, transcendentals=0, bytes_accessed=1)
 
 
 def head_columns(head):
@@ -141,39 +140,50 @@
     return (rows * scale * gain_ref[...][None, :]).astype(jnp.bfloat16)
 
 
-def prepare_kernel(queries, keys, query_gain, key_gain, squares, other_squares, *refs):
-    *row_refs, query_ref, key_ref, packed_ref, pair_ref = refs
+def prepare_kernel(
+    queries, keys, query_gain, key_gain, squares, other_squares, query_ref, key_ref
+):
+    query_ref[...] = normalized(queries, query_gain, (squares, other_squares), 0)
+    key_ref[...] = normalized(keys, key_gain, (squares, other_squares), 1)
+
+
+def prepare(queries, keys, gains, squares):
+    return pl.pallas_call(
+        prepare_kernel,
+        out_shape=(pltpu.VMEM(keys.shape, jnp.bfloat16),) * 2,
+        in_specs=[VMEM] * 6,
+        out_specs=(VMEM,) * 2,
+        compiler_params=PARAMS,
+        cost_estimate=CHEAP,
+        name="prepare",
+    )(*map(in_vmem, (queries, keys, *gains, *squares)))
+
+
+def attach_kernel(keys_ref, own_rows, other_rows, packed_ref, pair_ref):
+    slots = own_rows.shape[0]
+    pair_ref[:slots] = own_rows[...]
+    pair_ref[slots:] = other_rows[...]
+    tokens, features = keys_ref.shape
+    packed_ref[:tokens] = keys_ref[...]
+    packed_ref[tokens : tokens + 2 * slots] = pair_ref[:, :features]
+    packed_ref[tokens + 2 * slots :] = pair_ref[:, features:]
+
+
+def attach_rows(keys, own_rows, other_rows):
     tokens, features = keys.shape
-    query_ref[...] = normalized(queries, query_gain, (squares, other_squares), 0)
-    normed_keys = normalized(keys, key_gain, (squares, other_squares), 1)
-    key_ref[...] = normed_keys
-    packed_ref[:tokens] = normed_keys
-    count = pair_ref.shape[0]
-    first = 0
-    for ref in row_refs:
-        pair_ref[first : first + ref.shape[0]] = ref[...]
-        first += ref.shape[0]
-    packed_ref[tokens : tokens + count] = pair_ref[:, :features]
-    packed_ref[tokens + count :] = pair_ref[:, features:]
-
-
-def prepare(queries, keys, gains, squares, rows):
-    tokens, features = keys.shape
-    count = sum(part.shape[0] for part in rows)
-    return pl.pallas_call(
-        prepare_kernel,
+    count = 2 * own_rows.shape[0]
+    return pl.pallas_call(
+        attach_kernel,
         out_shape=(
-            pltpu.VMEM((tokens, features), jnp.bfloat16),
-            pltpu.VMEM((tokens, features), jnp.bfloat16),
             pltpu.VMEM((tokens + 2 * count, features), jnp.bfloat16),
             pltpu.VMEM((count, 2 * features), jnp.bfloat16),
         ),
-        in_specs=[VMEM] * (6 + len(rows)),
-        out_specs=(VMEM,) * 4,
-        compiler_params=PARAMS,
-        cost_estimate=CHEAP,
-        name="prepare",
-    )(*map(in_vmem, (queries, keys, *gains, *squares, *rows)))
+        in_specs=[VMEM] * 3,
+        out_specs=(VMEM,) * 2,
+        compiler_params=PARAMS,
+        cost_estimate=CHEAP,
+        name="attach_rows",
+    )(*map(in_vmem, (keys, own_rows, other_rows)))
 
 
 def halve_kernel(rows, first_ref, second_ref):
@@ -276,7 +286,6 @@
     query_ref,
     passed_keys,
     far_packed,
-    far1_packed,
     old_peaks_ref,
     old_totals_ref,
     old_partial_ref,
@@ -294,12 +303,9 @@
         keys_ref[blocks + first : blocks + first + count] = ref[:, :features]
         values_ref[first : first + count] = ref[:, features:]
         first += count
-    for packed in (far_packed, far1_packed):
-        count = (packed.shape[0] - tokens) // 2
-        if count:
-            keys_ref[blocks + first : blocks + first + count] = packed[tokens : tokens + count]
-            values_ref[first : first + count] = packed[tokens + count :]
-            first += count
+    count = (far_packed.shape[0] - tokens) // 2
+    keys_ref[blocks + first :] = far_packed[tokens : tokens + count]
+    values_ref[first:] = far_packed[tokens + count :]
     marks = score(jnp.ones((8, LANES), jnp.bfloat16), keys_ref[blocks:, :LANES])
     bias = jnp.concatenate(
         [
@@ -376,13 +382,13 @@
     )(pattern, *map(in_vmem, (queries, *keys, *values)))
 
 
-def attend_late_keys(pattern, queries, passed_keys, far_packed, far1_packed, rows, state):
+def attend_late_keys(pattern, queries, passed_keys, far_packed, rows, state):
     tokens, features = queries.shape
     heads = features // HEAD_DIM
-    attached = (far_packed.shape[0] + far1_packed.shape[0]) // 2 - tokens
+    attached = (far_packed.shape[0] - tokens) // 2
     slots = attached + sum(part.shape[0] for part in rows)
     count = 2 * tokens + slots
-    operands = (queries, passed_keys, far_packed, far1_packed, *state, *rows)
+    operands = (queries, passed_keys, far_packed, *state, *rows)
     return pl.pallas_call(
         late_keys_kernel,
         out_shape=(
@@ -439,23 +445,19 @@
 ):
     tokens = queries.shape[0]
     far1_values = fetch(values, far_first)
-    rows = pack_rows(reference_live, reference_keys, reference_values)
-    rows = [rows, fetch(rows, beside)]
-    near_values = fetch(after(values, *rows), beside)
+    near_values = fetch(values, beside)
     *loaded, squares = load(queries, key_rows, (query_gain, key_gain))
     own_squares = (squares, fetch(squares, lambda i: i ^ 1, "tp"))
-    normed_queries, normed_keys, packed_keys, pair = prepare(
-        *loaded[:2], loaded[2:], own_squares, rows
-    )
+    normed_queries, normed_keys = prepare(*loaded[:2], loaded[2:], own_squares)
     near_keys = fetch(normed_keys, beside)
-    far1_packed = fetch(packed_keys, far_first)
-    held = strip(after(pair, far1_values), pair.shape[0], SMALL_HOLD)
-    held = strip(after(held, near_values), pair.shape[0], HOLD)
-    rows = [pair] + other_rows(held)
-
-    far1_keys = strip(far1_packed, tokens)
+    far1_keys = fetch(normed_keys, far_first)
+    own_rows = pack_rows(reference_live, reference_keys, reference_values)
+    packed_keys, pair = attach_rows(normed_keys, own_rows, fetch(own_rows, beside))
+    held = strip(after(pair, far1_values, near_values), pair.shape[0], HOLD)
+    rows = [pair, fetch(held, far_first)] + other_rows(held)
+
     passed_keys = fetch(after(far1_keys, near_keys, *rows), beside)
-    far2_packed = fetch(after(packed_keys, far1_packed), far_second)
+    far2_packed = fetch(after(packed_keys, far1_keys), far_second)
     far2_values = fetch(after(values, far1_keys), far_second)
     first_half, second_half = halve(far1_values)
     passed_first = fetch(first_half, beside)
@@ -468,7 +470,7 @@
         (values, near_values, far1_values),
     )
     inverses, partial, weights = attend_late_keys(
-        pattern, normed_queries, passed_keys, far2_packed, far1_packed, rows, state
+        pattern, normed_queries, passed_keys, far2_packed, rows, state
     )
     return attend_late_values(inverses, partial, weights, (passed_first, passed_second, far2_values))
 

time: 56.7 us -> 53.9 us (0.951)
  waiting for transfers between devices: 32.8 us -> 24.1 us
  starting transfers between devices: 12.3 us -> 18.2 us
    ppermute x12 -> x13, waiting for transfers between devices: 32.8 us -> 24.1 us  [fetch(): return lax.ppermute(block, axis, [(source_of(i) % n, i) for i in range(n)])]
    ppermute x12 -> x13, starting transfers between devices: 12.3 us -> 18.2 us  [fetch(): return lax.ppermute(block, axis, [(source_of(i) % n, i) for i in range(n)])]
  transfers between devices with their start and end apart: 12 -> 13, of which waited for: 8 -> 8; matrix products, arithmetic and copies ran while one was open for 0% -> 0% of each run, Pallas kernels for 17% -> 17%
where the time goes in v6:
time: 53.9 us; the launch traced here: 53.7 us
  waiting for transfers between devices  24.1 us (45%)
  starting transfers between devices  18.2 us (34%)
  Pallas kernels  10.6 us (20%)
  between operations  0.77 us (1%)
    ppermute x13, waiting for transfers between devices, fetch(): return lax.ppermute(block, axis, [(source_of(i) % n, i) for i in range(n)])  24.1 us
    ppermute x13, starting transfers between devices, fetch(): return lax.ppermute(block, axis, [(source_of(i) % n, i) for i in range(n)])  18.2 us
    pallas_call x1, Pallas kernels, attend_late_keys(): pl.pallas_call(late_keys_kernel, out_shape=(pltpu.VMEM((heads, tokens, LA...  3.82 us
    pallas_call x1, Pallas kernels, attend_early(): pl.pallas_call(early_kernel, out_shape=(pltpu.VMEM((heads, tokens, LANES)...  2.92 us
    pallas_call x1, Pallas kernels, load(): pl.pallas_call(load_kernel, out_shape=(*(pltpu.VMEM(operand.shape, operan...  1.42 us
    pallas_call x1, Pallas kernels, attend_late_values(): pl.pallas_call(late_values_kernel, out_shape=jax.ShapeDtypeStruct((tokens...  1.3 us
  transfers between devices with their start and end apart: 13, of which 8 were waited for; matrix products, arithmetic and copies ran while one was open for 0% of the time, Pallas kernels for 17%

profile of v6, /device:TPU:0, one launch (start us, length us, event | category | flops | bytes accessed | tf_op | source)
XLA Modules:
  0.0 53.7 jit_solution(10868178280558501268)
XLA Ops:
  0.0 5.0 %collective-permute-start.4 = (bf16[192,1280]{1,0:T(8,128)(2,1)}, bf16[192,1280]{1,0:T(8,128)(2,1)S(1)}, u32[]{:S(2)}, u32[]{:S(2)}) collective-permute-start(bf16[192,1280]{1,0:T(8,128)(2,1)} %own_values.1), channel_id=1, source_target_pairs={{4,0},{14,2},{8,4},{2,6},{12,8},{6,10},{0,12},{10,14},{5,1},{15,3}... | collective-permute-start | bytes 1474568 | tf_op jit(solution)/shard_map/ppermute | solution.py:22
  5.0 0.0 collective-permute-start.5
  5.1 1.4 %load.1 = (bf16[192,1280]{1,0:T(8,128)(2,1)S(1)}, bf16[192,1280]{1,0:T(8,128)(2,1)S(1)}, f32[1280]{0:T(1024)S(1)}, f32[1280]{0:T(1024)S(1)}, f32[192,128]{1,0:T(8,128)S(1)}) custom-call(bf16[192,1280]{1,0:T(8,128)(2,1)} %refs_0_.1, bf16[192,1280]{1,0:T(8,128)(2,1)} %refs_1_.1, f32[1280]{0:T(1024)} %refs_2_.1, f32[1280]{0:T(1024)} %refs_3_.1), custom_call_target="tpu_custom_call" | custom-call | flops 1 | bytes 1 | tf_op jit(solution)/shard_map/load/pallas_call | solution.py:121
  6.5 0.1 collective-permute-start
  7.2 0.7 %pack_rows.1.own_rows = bf16[4,2560]{1,0:T(4,128)(2,1)S(1)} custom-call(s32[1]{0:T(128)S(6)} %copy.10.live_ref, bf16[4,1280]{1,0:T(4,128)(2,1)} %keys_ref.1, bf16[4,1280]{1,0:T(4,128)(2,1)} %values_ref.1), custom_call_target="tpu_custom_call" | custom-call | flops 1 | bytes 1 | tf_op jit(solution)/shard_map/pack_rows/pallas_call | solution.py:87
  8.0 2.1 %collective-permute-start.3 = (bf16[4,2560]{1,0:T(4,128)(2,1)S(1)}, bf16[4,2560]{1,0:T(4,128)(2,1)S(1)}, u32[]{:S(2)}, u32[]{:S(2)}) collective-permute-start(bf16[4,2560]{1,0:T(4,128)(2,1)S(1)} %pack_rows.1.own_rows), channel_id=1, source_target_pairs={{2,0},{0,2},{6,4},{4,6},{10,8},{8,10},{14,12},{12,14},{3,1},{1,3},... | collective-permute-start | bytes 61448 | tf_op jit(solution)/shard_map/ppermute | solution.py:22
  10.1 0.0 collective-permute-done.other_squares
  10.1 0.3 prepare.1
  10.4 0.1 collective-permute-start.2
  10.4 1.7 %collective-permute-start.1 = (bf16[192,1280]{1,0:T(8,128)(2,1)S(1)}, bf16[192,1280]{1,0:T(8,128)(2,1)S(1)}, u32[]{:S(2)}, u32[]{:S(2)}) collective-permute-start(bf16[192,1280]{1,0:T(8,128)(2,1)S(1)} %get-tuple-element.34.keys_ref.own_keys), channel_id=1, source_target_pairs={{4,0},{14,2},{8,4},{2,6},{12,8},{6,10},{0,12},{10,14},{5,1},{15,3}... | collective-permute-start | bytes 1474568 | tf_op jit(solution)/shard_map/ppermute | solution.py:22
  12.1 7.7 %collective-permute-done.3.other_rows = bf16[4,2560]{1,0:T(4,128)(2,1)S(1)} collective-permute-done((bf16[4,2560]{1,0:T(4,128)(2,1)S(1)}, bf16[4,2560]{1,0:T(4,128)(2,1)S(1)}, u32[]{:S(2)}, u32[]{:S(2)}) %collective-permute-start.3) | collective-permute-done | bytes 20512 | tf_op jit(solution)/shard_map/ppermute | solution.py:22
  19.9 0.0 collective-permute-done.4.rows.far_values
  19.9 0.1 collective-permute-start.10
  20.0 0.0 collective-permute-done.5.near_values
  20.0 0.0 copy-start.1
  20.0 0.0 copy-start
  20.1 2.1 %collective-permute-start.7 = (bf16[8,2560]{1,0:T(8,128)(2,1)S(1)}, bf16[8,2560]{1,0:T(8,128)(2,1)S(1)}, u32[]{:S(2)}, u32[]{:S(2)}) collective-permute-start(bf16[8,2560]{1,0:T(8,128)(2,1)S(1)} %strip.1), channel_id=1, source_target_pairs={{8,0},{10,2},{12,4},{14,6},{0,8},{2,10},{4,12},{6,14},{9,1},{11,3}... | collective-permute-start | bytes 122888 | tf_op jit(solution)/shard_map/ppermute | solution.py:22
  22.1 1.3 %collective-permute-start.6 = (bf16[8,2560]{1,0:T(8,128)(2,1)S(1)}, bf16[8,2560]{1,0:T(8,128)(2,1)S(1)}, u32[]{:S(2)}, u32[]{:S(2)}) collective-permute-start(bf16[8,2560]{1,0:T(8,128)(2,1)S(1)} %strip.1), channel_id=1, source_target_pairs={{4,0},{14,2},{8,4},{2,6},{12,8},{6,10},{0,12},{10,14},{5,1},{15,3}... | collective-permute-start | bytes 122888 | tf_op jit(solution)/shard_map/ppermute | solution.py:22
  23.5 4.0 %collective-permute-done.1.far_keys = bf16[192,1280]{1,0:T(8,128)(2,1)S(1)} collective-permute-done((bf16[192,1280]{1,0:T(8,128)(2,1)S(1)}, bf16[192,1280]{1,0:T(8,128)(2,1)S(1)}, u32[]{:S(2)}, u32[]{:S(2)}) %collective-permute-start.1) | collective-permute-done | bytes 491552 | tf_op jit(solution)/shard_map/ppermute | solution.py:22
  27.5 0.6 %collective-permute-start.9 = (bf16[208,1280]{1,0:T(8,128)(2,1)S(1)}, bf16[208,1280]{1,0:T(8,128)(2,1)S(1)}, u32[]{:S(2)}, u32[]{:S(2)}) collective-permute-start(bf16[208,1280]{1,0:T(8,128)(2,1)S(1)} %get-tuple-element.39), channel_id=1, source_target_pairs={{12,0},{6,2},{0,4},{10,6},{4,8},{14,10},{8,12},{2,14},{13,1},{7,3}... | collective-permute-start | bytes 1597448 | tf_op jit(solution)/shard_map/ppermute | solution.py:22
  28.0 0.3 collective-permute-done.7.refs_2_
  28.3 0.9 %collective-permute-done.6.refs_1_ = bf16[8,2560]{1,0:T(8,128)(2,1)S(1)} collective-permute-done((bf16[8,2560]{1,0:T(8,128)(2,1)S(1)}, bf16[8,2560]{1,0:T(8,128)(2,1)S(1)}, u32[]{:S(2)}, u32[]{:S(2)}) %collective-permute-start.6) | collective-permute-done | bytes 40992 | tf_op jit(solution)/shard_map/ppermute | solution.py:22
  29.2 1.2 %collective-permute-done.2.near_keys = bf16[192,1280]{1,0:T(8,128)(2,1)S(1)} collective-permute-done((bf16[192,1280]{1,0:T(8,128)(2,1)S(1)}, bf16[192,1280]{1,0:T(8,128)(2,1)S(1)}, u32[]{:S(2)}, u32[]{:S(2)}) %collective-permute-start.2) | collective-permute-done | bytes 491552 | tf_op jit(solution)/shard_map/ppermute | solution.py:22
  30.4 0.9 %collective-permute-start.8 = (bf16[192,1280]{1,0:T(8,128)(2,1)S(1)}, bf16[192,1280]{1,0:T(8,128)(2,1)S(1)}, u32[]{:S(2)}, u32[]{:S(2)}) collective-permute-start(bf16[192,1280]{1,0:T(8,128)(2,1)S(1)} %collective-permute-done.1.far_keys), channel_id=1, source_target_pairs={{2,0},{0,2},{6,4},{4,6},{10,8},{8,10},{14,12},{12,14},{3,1},{1,3},... | collective-permute-start | bytes 1474568 | tf_op jit(solution)/shard_map/ppermute | solution.py:22
  31.3 0.0 copy-done.1
  31.3 0.3 collective-permute-start.12
  31.6 3.9 %collective-permute-start.11 = (bf16[96,1280]{1,0:T(8,128)(2,1)S(1)}, bf16[96,1280]{1,0:T(8,128)(2,1)S(1)}, u32[]{:S(2)}, u32[]{:S(2)}) collective-permute-start(bf16[96,1280]{1,0:T(8,128)(2,1)S(1)} %get-tuple-element.49), channel_id=1, source_target_pairs={{2,0},{0,2},{6,4},{4,6},{10,8},{8,10},{14,12},{12,14},{3,1},{1,3},... | collective-permute-start | bytes 737288 | tf_op jit(solution)/shard_map/ppermute | solution.py:22
  35.5 0.1 collective-permute-done.10.first_half
  35.6 0.0 copy-done
  35.6 2.9 %attend_early.1 = (f32[10,192,128]{2,1,0:T(8,128)S(1)}, f32[10,192,128]{2,1,0:T(8,128)S(1)}, f32[192,1280]{1,0:T(8,128)S(1)}) custom-call(s32[1,4]{1,0:T(1,128)S(1)} %copy-done, bf16[192,1280]{1,0:T(8,128)(2,1)S(1)} %get-tuple-element.41.query_ref, bf16[192,1280]{1,0:T(8,128)(2,1)S(1)} %get-tuple-element.34.keys_ref.own_keys, ...), custom_call_target="tpu_custom_call" | custom-call | flops 5000000000 | bytes 1 | tf_op jit(solution)/shard_map/attend_early/pallas_call | solution.py:366
  38.6 7.6 %collective-permute-done.8.passed_keys = bf16[192,1280]{1,0:T(8,128)(2,1)S(1)} collective-permute-done((bf16[192,1280]{1,0:T(8,128)(2,1)S(1)}, bf16[192,1280]{1,0:T(8,128)(2,1)S(1)}, u32[]{:S(2)}, u32[]{:S(2)}) %collective-permute-start.8) | collective-permute-done | bytes 491552 | tf_op jit(solution)/shard_map/ppermute | solution.py:22
  46.2 0.0 collective-permute-done.9.far_packed
  46.2 3.8 %attend_late_keys.1 = (f32[10,192,128]{2,1,0:T(8,128)S(1)}, f32[192,1280]{1,0:T(8,128)S(1)}, bf16[10,192,384]{2,1,0:T(8,128)(2,1)S(1)}) custom-call(s32[1,4]{1,0:T(1,128)S(1)} %copy-done, bf16[192,1280]{1,0:T(8,128)(2,1)S(1)} %get-tuple-element.41.query_ref, bf16[192,1280]{1,0:T(8,128)(2,1)S(1)} %collective-permute-done.8.passed_keys, ...), custom_call_target="tpu_custom_call" | custom-call | flops 1 | bytes 1 | tf_op jit(solution)/shard_map/attend_late_keys/pallas_call | solution.py:392
  50.0 0.0 collective-permute-done.11.second_half
  50.0 2.3 %collective-permute-done.12.far_values = bf16[192,1280]{1,0:T(8,128)(2,1)S(1)} collective-permute-done((bf16[192,1280]{1,0:T(8,128)(2,1)S(1)}, bf16[192,1280]{1,0:T(8,128)(2,1)S(1)}, u32[]{:S(2)}, u32[]{:S(2)}) %collective-permute-start.12) | collective-permute-done | bytes 491552 | tf_op jit(solution)/shard_map/ppermute | solution.py:22
  52.4 1.3 %attend_late_values.1 = bf16[192,1280]{1,0:T(8,128)(2,1)} custom-call(f32[10,192,128]{2,1,0:T(8,128)S(1)} %get-tuple-element.45.inverses_ref, f32[192,1280]{1,0:T(8,128)S(1)} %get-tuple-element.46.partial_ref, bf16[10,192,384]{2,1,0:T(8,128)(2,1)S(1)} %get-tuple-element.47.weights_ref, bf16[96,1280]{1,0:T(8,128)(2,1)S(1)} %collective-permute-done.10.first_half, ...), custom_call_target="tpu_custom_call" | custom-call | flops 1 | bytes 1 | tf_op jit(solution)/shard_map/attend_late_values/pallas_call | solution.py:415
  (3 shorter events, 0.1 us)
Async XLA Ops:
  0.0 19.9 %collective-permute-start.4 = (bf16[192,1280]{1,0:T(8,128)(2,1)}, bf16[192,1280]{1,0:T(8,128)(2,1)S(1)}, u32[]{:S(2)}, u32[]{:S(2)}) collective-permute-start(bf16[192,1280]{1,0:T(8,128)(2,1)} %own_values.1), channel_id=1, source_target_pairs={{4,0},{14,2},{8,4},{2,6},{12,8},{6,10},{0,12},{10,14},{5,1},{15,3}... | collective-permute-start | bytes 1474568 | tf_op jit(solution)/shard_map/ppermute | solution.py:22
  5.0 15.0 %collective-permute-start.5 = (bf16[192,1280]{1,0:T(8,128)(2,1)}, bf16[192,1280]{1,0:T(8,128)(2,1)S(1)}, u32[]{:S(2)}, u32[]{:S(2)}) collective-permute-start(bf16[192,1280]{1,0:T(8,128)(2,1)} %own_values.1), channel_id=1, source_target_pairs={{2,0},{0,2},{6,4},{4,6},{10,8},{8,10},{14,12},{12,14},{3,1},{1,3},... | collective-permute-start | bytes 1474568 | tf_op jit(solution)/shard_map/ppermute | solution.py:22
  6.5 3.6 %collective-permute-start = (f32[192,128]{1,0:T(8,128)S(1)}, f32[192,128]{1,0:T(8,128)S(1)}, u32[]{:S(2)}, u32[]{:S(2)}) collective-permute-start(f32[192,128]{1,0:T(8,128)S(1)} %get-tuple-element.32.squares), channel_id=1, source_target_pairs={{1,0},{0,1},{3,2},{2,3},{5,4},{4,5},{7,6},{6,7},{9,8},{8,9},{11,10... | collective-permute-start | bytes 294920 | tf_op jit(solution)/shard_map/ppermute | solution.py:22
  8.0 11.9 %collective-permute-start.3 = (bf16[4,2560]{1,0:T(4,128)(2,1)S(1)}, bf16[4,2560]{1,0:T(4,128)(2,1)S(1)}, u32[]{:S(2)}, u32[]{:S(2)}) collective-permute-start(bf16[4,2560]{1,0:T(4,128)(2,1)S(1)} %pack_rows.1.own_rows), channel_id=1, source_target_pairs={{2,0},{0,2},{6,4},{4,6},{10,8},{8,10},{14,12},{12,14},{3,1},{1,3},... | collective-permute-start | bytes 61448 | tf_op jit(solution)/shard_map/ppermute | solution.py:22
  10.4 20.0 %collective-permute-start.2 = (bf16[192,1280]{1,0:T(8,128)(2,1)S(1)}, bf16[192,1280]{1,0:T(8,128)(2,1)S(1)}, u32[]{:S(2)}, u32[]{:S(2)}) collective-permute-start(bf16[192,1280]{1,0:T(8,128)(2,1)S(1)} %get-tuple-element.34.keys_ref.own_keys), channel_id=1, source_target_pairs={{2,0},{0,2},{6,4},{4,6},{10,8},{8,10},{14,12},{12,14},{3,1},{1,3},... | collective-permute-start | bytes 1474568 | tf_op jit(solution)/shard_map/ppermute | solution.py:22
  10.4 17.0 %collective-permute-start.1 = (bf16[192,1280]{1,0:T(8,128)(2,1)S(1)}, bf16[192,1280]{1,0:T(8,128)(2,1)S(1)}, u32[]{:S(2)}, u32[]{:S(2)}) collective-permute-start(bf16[192,1280]{1,0:T(8,128)(2,1)S(1)} %get-tuple-element.34.keys_ref.own_keys), channel_id=1, source_target_pairs={{4,0},{14,2},{8,4},{2,6},{12,8},{6,10},{0,12},{10,14},{5,1},{15,3}... | collective-permute-start | bytes 1474568 | tf_op jit(solution)/shard_map/ppermute | solution.py:22
  19.9 15.7 %collective-permute-start.10 = (bf16[96,1280]{1,0:T(8,128)(2,1)S(1)}, bf16[96,1280]{1,0:T(8,128)(2,1)S(1)}, u32[]{:S(2)}, u32[]{:S(2)}) collective-permute-start(bf16[96,1280]{1,0:T(8,128)(2,1)S(1)} %get-tuple-element.40), channel_id=1, source_target_pairs={{2,0},{0,2},{6,4},{4,6},{10,8},{8,10},{14,12},{12,14},{3,1},{1,3},... | collective-permute-start | bytes 737288 | tf_op jit(solution)/shard_map/ppermute | solution.py:22
  20.0 11.2 %copy-start.1 = (bf16[192,1280]{1,0:T(8,128)(2,1)S(1)}, bf16[192,1280]{1,0:T(8,128)(2,1)}, u32[]{:S(2)}) copy-start(bf16[192,1280]{1,0:T(8,128)(2,1)} %own_values.1) | copy-start | bytes 1474564
  20.0 15.6 %copy-start = (s32[1,4]{1,0:T(1,128)S(1)}, s32[1,4]{1,0:T(1,128)}, u32[]{:S(2)}) copy-start(s32[1,4]{1,0:T(1,128)} %pattern_ref.3) | copy-start | bytes 52
  20.1 8.3 %collective-permute-start.7 = (bf16[8,2560]{1,0:T(8,128)(2,1)S(1)}, bf16[8,2560]{1,0:T(8,128)(2,1)S(1)}, u32[]{:S(2)}, u32[]{:S(2)}) collective-permute-start(bf16[8,2560]{1,0:T(8,128)(2,1)S(1)} %strip.1), channel_id=1, source_target_pairs={{8,0},{10,2},{12,4},{14,6},{0,8},{2,10},{4,12},{6,14},{9,1},{11,3}... | collective-permute-start | bytes 122888 | tf_op jit(solution)/shard_map/ppermute | solution.py:22
  22.1 7.1 %collective-permute-start.6 = (bf16[8,2560]{1,0:T(8,128)(2,1)S(1)}, bf16[8,2560]{1,0:T(8,128)(2,1)S(1)}, u32[]{:S(2)}, u32[]{:S(2)}) collective-permute-start(bf16[8,2560]{1,0:T(8,128)(2,1)S(1)} %strip.1), channel_id=1, source_target_pairs={{4,0},{14,2},{8,4},{2,6},{12,8},{6,10},{0,12},{10,14},{5,1},{15,3}... | collective-permute-start | bytes 122888 | tf_op jit(solution)/shard_map/ppermute | solution.py:22
  27.5 18.7 %collective-permute-start.9 = (bf16[208,1280]{1,0:T(8,128)(2,1)S(1)}, bf16[208,1280]{1,0:T(8,128)(2,1)S(1)}, u32[]{:S(2)}, u32[]{:S(2)}) collective-permute-start(bf16[208,1280]{1,0:T(8,128)(2,1)S(1)} %get-tuple-element.39), channel_id=1, source_target_pairs={{12,0},{6,2},{0,4},{10,6},{4,8},{14,10},{8,12},{2,14},{13,1},{7,3}... | collective-permute-start | bytes 1597448 | tf_op jit(solution)/shard_map/ppermute | solution.py:22
  30.4 15.8 %collective-permute-start.8 = (bf16[192,1280]{1,0:T(8,128)(2,1)S(1)}, bf16[192,1280]{1,0:T(8,128)(2,1)S(1)}, u32[]{:S(2)}, u32[]{:S(2)}) collective-permute-start(bf16[192,1280]{1,0:T(8,128)(2,1)S(1)} %collective-permute-done.1.far_keys), channel_id=1, source_target_pairs={{2,0},{0,2},{6,4},{4,6},{10,8},{8,10},{14,12},{12,14},{3,1},{1,3},... | collective-permute-start | bytes 1474568 | tf_op jit(solution)/shard_map/ppermute | solution.py:22
  31.3 21.1 %collective-permute-start.12 = (bf16[192,1280]{1,0:T(8,128)(2,1)S(1)}, bf16[192,1280]{1,0:T(8,128)(2,1)S(1)}, u32[]{:S(2)}, u32[]{:S(2)}) collective-permute-start(bf16[192,1280]{1,0:T(8,128)(2,1)S(1)} %copy-done.1), channel_id=1, source_target_pairs={{12,0},{6,2},{0,4},{10,6},{4,8},{14,10},{8,12},{2,14},{13,1},{7,3}... | collective-permute-start | bytes 1474568 | tf_op jit(solution)/shard_map/ppermute | solution.py:22
  31.6 18.4 %collective-permute-start.11 = (bf16[96,1280]{1,0:T(8,128)(2,1)S(1)}, bf16[96,1280]{1,0:T(8,128)(2,1)S(1)}, u32[]{:S(2)}, u32[]{:S(2)}) collective-permute-start(bf16[96,1280]{1,0:T(8,128)(2,1)S(1)} %get-tuple-element.49), channel_id=1, source_target_pairs={{2,0},{0,2},{6,4},{4,6},{10,8},{8,10},{14,12},{12,14},{3,1},{1,3},... | collective-permute-start | bytes 737288 | tf_op jit(solution)/shard_map/ppermute | solution.py:22

commit v7 on v6

--- a/solution.py
+++ b/solution.py
@@ -336,17 +336,31 @@
         partial_ref[:, columns] = (old_partial_ref[:, columns] * fading + product) * inverse
 
 
+def passed_values_kernel(
+    inverses_ref, old_partial_ref, weights_ref, first_half, second_half, partial_ref
+):
+    heads, tokens = weights_ref.shape[:2]
+    for head in range(heads):
+        columns = head_columns(head)
+        values = jnp.concatenate([first_half[:, columns], second_half[:, columns]], axis=0)
+        product = jnp.dot(
+            weights_ref[head, :, :tokens], values, preferred_element_type=jnp.float32
+        )
+        partial_ref[:, columns] = old_partial_ref[:, columns] + product * inverses_ref[head]
+
+
 def late_values_kernel(
-    inverses_ref, partial_ref, weights_ref, first_half, second_half, far_values, out_ref, out_vmem, sems
+    inverses_ref, partial_ref, weights_ref, far_values, out_ref, out_vmem, sems
 ):
-    heads = weights_ref.shape[0]
+    heads, tokens = weights_ref.shape[:2]
     copies = []
     for head in range(heads):
         columns = head_columns(head)
-        values = jnp.concatenate(
-            [ref[:, columns] for ref in (first_half, second_half, far_values)], axis=0
+        product = jnp.dot(
+            weights_ref[head, :, tokens:],
+            far_values[:, columns],
+            preferred_element_type=jnp.float32,
         )
-        product = jnp.dot(weights_ref[head], values, preferred_element_type=jnp.float32)
         out_vmem[:, columns] = (
             partial_ref[:, columns] + product * inverses_ref[head]
         ).astype(jnp.bfloat16)
@@ -409,13 +423,25 @@
     )(pattern, *map(in_vmem, operands))
 
 
-def attend_late_values(inverses, partial, weights, values):
+def attend_passed_values(inverses, partial, weights, halves):
+    return pl.pallas_call(
+        passed_values_kernel,
+        out_shape=pltpu.VMEM(partial.shape, jnp.float32),
+        in_specs=[VMEM] * 5,
+        out_specs=VMEM,
+        compiler_params=PARAMS,
+        cost_estimate=CHEAP,
+        name="attend_passed_values",
+    )(*map(in_vmem, (inverses, partial, weights, *halves)))
+
+
+def attend_late_values(inverses, partial, weights, far_values):
     tokens, features = partial.shape
     heads = features // HEAD_DIM
     return pl.pallas_call(
         late_values_kernel,
         out_shape=jax.ShapeDtypeStruct((tokens, features), jnp.bfloat16),
-        in_specs=[VMEM] * 6,
+        in_specs=[VMEM] * 4,
         out_specs=pl.BlockSpec(memory_space=pl.ANY),
         scratch_shapes=[
             pltpu.VMEM((tokens, features), jnp.bfloat16),
@@ -424,7 +450,7 @@
         compiler_params=PARAMS,
         cost_estimate=CHEAP,
         name="attend_late_values",
-    )(*map(in_vmem, (inverses, partial, weights, *values)))
+    )(*map(in_vmem, (inverses, partial, weights, far_values)))
 
 
 def other_rows(pair):
@@ -472,7 +498,10 @@
     inverses, partial, weights = attend_late_keys(
         pattern, normed_queries, passed_keys, far2_packed, rows, state
     )
-    return attend_late_values(inverses, partial, weights, (passed_first, passed_second, far2_values))
+    partial = attend_passed_values(
+        inverses, partial, weights, (passed_first, passed_second)
+    )
+    return attend_late_values(inverses, partial, weights, far2_values)
 
 
 def solution(mesh):

time: 53.9 us -> 53.9 us (level)
  transfers between devices with their start and end apart: 13 -> 13, of which waited for: 8 -> 8; matrix products, arithmetic and copies ran while one was open for 0% -> 0% of each run, Pallas kernels for 17% -> 18%
where the time goes in v7:
time: 53.9 us; the launch traced here: 53.6 us
  waiting for transfers between devices  23.6 us (44%)
  starting transfers between devices  18.2 us (34%)
  Pallas kernels  11 us (20%)
  between operations  0.78 us (1%)
    ppermute x13, waiting for transfers between devices, fetch(): return lax.ppermute(block, axis, [(source_of(i) % n, i) for i in range(n)])  23.6 us
    ppermute x13, starting transfers between devices, fetch(): return lax.ppermute(block, axis, [(source_of(i) % n, i) for i in range(n)])  18.2 us
    pallas_call x1, Pallas kernels, attend_late_keys(): pl.pallas_call(late_keys_kernel, out_shape=(pltpu.VMEM((heads, tokens, LA...  3.81 us
    pallas_call x1, Pallas kernels, attend_early(): pl.pallas_call(early_kernel, out_shape=(pltpu.VMEM((heads, tokens, LANES)...  2.94 us
    pallas_call x1, Pallas kernels, load(): pl.pallas_call(load_kernel, out_shape=(*(pltpu.VMEM(operand.shape, operan...  1.42 us
    pallas_call x1, Pallas kernels, attend_late_values(): pl.pallas_call(late_values_kernel, out_shape=jax.ShapeDtypeStruct((tokens...  1.25 us
  transfers between devices with their start and end apart: 13, of which 8 were waited for; matrix products, arithmetic and copies ran while one was open for 0% of the time, Pallas kernels for 18%

profile of v7, /device:TPU:0, one launch (start us, length us, event | category | flops | bytes accessed | tf_op | source)
XLA Modules:
  0.0 53.6 jit_solution(367079933088590664)
XLA Ops:
  0.0 5.0 %collective-permute-start.4 = (bf16[192,1280]{1,0:T(8,128)(2,1)}, bf16[192,1280]{1,0:T(8,128)(2,1)S(1)}, u32[]{:S(2)}, u32[]{:S(2)}) collective-permute-start(bf16[192,1280]{1,0:T(8,128)(2,1)} %own_values.1), channel_id=1, source_target_pairs={{4,0},{14,2},{8,4},{2,6},{12,8},{6,10},{0,12},{10,14},{5,1},{15,3}... | collective-permute-start | bytes 1474568 | tf_op jit(solution)/shard_map/ppermute | solution.py:22
  5.0 0.0 collective-permute-start.5
  5.1 1.4 %load.1 = (bf16[192,1280]{1,0:T(8,128)(2,1)S(1)}, bf16[192,1280]{1,0:T(8,128)(2,1)S(1)}, f32[1280]{0:T(1024)S(1)}, f32[1280]{0:T(1024)S(1)}, f32[192,128]{1,0:T(8,128)S(1)}) custom-call(bf16[192,1280]{1,0:T(8,128)(2,1)} %refs_0_.1, bf16[192,1280]{1,0:T(8,128)(2,1)} %refs_1_.1, f32[1280]{0:T(1024)} %refs_2_.1, f32[1280]{0:T(1024)} %refs_3_.1), custom_call_target="tpu_custom_call" | custom-call | flops 1 | bytes 1 | tf_op jit(solution)/shard_map/load/pallas_call | solution.py:121
  6.5 0.1 collective-permute-start
  7.2 0.7 %pack_rows.1.own_rows = bf16[4,2560]{1,0:T(4,128)(2,1)S(1)} custom-call(s32[1]{0:T(128)S(6)} %copy.10.live_ref, bf16[4,1280]{1,0:T(4,128)(2,1)} %keys_ref.1, bf16[4,1280]{1,0:T(4,128)(2,1)} %values_ref.1), custom_call_target="tpu_custom_call" | custom-call | flops 1 | bytes 1 | tf_op jit(solution)/shard_map/pack_rows/pallas_call | solution.py:87
  8.0 2.1 %collective-permute-start.3 = (bf16[4,2560]{1,0:T(4,128)(2,1)S(1)}, bf16[4,2560]{1,0:T(4,128)(2,1)S(1)}, u32[]{:S(2)}, u32[]{:S(2)}) collective-permute-start(bf16[4,2560]{1,0:T(4,128)(2,1)S(1)} %pack_rows.1.own_rows), channel_id=1, source_target_pairs={{2,0},{0,2},{6,4},{4,6},{10,8},{8,10},{14,12},{12,14},{3,1},{1,3},... | collective-permute-start | bytes 61448 | tf_op jit(solution)/shard_map/ppermute | solution.py:22
  10.1 0.0 collective-permute-done.other_squares
  10.1 0.3 prepare.1
  10.4 0.1 collective-permute-start.2
  10.4 1.7 %collective-permute-start.1 = (bf16[192,1280]{1,0:T(8,128)(2,1)S(1)}, bf16[192,1280]{1,0:T(8,128)(2,1)S(1)}, u32[]{:S(2)}, u32[]{:S(2)}) collective-permute-start(bf16[192,1280]{1,0:T(8,128)(2,1)S(1)} %get-tuple-element.34.keys_ref.own_keys), channel_id=1, source_target_pairs={{4,0},{14,2},{8,4},{2,6},{12,8},{6,10},{0,12},{10,14},{5,1},{15,3}... | collective-permute-start | bytes 1474568 | tf_op jit(solution)/shard_map/ppermute | solution.py:22
  12.1 7.7 %collective-permute-done.3.other_rows = bf16[4,2560]{1,0:T(4,128)(2,1)S(1)} collective-permute-done((bf16[4,2560]{1,0:T(4,128)(2,1)S(1)}, bf16[4,2560]{1,0:T(4,128)(2,1)S(1)}, u32[]{:S(2)}, u32[]{:S(2)}) %collective-permute-start.3) | collective-permute-done | bytes 20512 | tf_op jit(solution)/shard_map/ppermute | solution.py:22
  19.9 0.0 collective-permute-done.4.rows.far_values
  19.9 0.1 collective-permute-start.10
  20.0 0.0 collective-permute-done.5.near_values
  20.0 0.0 copy-start.1
  20.0 0.0 copy-start
  20.1 2.1 %collective-permute-start.7 = (bf16[8,2560]{1,0:T(8,128)(2,1)S(1)}, bf16[8,2560]{1,0:T(8,128)(2,1)S(1)}, u32[]{:S(2)}, u32[]{:S(2)}) collective-permute-start(bf16[8,2560]{1,0:T(8,128)(2,1)S(1)} %strip.1), channel_id=1, source_target_pairs={{8,0},{10,2},{12,4},{14,6},{0,8},{2,10},{4,12},{6,14},{9,1},{11,3}... | collective-permute-start | bytes 122888 | tf_op jit(solution)/shard_map/ppermute | solution.py:22
  22.1 1.3 %collective-permute-start.6 = (bf16[8,2560]{1,0:T(8,128)(2,1)S(1)}, bf16[8,2560]{1,0:T(8,128)(2,1)S(1)}, u32[]{:S(2)}, u32[]{:S(2)}) collective-permute-start(bf16[8,2560]{1,0:T(8,128)(2,1)S(1)} %strip.1), channel_id=1, source_target_pairs={{4,0},{14,2},{8,4},{2,6},{12,8},{6,10},{0,12},{10,14},{5,1},{15,3}... | collective-permute-start | bytes 122888 | tf_op jit(solution)/shard_map/ppermute | solution.py:22
  23.5 4.0 %collective-permute-done.1.far_keys = bf16[192,1280]{1,0:T(8,128)(2,1)S(1)} collective-permute-done((bf16[192,1280]{1,0:T(8,128)(2,1)S(1)}, bf16[192,1280]{1,0:T(8,128)(2,1)S(1)}, u32[]{:S(2)}, u32[]{:S(2)}) %collective-permute-start.1) | collective-permute-done | bytes 491552 | tf_op jit(solution)/shard_map/ppermute | solution.py:22
  27.5 0.6 %collective-permute-start.9 = (bf16[208,1280]{1,0:T(8,128)(2,1)S(1)}, bf16[208,1280]{1,0:T(8,128)(2,1)S(1)}, u32[]{:S(2)}, u32[]{:S(2)}) collective-permute-start(bf16[208,1280]{1,0:T(8,128)(2,1)S(1)} %get-tuple-element.39), channel_id=1, source_target_pairs={{12,0},{6,2},{0,4},{10,6},{4,8},{14,10},{8,12},{2,14},{13,1},{7,3}... | collective-permute-start | bytes 1597448 | tf_op jit(solution)/shard_map/ppermute | solution.py:22
  28.0 0.3 collective-permute-done.7.refs_2_
  28.3 0.9 %collective-permute-done.6.refs_1_ = bf16[8,2560]{1,0:T(8,128)(2,1)S(1)} collective-permute-done((bf16[8,2560]{1,0:T(8,128)(2,1)S(1)}, bf16[8,2560]{1,0:T(8,128)(2,1)S(1)}, u32[]{:S(2)}, u32[]{:S(2)}) %collective-permute-start.6) | collective-permute-done | bytes 40992 | tf_op jit(solution)/shard_map/ppermute | solution.py:22
  29.2 1.2 %collective-permute-done.2.near_keys = bf16[192,1280]{1,0:T(8,128)(2,1)S(1)} collective-permute-done((bf16[192,1280]{1,0:T(8,128)(2,1)S(1)}, bf16[192,1280]{1,0:T(8,128)(2,1)S(1)}, u32[]{:S(2)}, u32[]{:S(2)}) %collective-permute-start.2) | collective-permute-done | bytes 491552 | tf_op jit(solution)/shard_map/ppermute | solution.py:22
  30.4 0.9 %collective-permute-start.8 = (bf16[192,1280]{1,0:T(8,128)(2,1)S(1)}, bf16[192,1280]{1,0:T(8,128)(2,1)S(1)}, u32[]{:S(2)}, u32[]{:S(2)}) collective-permute-start(bf16[192,1280]{1,0:T(8,128)(2,1)S(1)} %collective-permute-done.1.far_keys), channel_id=1, source_target_pairs={{2,0},{0,2},{6,4},{4,6},{10,8},{8,10},{14,12},{12,14},{3,1},{1,3},... | collective-permute-start | bytes 1474568 | tf_op jit(solution)/shard_map/ppermute | solution.py:22
  31.3 0.0 copy-done.1
  31.3 0.3 collective-permute-start.12
  31.6 3.9 %collective-permute-start.11 = (bf16[96,1280]{1,0:T(8,128)(2,1)S(1)}, bf16[96,1280]{1,0:T(8,128)(2,1)S(1)}, u32[]{:S(2)}, u32[]{:S(2)}) collective-permute-start(bf16[96,1280]{1,0:T(8,128)(2,1)S(1)} %get-tuple-element.49), channel_id=1, source_target_pairs={{2,0},{0,2},{6,4},{4,6},{10,8},{8,10},{14,12},{12,14},{3,1},{1,3},... | collective-permute-start | bytes 737288 | tf_op jit(solution)/shard_map/ppermute | solution.py:22
  35.5 0.1 collective-permute-done.10.first_half
  35.6 0.0 copy-done
  35.6 2.9 %attend_early.1 = (f32[10,192,128]{2,1,0:T(8,128)S(1)}, f32[10,192,128]{2,1,0:T(8,128)S(1)}, f32[192,1280]{1,0:T(8,128)S(1)}) custom-call(s32[1,4]{1,0:T(1,128)S(1)} %copy-done, bf16[192,1280]{1,0:T(8,128)(2,1)S(1)} %get-tuple-element.41.query_ref, bf16[192,1280]{1,0:T(8,128)(2,1)S(1)} %get-tuple-element.34.keys_ref.own_keys, ...), custom_call_target="tpu_custom_call" | custom-call | flops 5000000000 | bytes 1 | tf_op jit(solution)/shard_map/attend_early/pallas_call | solution.py:380
  38.6 7.6 %collective-permute-done.8.passed_keys = bf16[192,1280]{1,0:T(8,128)(2,1)S(1)} collective-permute-done((bf16[192,1280]{1,0:T(8,128)(2,1)S(1)}, bf16[192,1280]{1,0:T(8,128)(2,1)S(1)}, u32[]{:S(2)}, u32[]{:S(2)}) %collective-permute-start.8) | collective-permute-done | bytes 491552 | tf_op jit(solution)/shard_map/ppermute | solution.py:22
  46.2 0.0 collective-permute-done.9.far_packed
  46.2 3.8 %attend_late_keys.1 = (f32[10,192,128]{2,1,0:T(8,128)S(1)}, f32[192,1280]{1,0:T(8,128)S(1)}, bf16[10,192,384]{2,1,0:T(8,128)(2,1)S(1)}) custom-call(s32[1,4]{1,0:T(1,128)S(1)} %copy-done, bf16[192,1280]{1,0:T(8,128)(2,1)S(1)} %get-tuple-element.41.query_ref, bf16[192,1280]{1,0:T(8,128)(2,1)S(1)} %collective-permute-done.8.passed_keys, ...), custom_call_target="tpu_custom_call" | custom-call | flops 1 | bytes 1 | tf_op jit(solution)/shard_map/attend_late_keys/pallas_call | solution.py:406
  50.0 0.0 collective-permute-done.11.second_half
  50.0 0.4 attend_passed_values.1.partial_ref
  50.4 1.9 %collective-permute-done.12.far_values = bf16[192,1280]{1,0:T(8,128)(2,1)S(1)} collective-permute-done((bf16[192,1280]{1,0:T(8,128)(2,1)S(1)}, bf16[192,1280]{1,0:T(8,128)(2,1)S(1)}, u32[]{:S(2)}, u32[]{:S(2)}) %collective-permute-start.12) | collective-permute-done | bytes 491552 | tf_op jit(solution)/shard_map/ppermute | solution.py:22
  52.4 1.2 %attend_late_values.1 = bf16[192,1280]{1,0:T(8,128)(2,1)} custom-call(f32[10,192,128]{2,1,0:T(8,128)S(1)} %get-tuple-element.45.inverses_ref, f32[192,1280]{1,0:T(8,128)S(1)} %attend_passed_values.1.partial_ref, bf16[10,192,384]{2,1,0:T(8,128)(2,1)S(1)} %get-tuple-element.47.weights_ref, bf16[192,1280]{1,0:T(8,128)(2,1)S(1)} %collective-permute-done.12.far_values), custom_call_target="tpu_custom_call" | custom-call | flops 1 | bytes 1 | tf_op jit(solution)/shard_map/attend_late_values/pallas_call | solution.py:441
  (3 shorter events, 0.1 us)
Async XLA Ops:
  0.0 19.9 %collective-permute-start.4 = (bf16[192,1280]{1,0:T(8,128)(2,1)}, bf16[192,1280]{1,0:T(8,128)(2,1)S(1)}, u32[]{:S(2)}, u32[]{:S(2)}) collective-permute-start(bf16[192,1280]{1,0:T(8,128)(2,1)} %own_values.1), channel_id=1, source_target_pairs={{4,0},{14,2},{8,4},{2,6},{12,8},{6,10},{0,12},{10,14},{5,1},{15,3}... | collective-permute-start | bytes 1474568 | tf_op jit(solution)/shard_map/ppermute | solution.py:22
  5.0 15.0 %collective-permute-start.5 = (bf16[192,1280]{1,0:T(8,128)(2,1)}, bf16[192,1280]{1,0:T(8,128)(2,1)S(1)}, u32[]{:S(2)}, u32[]{:S(2)}) collective-permute-start(bf16[192,1280]{1,0:T(8,128)(2,1)} %own_values.1), channel_id=1, source_target_pairs={{2,0},{0,2},{6,4},{4,6},{10,8},{8,10},{14,12},{12,14},{3,1},{1,3},... | collective-permute-start | bytes 1474568 | tf_op jit(solution)/shard_map/ppermute | solution.py:22
  6.5 3.6 %collective-permute-start = (f32[192,128]{1,0:T(8,128)S(1)}, f32[192,128]{1,0:T(8,128)S(1)}, u32[]{:S(2)}, u32[]{:S(2)}) collective-permute-start(f32[192,128]{1,0:T(8,128)S(1)} %get-tuple-element.32.squares), channel_id=1, source_target_pairs={{1,0},{0,1},{3,2},{2,3},{5,4},{4,5},{7,6},{6,7},{9,8},{8,9},{11,10... | collective-permute-start | bytes 294920 | tf_op jit(solution)/shard_map/ppermute | solution.py:22
  8.0 11.9 %collective-permute-start.3 = (bf16[4,2560]{1,0:T(4,128)(2,1)S(1)}, bf16[4,2560]{1,0:T(4,128)(2,1)S(1)}, u32[]{:S(2)}, u32[]{:S(2)}) collective-permute-start(bf16[4,2560]{1,0:T(4,128)(2,1)S(1)} %pack_rows.1.own_rows), channel_id=1, source_target_pairs={{2,0},{0,2},{6,4},{4,6},{10,8},{8,10},{14,12},{12,14},{3,1},{1,3},... | collective-permute-start | bytes 61448 | tf_op jit(solution)/shard_map/ppermute | solution.py:22
  10.4 20.0 %collective-permute-start.2 = (bf16[192,1280]{1,0:T(8,128)(2,1)S(1)}, bf16[192,1280]{1,0:T(8,128)(2,1)S(1)}, u32[]{:S(2)}, u32[]{:S(2)}) collective-permute-start(bf16[192,1280]{1,0:T(8,128)(2,1)S(1)} %get-tuple-element.34.keys_ref.own_keys), channel_id=1, source_target_pairs={{2,0},{0,2},{6,4},{4,6},{10,8},{8,10},{14,12},{12,14},{3,1},{1,3},... | collective-permute-start | bytes 1474568 | tf_op jit(solution)/shard_map/ppermute | solution.py:22
  10.4 17.0 %collective-permute-start.1 = (bf16[192,1280]{1,0:T(8,128)(2,1)S(1)}, bf16[192,1280]{1,0:T(8,128)(2,1)S(1)}, u32[]{:S(2)}, u32[]{:S(2)}) collective-permute-start(bf16[192,1280]{1,0:T(8,128)(2,1)S(1)} %get-tuple-element.34.keys_ref.own_keys), channel_id=1, source_target_pairs={{4,0},{14,2},{8,4},{2,6},{12,8},{6,10},{0,12},{10,14},{5,1},{15,3}... | collective-permute-start | bytes 1474568 | tf_op jit(solution)/shard_map/ppermute | solution.py:22
  19.9 15.7 %collective-permute-start.10 = (bf16[96,1280]{1,0:T(8,128)(2,1)S(1)}, bf16[96,1280]{1,0:T(8,128)(2,1)S(1)}, u32[]{:S(2)}, u32[]{:S(2)}) collective-permute-start(bf16[96,1280]{1,0:T(8,128)(2,1)S(1)} %get-tuple-element.40), channel_id=1, source_target_pairs={{2,0},{0,2},{6,4},{4,6},{10,8},{8,10},{14,12},{12,14},{3,1},{1,3},... | collective-permute-start | bytes 737288 | tf_op jit(solution)/shard_map/ppermute | solution.py:22
  20.0 11.2 %copy-start.1 = (bf16[192,1280]{1,0:T(8,128)(2,1)S(1)}, bf16[192,1280]{1,0:T(8,128)(2,1)}, u32[]{:S(2)}) copy-start(bf16[192,1280]{1,0:T(8,128)(2,1)} %own_values.1) | copy-start | bytes 1474564
  20.0 15.6 %copy-start = (s32[1,4]{1,0:T(1,128)S(1)}, s32[1,4]{1,0:T(1,128)}, u32[]{:S(2)}) copy-start(s32[1,4]{1,0:T(1,128)} %pattern_ref.3) | copy-start | bytes 52
  20.1 8.3 %collective-permute-start.7 = (bf16[8,2560]{1,0:T(8,128)(2,1)S(1)}, bf16[8,2560]{1,0:T(8,128)(2,1)S(1)}, u32[]{:S(2)}, u32[]{:S(2)}) collective-permute-start(bf16[8,2560]{1,0:T(8,128)(2,1)S(1)} %strip.1), channel_id=1, source_target_pairs={{8,0},{10,2},{12,4},{14,6},{0,8},{2,10},{4,12},{6,14},{9,1},{11,3}... | collective-permute-start | bytes 122888 | tf_op jit(solution)/shard_map/ppermute | solution.py:22
  22.1 7.1 %collective-permute-start.6 = (bf16[8,2560]{1,0:T(8,128)(2,1)S(1)}, bf16[8,2560]{1,0:T(8,128)(2,1)S(1)}, u32[]{:S(2)}, u32[]{:S(2)}) collective-permute-start(bf16[8,2560]{1,0:T(8,128)(2,1)S(1)} %strip.1), channel_id=1, source_target_pairs={{4,0},{14,2},{8,4},{2,6},{12,8},{6,10},{0,12},{10,14},{5,1},{15,3}... | collective-permute-start | bytes 122888 | tf_op jit(solution)/shard_map/ppermute | solution.py:22
  27.5 18.7 %collective-permute-start.9 = (bf16[208,1280]{1,0:T(8,128)(2,1)S(1)}, bf16[208,1280]{1,0:T(8,128)(2,1)S(1)}, u32[]{:S(2)}, u32[]{:S(2)}) collective-permute-start(bf16[208,1280]{1,0:T(8,128)(2,1)S(1)} %get-tuple-element.39), channel_id=1, source_target_pairs={{12,0},{6,2},{0,4},{10,6},{4,8},{14,10},{8,12},{2,14},{13,1},{7,3}... | collective-permute-start | bytes 1597448 | tf_op jit(solution)/shard_map/ppermute | solution.py:22
  30.4 15.8 %collective-permute-start.8 = (bf16[192,1280]{1,0:T(8,128)(2,1)S(1)}, bf16[192,1280]{1,0:T(8,128)(2,1)S(1)}, u32[]{:S(2)}, u32[]{:S(2)}) collective-permute-start(bf16[192,1280]{1,0:T(8,128)(2,1)S(1)} %collective-permute-done.1.far_keys), channel_id=1, source_target_pairs={{2,0},{0,2},{6,4},{4,6},{10,8},{8,10},{14,12},{12,14},{3,1},{1,3},... | collective-permute-start | bytes 1474568 | tf_op jit(solution)/shard_map/ppermute | solution.py:22
  31.3 21.1 %collective-permute-start.12 = (bf16[192,1280]{1,0:T(8,128)(2,1)S(1)}, bf16[192,1280]{1,0:T(8,128)(2,1)S(1)}, u32[]{:S(2)}, u32[]{:S(2)}) collective-permute-start(bf16[192,1280]{1,0:T(8,128)(2,1)S(1)} %copy-done.1), channel_id=1, source_target_pairs={{12,0},{6,2},{0,4},{10,6},{4,8},{14,10},{8,12},{2,14},{13,1},{7,3}... | collective-permute-start | bytes 1474568 | tf_op jit(solution)/shard_map/ppermute | solution.py:22
  31.6 18.4 %collective-permute-start.11 = (bf16[96,1280]{1,0:T(8,128)(2,1)S(1)}, bf16[96,1280]{1,0:T(8,128)(2,1)S(1)}, u32[]{:S(2)}, u32[]{:S(2)}) collective-permute-start(bf16[96,1280]{1,0:T(8,128)(2,1)S(1)} %get-tuple-element.49), channel_id=1, source_target_pairs={{2,0},{0,2},{6,4},{4,6},{10,8},{8,10},{14,12},{12,14},{3,1},{1,3},... | collective-permute-start | bytes 737288 | tf_op jit(solution)/shard_map/ppermute | solution.py:22
